TPU v7x, 32 devices: a whole 2x2x4 slice. The times are simulated.
32 devices in a mesh: img: 2 (over x), sp: 2 (over core), tp: 8 (over z, y).
Axes of the slice: x: 2, y: 2, z: 4, core: 2. Of those that a mesh axis runs over, the one named last changes fastest.
Arguments:
- tokens: bfloat16 [16, 32, 6144], P(('img', 'tp'), 'sp'), parts along dimension 0, may hold values from -6 to 6
- up_weight: bfloat16 [6144, 24576], P('sp', 'tp'), may hold values from -0.078125 to 0.078125
- up_bias: float32 [24576], P('tp'), may hold values from -3 to 3
- conv_weight: float32 [3, 3, 24576], P(None, None, 'tp'), may hold values from -2 to 2
- conv_bias: float32 [24576], P('tp'), may hold values from -3 to 3
- down_weight: bfloat16 [24576, 6144], P('tp', 'sp'), may hold values from -0.0390625 to 0.0390625
- down_bias: float32 [6144], replicated, may hold values from -3 to 3
Outputs:
- projected: bfloat16 [16, 32, 6144], P(('img', 'tp'), 'sp'), parts along dimension 0
There are 2 independent parts, one for each index of `img`. A program takes and returns all parts, laid end to end along the dimension named above; an argument that names none is the same for every part. Nothing has to cross between parts.
All inputs are finite; a program needn't handle non-finite values.
Results may differ from a plain program's by a relative error of at most 0.0053.
Values may be sent and summed in bfloat16 or wider, within the bound.
No kernel may reach another device: no remote copies, remote signals or barrier semaphores. Data moves between devices by JAX's collectives and lax.ppermute only.
A program may use at most 256 MiB of HBM per device.

v0:
```python
import jax
import jax.numpy as jnp
from jax import lax
from jax.sharding import PartitionSpec as P


def extended(block, sides, width):
    for axis, dim in sides:
        count = lax.axis_size(axis)
        forward = [(i, i + 1) for i in range(count - 1)]
        backward = [(target, source) for source, target in forward]
        low = lax.ppermute(
            lax.slice_in_dim(block, block.shape[dim] - width, None, axis=dim), axis, forward
        )
        high = lax.ppermute(lax.slice_in_dim(block, 0, width, axis=dim), axis, backward)
        block = jnp.concatenate([low, block, high], axis=dim)
    return block


def depthwise(hidden, conv_weight, conv_bias):
    padded = extended(hidden, (("sp", 1),), 1)
    padded = jnp.pad(padded, ((1, 1), (0, 0), (0, 0)))
    extent_x = hidden.shape[0]
    extent_y = hidden.shape[1]
    summed = jnp.zeros(hidden.shape, jnp.float32) + conv_bias
    for offset_x in range(3):
        for offset_y in range(3):
            window = padded[offset_x : offset_x + extent_x, offset_y : offset_y + extent_y]
            summed = summed + window.astype(jnp.float32) * conv_weight[offset_x, offset_y]
    return jax.nn.gelu(summed, approximate=False).astype(jnp.bfloat16)


def local(tokens, up_weight, up_bias, conv_weight, conv_bias, down_weight, down_bias):
    col_count = tokens.shape[0]
    row_count = tokens.shape[1]
    width_model = tokens.shape[2]
    hidden_dev = up_weight.shape[1]
    up_full, down_full = (
        lax.all_gather(up_weight, "sp", axis=0, tiled=True),
        lax.all_gather(down_weight, "sp", axis=1, tiled=True),
    )
    piece = lax.all_gather(tokens, "tp", axis=0, tiled=True)
    flat_piece = piece.reshape(-1, width_model)
    lifted = jnp.dot(flat_piece, up_full, preferred_element_type=jnp.float32) + up_bias
    hidden = lifted.astype(jnp.bfloat16).reshape(piece.shape[0], row_count, hidden_dev)
    mixed = depthwise(hidden, conv_weight, conv_bias)
    product = jnp.dot(mixed.reshape(-1, hidden_dev), down_full, preferred_element_type=jnp.float32)
    summed_terms = lax.psum_scatter(
        product.reshape(col_count * lax.axis_size("tp"), row_count, width_model),
        "tp",
        scatter_dimension=0,
        tiled=True,
    )
    return (summed_terms + down_bias).astype(jnp.bfloat16)


def solution(mesh):
    placed = (
        P(("img", "tp"), "sp", None),
        P("sp", "tp"),
        P("tp"),
        P(None, None, "tp"),
        P("tp"),
        P("tp", "sp"),
        P(),
    )
    return jax.shard_map(
        local, mesh=mesh, in_specs=placed, out_specs=P(("img", "tp"), "sp", None), check_vma=False
    )
```

profile of v0, /device:TPU:0, one launch (start us, length us, event | category | flops | bytes accessed | tf_op | source)
XLA Modules:
  0.0 277.0 jit_solution(13013426997348441983)
XLA Ops:
  6.5 0.7 all-gather.4.cloned.1.call-update
  7.3 0.0 all-gather.6.cloned.1.call-start
  7.3 0.7 all-gather.6.cloned.1.call-update
  8.0 0.0 copy-start.2
  8.0 0.0 all-gather.8.cloned.1.call-start
  8.1 0.7 all-gather.8.cloned.1.call-update
  8.8 0.0 reduce-scatter.2.cloned.1.call-start
  8.8 47.7 %all-gather.4.cloned.1.call-done = bf16[8,16,6144]{2,1,0:T(8,128)(2,1)} async-done(((bf16[1,16,6144]{2,1,0:T(8,128)(2,1)}), bf16[8,16,6144]{2,1,0:T(8,128)(2,1)}) %all-gather.4.cloned.1.call-update) | async-done | bytes 1572880 | tf_op jit(solution)/shard_map/all_gather | solution.py:42
  56.5 58.2 %all-gather.6.cloned.1.call-done = bf16[6144,3072]{1,0:T(8,128)(2,1)} async-done(((bf16[3072,3072]{1,0:T(8,128)(2,1)}), bf16[6144,3072]{1,0:T(8,128)(2,1)}) %all-gather.6.cloned.1.call-update) | async-done | bytes 37748752 | tf_op jit(solution)/shard_map/all_gather | solution.py:39
  114.7 18.7 %fusion.2 = bf16[128,3072]{1,0:T(8,128)(2,1)S(1)} fusion(bf16[128,6144]{1,0:T(8,128)(2,1)} %bitcast.19, bf16[6144,3072]{1,0:T(8,128)(2,1)} %all-gather.6.cloned.1.call-done, f32[3072]{0:T(1024)S(1)} %copy-done.2), kind=kOutput, calls=%fused_computation.5 | convolution fusion | flops 4832624640 | bytes 40120320 | tf_op jit(solution)/shard_map/dot_general | solution.py:44
  133.3 0.0 copy-start.3
  133.3 0.2 fusion.99
  133.5 2.0 collective-permute-start
  135.5 1.3 collective-permute-start.1
  136.8 0.1 fusion.100
  136.9 0.0 collective-permute-done
  136.9 1.8 collective-permute-done.1
  138.7 0.5 fusion.18
  139.2 36.0 %all-gather.8.cloned.1.call-done = bf16[3072,6144]{1,0:T(8,128)(2,1)} async-done(((bf16[3072,3072]{1,0:T(8,128)(2,1)}), bf16[3072,6144]{1,0:T(8,128)(2,1)}) %all-gather.8.cloned.1.call-update) | async-done | bytes 37748752 | tf_op jit(solution)/shard_map/all_gather | solution.py:40
  175.2 18.0 %fusion = f32[8,16,6144]{2,1,0:T(8,128)} fusion(bf16[3072,6144]{1,0:T(8,128)(2,1)} %all-gather.8.cloned.1.call-done, bf16[8,16,3072]{2,1,0:T(8,128)(2,1)S(1)} %bitcast.18, bf16[10,18,3072]{2,1,0:T(8,128)(2,1)S(1)} %fusion.18, bf16[8,1,3072]{2,1,0:T(2,128)(2,1)S(1)} %collective-permute-done.1, bf16[8,1,3072]{2,1,0:T(2,128)(2,1)S(1)} %collective-permute-done, ...), kind=kOutput, calls=%fused_computation | convolution fusion | flops 4870373376 | bytes 46718976 | tf_op jit(solution)/shard_map/dot_general | solution.py:47
  193.1 0.0 reduce-scatter.2.cloned.1.call-update
  193.2 75.6 %reduce-scatter.2.cloned.1.call-done = f32[1,16,6144]{2,1,0:T(8,128)} async-done(((f32[8,16,6144]{2,1,0:T(8,128)}), f32[1,16,6144]{2,1,0:T(8,128)}) %reduce-scatter.2.cloned.1.call-update) | async-done | bytes 393232 | tf_op jit(solution)/shard_map/reduce_scatter | solution.py:48
  268.7 0.0 copy-done.1
  268.7 1.7 add_convert_fusion
  (6 shorter events, 0.0 us)
Async XLA Ops:
  6.5 49.9 %all-gather.4.cloned.1.call-start = ((), (), s32[]{:S(2)}) async-start(), calls=%async_computation.1 | async-start | bytes 1769472 | tf_op jit(solution)/shard_map/all_gather | solution.py:42
  7.3 107.4 %all-gather.6.cloned.1.call-start = ((), (), s32[]{:S(2)}) async-start(), calls=%async_computation.2 | async-start | bytes 56623104 | tf_op jit(solution)/shard_map/all_gather | solution.py:39
  8.0 106.7 %copy-start.2 = (f32[3072]{0:T(1024)S(1)}, f32[3072]{0:T(1024)}, u32[]{:S(2)}) copy-start(f32[3072]{0:T(1024)} %param.9) | copy-start | bytes 36868
  8.0 167.2 %all-gather.8.cloned.1.call-start = ((), (), s32[]{:S(2)}) async-start(), calls=%async_computation.3 | async-start | bytes 56623104 | tf_op jit(solution)/shard_map/all_gather | solution.py:40
  8.8 260.0 %reduce-scatter.2.cloned.1.call-start = ((), (), s32[]{:S(2)}) async-start(), calls=%async_computation.4 | async-start | bytes 3538944 | tf_op jit(solution)/shard_map/reduce_scatter | solution.py:48
  114.7 22.1 %copy-start = (f32[3,3,3072]{2,1,0:T(4,128)S(1)}, f32[3,3,3072]{2,1,0:T(4,128)}, u32[]{:S(2)}) copy-start(f32[3,3,3072]{2,1,0:T(4,128)} %param.10) | copy-start | bytes 331780
  133.3 41.8 %copy-start.3 = (f32[3072]{0:T(1024)S(1)}, f32[3072]{0:T(1024)}, u32[]{:S(2)}) copy-start(f32[3072]{0:T(1024)} %param.11) | copy-start | bytes 36868
  133.5 3.4 %collective-permute-start = (bf16[8,1,3072]{2,1,0:T(2,128)(2,1)S(1)}, bf16[8,1,3072]{2,1,0:T(2,128)(2,1)S(1)}, u32[]{:S(2)}, u32[]{:S(2)}) collective-permute-start(bf16[8,1,3072]{2,1,0:T(2,128)(2,1)S(1)} %get-tuple-element.5), channel_id=1, source_target_pairs={{0,8},{1,9},{2,10},{3,11},{4,12},{5,13},{6,14},{7,15},{16,24},{17,... | collective-permute-start | bytes 147464 | tf_op jit(solution)/shard_map/ppermute | solution.py:12
  135.5 3.2 %collective-permute-start.1 = (bf16[8,1,3072]{2,1,0:T(2,128)(2,1)S(1)}, bf16[8,1,3072]{2,1,0:T(2,128)(2,1)S(1)}, u32[]{:S(2)}, u32[]{:S(2)}) collective-permute-start(bf16[8,1,3072]{2,1,0:T(2,128)(2,1)S(1)} %get-tuple-element.6), channel_id=1, source_target_pairs={{8,0},{9,1},{10,2},{11,3},{12,4},{13,5},{14,6},{15,7},{24,16},{25,... | collective-permute-start | bytes 147464 | tf_op jit(solution)/shard_map/ppermute | solution.py:15
  193.1 75.6 %copy-start.1 = (f32[6144]{0:T(1024)S(1)}, f32[6144]{0:T(1024)}, u32[]{:S(2)}) copy-start(f32[6144]{0:T(1024)} %param.13) | copy-start | bytes 73732
Sparse Core Ops, SparseCore 0:
  9.5 46.8 all-gather.3
  58.0 56.5 all-gather.5
  116.2 58.9 all-gather.7
  193.3 75.3 reduce-scatter.1
where the time goes:
time: 277 us
  waiting for transfers between devices  221 us (80%)
  matrix products  36.6 us (13%)
  between operations  13.2 us (5%)
  starting transfers between devices  3.38 us (1%)
    reduce_scatter x1, waiting for transfers between devices, local(): lax.psum_scatter(product.reshape(col_count * lax.axis_size('tp'), row_cou...  75.6 us
    all_gather x1, waiting for transfers between devices, local(): lax.all_gather(up_weight, 'sp', axis=0, tiled=True)  58.2 us
    all_gather x1, waiting for transfers between devices, local(): piece = lax.all_gather(tokens, 'tp', axis=0, tiled=True)  47.7 us
    all_gather x1, waiting for transfers between devices, local(): lax.all_gather(down_weight, 'sp', axis=1, tiled=True)  36 us
    dot_general x1, matrix products, local(): jnp.dot(flat_piece, up_full, preferred_element_type=jnp.float32) + up_bias  18.7 us
    dot_general x1, matrix products, local(): jnp.dot(mixed.reshape(-1, hidden_dev), down_full, preferred_element_type=...  18 us
  transfers between devices with their start and end apart: 6, of which 5 were waited for; matrix products, arithmetic and copies ran while one was open for 7% of the time, Pallas kernels for 0%

commit v1 on v0

v1 whole, which is shorter than its diff:
```python
import functools

import jax
import jax.numpy as jnp
from jax import lax
from jax.experimental import pallas as pl
from jax.experimental.pallas import tpu as pltpu
from jax.sharding import PartitionSpec as P

F32 = jnp.float32
BF16 = jnp.bfloat16
VMEM = pl.BlockSpec(memory_space=pltpu.VMEM)
HBM = pl.BlockSpec(memory_space=pltpu.HBM)
SMEM = pl.BlockSpec(memory_space=pltpu.SMEM)
MIB = 1 << 20

ERF_NUM = (0.00022905065861350646, 0.0034082910107109506, 0.050955695062380861, 0.18520832239976145, 1.128379143519084)
ERF_DEN = (
    -1.1791602954361697e-7,
    0.000023547966471313185,
    0.0010179625278914885,
    0.014070470171167667,
    0.11098505178285362,
    0.49746925110067538,
    1.0,
)


def tile_of(size, most):
    for tile in range(most, 0, -128):
        if size % tile == 0:
            return tile
    return size


def cost(flops, moved, transcendentals=0):
    return pl.CostEstimate(flops=int(flops), bytes_accessed=int(moved), transcendentals=int(transcendentals))


def params(limit):
    return pltpu.CompilerParams(vmem_limit_bytes=limit * MIB)


def row_copies(weight_ref, first, out_ref, sems):
    parts = sems.shape[0]
    step = out_ref.shape[0] // parts
    return [
        pltpu.make_async_copy(
            weight_ref.at[pl.ds(first + part * step, step)], out_ref.at[pl.ds(part * step, step)], sems.at[part]
        )
        for part in range(parts)
    ]


def fetch(info, weight, start, count, held, parts=4):
    own_bytes = count * weight.shape[1] * 2
    limit = max(1, (60 * MIB - held - own_bytes) // MIB - 8)

    def kernel(info_ref, weight_ref, out_ref, sems):
        copies = row_copies(weight_ref, pl.multiple_of(start(info_ref[0]), 16), out_ref, sems)
        for copy in copies:
            copy.start()
        for copy in copies:
            copy.wait()

    return pl.pallas_call(
        kernel,
        out_shape=pltpu.VMEM((count, weight.shape[1]), weight.dtype),
        in_specs=[SMEM, HBM],
        out_specs=VMEM,
        scratch_shapes=[pltpu.SemaphoreType.DMA((parts,))],
        cost_estimate=cost(0, 2 * count * weight.shape[1] * 2),
        compiler_params=params(limit),
    )(info, weight)


def up_other(info, slots, upper, lower, width):
    rows = slots[0].shape[0]
    depth = slots[0].shape[1]
    total = rows * len(slots)
    split = upper.shape[0]
    tile = tile_of(width, 768)
    high = tile_of(total, 256)

    def kernel(info_ref, *refs):
        slot_refs = refs[: len(slots)]
        upper_ref, lower_ref, out_ref, tokens_ref = refs[len(slots) :]
        for index, ref in enumerate(slot_refs):
            tokens_ref[index * rows : (index + 1) * rows, :] = ref[...]
        base = (1 - info_ref[0]) * width

        def body(step, carry):
            row, col = step // (width // tile), step % (width // tile)
            down = pl.ds(pl.multiple_of(row * high, high), high)
            across = pl.ds(pl.multiple_of(base + col * tile, 128), tile)
            product = jnp.dot(tokens_ref[down, :split], upper_ref[:, across], preferred_element_type=F32) + jnp.dot(
                tokens_ref[down, split:], lower_ref[:, across], preferred_element_type=F32
            )
            out_ref[down, pl.ds(pl.multiple_of(col * tile, 128), tile)] = product.astype(BF16)
            return carry

        lax.fori_loop(0, (total // high) * (width // tile), body, 0)

    return pl.pallas_call(
        kernel,
        out_shape=(
            pltpu.VMEM((total, width), BF16),
            pltpu.VMEM((total, depth), BF16),
        ),
        in_specs=[SMEM] + [VMEM] * (len(slots) + 2),
        out_specs=(VMEM, VMEM),
        cost_estimate=cost(2 * total * depth * width, 2 * depth * width),
        compiler_params=params(12),
    )(info, *slots, upper, lower)


def up_own(info, tokens, upper, lower, width):
    total, depth = tokens.shape
    split = upper.shape[0]
    tile = tile_of(width, 768)
    high = tile_of(total, 256)

    def kernel(info_ref, tokens_ref, upper_ref, lower_ref, out_ref):
        base = info_ref[0] * width

        def body(step, carry):
            row, col = step // (width // tile), step % (width // tile)
            down = pl.ds(pl.multiple_of(row * high, high), high)
            across = pl.ds(pl.multiple_of(base + col * tile, 128), tile)
            out_ref[down, pl.ds(pl.multiple_of(col * tile, 128), tile)] = jnp.dot(
                tokens_ref[down, :split], upper_ref[:, across], preferred_element_type=F32
            ) + jnp.dot(tokens_ref[down, split:], lower_ref[:, across], preferred_element_type=F32)
            return carry

        lax.fori_loop(0, (total // high) * (width // tile), body, 0)

    return pl.pallas_call(
        kernel,
        out_shape=pltpu.VMEM((total, width), F32),
        in_specs=[SMEM] + [VMEM] * 3,
        out_specs=VMEM,
        cost_estimate=cost(2 * total * depth * width, 2 * depth * width),
        compiler_params=params(12),
    )(info, tokens, upper, lower)


def gelu(value):
    arg = jnp.clip(value * 0.7071067811865476, -3.832506856900711, 3.832506856900711)
    square = arg * arg
    num = jnp.full_like(square, ERF_NUM[0])
    for coefficient in ERF_NUM[1:]:
        num = num * square + coefficient
    den = jnp.full_like(square, ERF_DEN[0])
    for coefficient in ERF_DEN[1:]:
        den = den * square + coefficient
    return 0.5 * value * (1.0 + arg * num / den)


def conv(info, own, received, up_bias, conv_weight, conv_bias, later, ring_size, lanes_of, grid_y):
    total, width = own.shape
    blocks = ring_size * lanes_of
    rows = total // blocks
    lanes = 128
    extent_x = total // grid_y

    def kernel(info_ref, own_ref, received_ref, up_bias_ref, weight_ref, bias_ref, later_ref, out_ref, later_out, hidden, sems):
        copies = row_copies(later_ref, pl.multiple_of(info_ref[0] * width, 16), later_out, sems)
        for copy in copies:
            copy.start()
        hidden[0:grid_y, :] = jnp.zeros((grid_y, lanes), F32)
        hidden[(extent_x + 1) * grid_y : (extent_x + 2) * grid_y, :] = jnp.zeros((grid_y, lanes), F32)
        at_y = lax.broadcasted_iota(jnp.int32, (grid_y, lanes), 0)
        first, last = at_y == 0, at_y == grid_y - 1
        base = info_ref[0] * width
        places = [
            lax.rem(info_ref[1] + (ring_size - j), ring_size) * lanes_of + lax.rem(info_ref[2] + q, lanes_of)
            for q in range(lanes_of)
            for j in range(ring_size)
        ]

        def body(col, carry):
            across = pl.ds(pl.multiple_of(col * lanes, lanes), lanes)
            absolute = pl.ds(pl.multiple_of(base + col * lanes, lanes), lanes)
            shift = up_bias_ref[:, absolute]
            for slot in range(blocks):
                down = slice(slot * rows, (slot + 1) * rows)
                value = own_ref[down, across] + received_ref[down, across].astype(F32) + shift
                target = pl.multiple_of(places[slot] * rows + grid_y, grid_y)
                hidden[pl.ds(target, rows), :] = value.astype(BF16).astype(F32)
            weights = [[weight_ref[a, b : b + 1, absolute] for b in range(3)] for a in range(3)]
            offset = bias_ref[:, absolute]
            for slot in range(blocks):
                for line in range(rows // grid_y):
                    start = places[slot] * rows + line * grid_y
                    near = [hidden[pl.ds(pl.multiple_of(start + a * grid_y, grid_y), grid_y), :] for a in range(3)]
                    sums = [near[0] * weights[0][b] + near[1] * weights[1][b] + near[2] * weights[2][b] for b in range(3)]
                    before = jnp.where(first, 0.0, pltpu.roll(sums[0], 1, axis=0))
                    after = jnp.where(last, 0.0, pltpu.roll(sums[2], grid_y - 1, axis=0))
                    value = sums[1] + before + after + offset
                    out_ref[slot * rows + line * grid_y : slot * rows + (line + 1) * grid_y, across] = gelu(value).astype(BF16)
            return carry

        lax.fori_loop(0, width // lanes, body, 0)
        for copy in copies:
            copy.wait()

    return pl.pallas_call(
        kernel,
        out_shape=(pltpu.VMEM((total, width), BF16), pltpu.VMEM((width, later.shape[1]), BF16)),
        in_specs=[SMEM] + [VMEM] * 5 + [HBM],
        out_specs=(VMEM, VMEM),
        scratch_shapes=[pltpu.VMEM(((extent_x + 2) * grid_y, lanes), F32), pltpu.SemaphoreType.DMA((4,))],
        cost_estimate=cost(60 * total * width, 8 * total * width),
        compiler_params=params(33),
    )(info, own, received, up_bias, conv_weight, conv_bias, later)


def down_own(info, mixed, weight, later):
    total, depth = mixed.shape
    width = weight.shape[1]
    tile = tile_of(width, 1024)
    high = tile_of(total, 256)

    def kernel(info_ref, mixed_ref, weight_ref, later_ref, out_ref, later_out, sems):
        copies = row_copies(later_ref, pl.multiple_of((1 - info_ref[0]) * depth, 16), later_out, sems)
        for copy in copies:
            copy.start()

        def body(step, carry):
            row, col = step // (width // tile), step % (width // tile)
            down = pl.ds(pl.multiple_of(row * high, high), high)
            across = pl.ds(pl.multiple_of(col * tile, tile), tile)
            out_ref[down, across] = jnp.dot(mixed_ref[down, :], weight_ref[:, across], preferred_element_type=F32)
            return carry

        lax.fori_loop(0, (total // high) * (width // tile), body, 0)
        for copy in copies:
            copy.wait()

    return pl.pallas_call(
        kernel,
        out_shape=(pltpu.VMEM((total, width), F32), pltpu.VMEM((depth, width), BF16)),
        in_specs=[SMEM] + [VMEM] * 2 + [HBM],
        out_specs=(VMEM, VMEM),
        scratch_shapes=[pltpu.SemaphoreType.DMA((4,))],
        cost_estimate=cost(2 * total * depth * width, 2 * depth * width),
        compiler_params=params(26),
    )(info, mixed, weight, later)


def down_other(mixed, weight, partial, kept):
    total, depth = mixed.shape
    width = weight.shape[1]
    tile = tile_of(width, 1024)

    def kernel(mixed_ref, weight_ref, partial_ref, keep_ref, *send_refs):
        def body(col, carry):
            across = pl.ds(pl.multiple_of(col * tile, tile), tile)
            for first in range(0, total, 256):
                high = min(256, total - first)
                value = partial_ref[first : first + high, across] + jnp.dot(
                    mixed_ref[first : first + high, :], weight_ref[:, across], preferred_element_type=F32
                )
                inside = max(0, min(high, kept - first))
                if inside:
                    keep_ref[first : first + inside, across] = value[:inside]
                if inside < high:
                    low = first + inside - kept
                    send_refs[0][low : low + high - inside, across] = value[inside:].astype(BF16)
            return carry

        lax.fori_loop(0, width // tile, body, 0)

    shapes = [pltpu.VMEM((kept, width), F32)]
    if kept < total:
        shapes.append(pltpu.VMEM((total - kept, width), BF16))
    return pl.pallas_call(
        kernel,
        out_shape=tuple(shapes),
        in_specs=[VMEM] * 3,
        out_specs=(VMEM,) * len(shapes),
        cost_estimate=cost(2 * total * depth * width, 2 * depth * width),
        compiler_params=params(12),
    )(mixed, weight, partial)


def tie(*values):
    return lax.optimization_barrier(values)


def local(tokens, up_weight, up_bias, conv_weight, conv_bias, down_weight, down_bias):
    cols, grid_half, width_model = tokens.shape
    half = width_model // 2
    units = up_weight.shape[1]
    units_half = units // 2
    grid_y = grid_half * 2
    rows = cols * grid_y

    count = lax.axis_size("tp")
    lanes = 2 if count % 2 == 0 else 1
    ring_size = count // lanes
    core = lax.axis_index("sp")
    mine = lax.axis_index("tp")
    ring_at, lane_at = mine // lanes, mine % lanes
    ring = [(t, (t + lanes) % count) for t in range(count)]
    cross = [(t, t ^ 1) for t in range(count)]
    swap = [(0, 1), (1, 0)]

    flat = tokens.reshape(cols * grid_half, width_model)
    keep = lax.dynamic_slice_in_dim(flat, core * half, half, axis=1)
    give = lax.dynamic_slice_in_dim(flat, (1 - core) * half, half, axis=1)
    take = lax.ppermute(give, "sp", swap)
    keep, take = (x.reshape(cols, 1, grid_half, half) for x in (keep, take))
    block = jnp.where(core == 0, jnp.concatenate([keep, take], 1), jnp.concatenate([take, keep], 1))
    block = block.reshape(rows, half)

    info = jnp.stack([core, ring_at, lane_at]).astype(jnp.int32)
    block, info = tie(block, info)

    up_split = half // 2
    up_bytes = up_split * units * 2
    fetches = [
        lambda: fetch(info, up_weight, lambda c: 0 * c, up_split, 0),
        lambda: fetch(info, up_weight, lambda c: 0 * c + up_split, up_split, up_bytes),
    ]

    column, beside, fetched = [block], [], []
    for step in range(ring_size):
        current = column[-1]
        pending = []
        if lanes > 1:
            pending.append(lax.ppermute(current, "tp", cross))
        if step < ring_size - 1:
            pending.append(lax.ppermute(current, "tp", ring))
        if fetches:
            fetched.append(fetches.pop(0)())
            pending.append(fetched[-1])
        done = list(tie(*pending))
        if lanes > 1:
            beside.append(done.pop(0))
        if step < ring_size - 1:
            column.append(done.pop(0))
        if done:
            fetched[-1] = done.pop(0)
    fetched += [make() for make in fetches]
    upper, lower = fetched
    slots = column + beside

    partial_other, gathered = up_other(info, slots, upper, lower, units_half)
    partial_received = lax.ppermute(partial_other, "sp", swap)
    partial_own = up_own(info, gathered, upper, lower, units_half)
    mixed, down_mine = conv(
        info,
        partial_own,
        partial_received,
        up_bias.reshape(1, units),
        conv_weight,
        conv_bias.reshape(1, units),
        down_weight,
        ring_size,
        lanes,
        grid_y,
    )
    mixed_received = lax.ppermute(mixed, "sp", swap)
    product, down_theirs = down_own(info, mixed, down_mine, down_weight)
    sums = down_other(mixed_received, down_theirs, product, ring_size * rows)
    kept = sums[0].reshape(ring_size, rows, half)

    order = list(range(1, ring_size)) + [0]
    if lanes > 1:
        sent = sums[1].reshape(ring_size, rows, half)
    travelling = None
    for position, j in enumerate(order):
        value = kept[j]
        if lanes > 1:
            value = value + lax.ppermute(sent[j], "tp", cross).astype(F32)
        if travelling is not None:
            value = value + travelling.astype(F32)
        if position < ring_size - 1:
            travelling = lax.ppermute(value.astype(BF16), "tp", ring)
    bias = lax.dynamic_slice_in_dim(down_bias, core * half, half)
    final = (value + bias).astype(BF16).reshape(cols, 2, grid_half, half)
    stay = lax.dynamic_index_in_dim(final, core, 1, keepdims=False)
    leave = lax.dynamic_index_in_dim(final, 1 - core, 1, keepdims=False)
    arrive = lax.ppermute(leave, "sp", swap)
    return jnp.where(core == 0, jnp.concatenate([stay, arrive], -1), jnp.concatenate([arrive, stay], -1))


def solution(mesh):
    placed = (
        P(("img", "tp"), "sp", None),
        P("sp", "tp"),
        P("tp"),
        P(None, None, "tp"),
        P("tp"),
        P("tp", "sp"),
        P(),
    )
    return jax.shard_map(
        local, mesh=mesh, in_specs=placed, out_specs=P(("img", "tp"), "sp", None), check_vma=False
    )
```

time: 277 us -> 88.9 us (0.32)
  waiting for transfers between devices: 221 us -> 47.1 us
  matrix products: 36.6 us -> 0 us
  Pallas kernels: 0 us -> 27.2 us
  between operations: 13.2 us -> 0.23 us
  starting transfers between devices: 3.38 us -> 12.1 us
    all_gather x3 -> x0, waiting for transfers between devices: 142 us -> none  [the longest x1 58.2 us: local(): lax.all_gather(up_weight, 'sp', axis=0, tiled=True)]
    reduce_scatter x1 -> x0, waiting for transfers between devices: 75.6 us -> none  [local(): lax.psum_scatter(product.reshape(col_count * lax.axis_size('tp'), row_cou...]
    ppermute x2 -> x18, waiting for transfers between devices: 1.79 us -> 47.1 us  [the longest x3 17.5 us: local(): travelling = lax.ppermute(value.astype(BF16), 'tp', ring)]
    dot_general x2 -> x0, matrix products: 36.6 us -> none  [the longest x1 18.7 us: local(): jnp.dot(flat_piece, up_full, preferred_element_type=jnp.float32) + up_bias]
    pallas_call x0 -> x7, Pallas kernels: none -> 27.2 us  [the longest x2 8.68 us: fetch(): pl.pallas_call(kernel, out_shape=pltpu.VMEM((count, weight.shape[1]), wei...]
    ppermute x2 -> x18, starting transfers between devices: 3.27 us -> 12.1 us  [the longest x4 5.47 us: local(): pending.append(lax.ppermute(current, 'tp', cross))]
  transfers between devices with their start and end apart: 6 -> 18, of which waited for: 5 -> 13; matrix products, arithmetic and copies ran while one was open for 7% -> 0% of each run, Pallas kernels for 0% -> 18%
where the time goes in v1:
time: 88.9 us; the launch traced here: 88.7 us
  waiting for transfers between devices  47.1 us (53%)
  Pallas kernels  27.2 us (31%)
  starting transfers between devices  12.1 us (14%)
  other arithmetic  1.08 us (1%)
  local copies, waits for them, and re-layouts  1.07 us (1%)
    ppermute x3, waiting for transfers between devices, local(): travelling = lax.ppermute(value.astype(BF16), 'tp', ring)  17.5 us
    ppermute x4, waiting for transfers between devices, local(): pending.append(lax.ppermute(current, 'tp', cross))  10.3 us
    ppermute x4, waiting for transfers between devices, local(): value = value + lax.ppermute(sent[j], 'tp', cross).astype(F32)  9.08 us
    pallas_call x2, Pallas kernels, fetch(): pl.pallas_call(kernel, out_shape=pltpu.VMEM((count, weight.shape[1]), wei...  8.68 us
    ppermute x3, waiting for transfers between devices, local(): pending.append(lax.ppermute(current, 'tp', ring))  8.01 us
    ppermute x4, starting transfers between devices, local(): pending.append(lax.ppermute(current, 'tp', cross))  5.47 us
    pallas_call x1, Pallas kernels, conv(): pl.pallas_call(kernel, out_shape=(pltpu.VMEM((total, width), BF16), pltpu...  4.35 us
    pallas_call x1, Pallas kernels, down_own(): pl.pallas_call(kernel, out_shape=(pltpu.VMEM((total, width), F32), pltpu....  4.35 us
  transfers between devices with their start and end apart: 18, of which 13 were waited for; matrix products, arithmetic and copies ran while one was open for 0% of the time, Pallas kernels for 18%

profile of v1, /device:TPU:0, one launch (start us, length us, event | category | flops | bytes accessed | tf_op | source)
XLA Modules:
  0.0 88.7 jit_solution(10021919107892355220)
XLA Ops:
  0.0 1.0 %dynamic-slice_bitcast_fusion.3 = (bf16[1,1,16,3072]{3,2,1,0:T(8,128)(2,1)S(1)}, bf16[16,3072]{1,0:T(8,128)(2,1)S(1)}) fusion(bf16[1,16,6144]{2,1,0:T(8,128)(2,1)} %param.7, s32[]{:T(128)} %select_n.57, s32[]{:T(128)S(6)} %select_n.58), kind=kLoop, calls=%fused_computation.9 | loop fusion | bytes 393224 | tf_op jit(solution)/shard_map/concatenate | solution.py:314
  2.4 2.9 %collective-permute-start.1 = (bf16[32,3072]{1,0:T(8,128)(2,1)S(1)}, bf16[32,3072]{1,0:T(8,128)(2,1)S(1)}, u32[]{:S(2)}, u32[]{:S(2)}) collective-permute-start(bf16[32,3072]{1,0:T(8,128)(2,1)S(1)} %bitcast.16), channel_id=1, source_target_pairs={{0,1},{1,0},{2,3},{3,2},{4,5},{5,4},{6,7},{7,6},{8,9},{9,8},{10,11... | collective-permute-start | bytes 589832 | tf_op jit(solution)/shard_map/ppermute | solution.py:332
  5.4 1.6 %collective-permute-start.2 = (bf16[32,3072]{1,0:T(8,128)(2,1)S(1)}, bf16[32,3072]{1,0:T(8,128)(2,1)S(1)}, u32[]{:S(2)}, u32[]{:S(2)}) collective-permute-start(bf16[32,3072]{1,0:T(8,128)(2,1)S(1)} %bitcast.17), channel_id=1, source_target_pairs={{0,2},{1,3},{2,4},{3,5},{4,6},{5,7},{6,0},{7,1},{8,10},{9,11},{10,... | collective-permute-start | bytes 589832 | tf_op jit(solution)/shard_map/ppermute | solution.py:334
  7.0 4.3 %shard_map.73.refs_8_.upper_ref = bf16[1536,3072]{1,0:T(8,128)(2,1)S(1)} custom-call(s32[3]{0:T(128)S(1)} %pad_add_fusion.info_ref, bf16[3072,3072]{1,0:T(8,128)(2,1)} %weight_ref.4), custom_call_target="tpu_custom_call" | custom-call | bytes 18874368 | tf_op jit(solution)/shard_map/pallas_call | solution.py:66
  11.3 2.6 %collective-permute-done.2.refs_1_ = bf16[32,3072]{1,0:T(8,128)(2,1)S(1)} collective-permute-done((bf16[32,3072]{1,0:T(8,128)(2,1)S(1)}, bf16[32,3072]{1,0:T(8,128)(2,1)S(1)}, u32[]{:S(2)}, u32[]{:S(2)}) %collective-permute-start.2) | collective-permute-done | bytes 196640 | tf_op jit(solution)/shard_map/ppermute | solution.py:334
  14.4 4.3 %shard_map.74.refs_9_.lower_ref = bf16[1536,3072]{1,0:T(8,128)(2,1)S(1)} custom-call(s32[3]{0:T(128)S(1)} %pad_add_fusion.info_ref, bf16[3072,3072]{1,0:T(8,128)(2,1)} %weight_ref.4), custom_call_target="tpu_custom_call" | custom-call | bytes 18874368 | tf_op jit(solution)/shard_map/pallas_call | solution.py:66
  18.8 1.0 %collective-permute-done.3.refs_5_ = bf16[32,3072]{1,0:T(8,128)(2,1)S(1)} collective-permute-done((bf16[32,3072]{1,0:T(8,128)(2,1)S(1)}, bf16[32,3072]{1,0:T(8,128)(2,1)S(1)}, u32[]{:S(2)}, u32[]{:S(2)}) %collective-permute-start.3) | collective-permute-done | bytes 196640 | tf_op jit(solution)/shard_map/ppermute | solution.py:332
  19.8 2.3 %collective-permute-done.4.refs_2_ = bf16[32,3072]{1,0:T(8,128)(2,1)S(1)} collective-permute-done((bf16[32,3072]{1,0:T(8,128)(2,1)S(1)}, bf16[32,3072]{1,0:T(8,128)(2,1)S(1)}, u32[]{:S(2)}, u32[]{:S(2)}) %collective-permute-start.4) | collective-permute-done | bytes 196640 | tf_op jit(solution)/shard_map/ppermute | solution.py:334
  22.1 1.3 %collective-permute-start.5 = (bf16[32,3072]{1,0:T(8,128)(2,1)S(1)}, bf16[32,3072]{1,0:T(8,128)(2,1)S(1)}, u32[]{:S(2)}, u32[]{:S(2)}) collective-permute-start(bf16[32,3072]{1,0:T(8,128)(2,1)S(1)} %collective-permute-done.4.refs_2_), channel_id=1, source_target_pairs={{0,1},{1,0},{2,3},{3,2},{4,5},{5,4},{6,7},{7,6},{8,9},{9,8},{10,11... | collective-permute-start | bytes 589832 | tf_op jit(solution)/shard_map/ppermute | solution.py:332
  23.4 4.3 %collective-permute-done.5.refs_6_ = bf16[32,3072]{1,0:T(8,128)(2,1)S(1)} collective-permute-done((bf16[32,3072]{1,0:T(8,128)(2,1)S(1)}, bf16[32,3072]{1,0:T(8,128)(2,1)S(1)}, u32[]{:S(2)}, u32[]{:S(2)}) %collective-permute-start.5) | collective-permute-done | bytes 196640 | tf_op jit(solution)/shard_map/ppermute | solution.py:332
  27.7 3.1 %collective-permute-done.6.refs_3_ = bf16[32,3072]{1,0:T(8,128)(2,1)S(1)} collective-permute-done((bf16[32,3072]{1,0:T(8,128)(2,1)S(1)}, bf16[32,3072]{1,0:T(8,128)(2,1)S(1)}, u32[]{:S(2)}, u32[]{:S(2)}) %collective-permute-start.6) | collective-permute-done | bytes 196640 | tf_op jit(solution)/shard_map/ppermute | solution.py:334
  31.6 5.0 %collective-permute-done.7.refs_7_ = bf16[32,3072]{1,0:T(8,128)(2,1)S(1)} collective-permute-done((bf16[32,3072]{1,0:T(8,128)(2,1)S(1)}, bf16[32,3072]{1,0:T(8,128)(2,1)S(1)}, u32[]{:S(2)}, u32[]{:S(2)}) %collective-permute-start.7) | collective-permute-done | bytes 196640 | tf_op jit(solution)/shard_map/ppermute | solution.py:332
  36.6 3.5 %shard_map.75 = (bf16[256,1536]{1,0:T(8,128)(2,1)S(1)}, bf16[256,3072]{1,0:T(8,128)(2,1)S(1)}) custom-call(s32[3]{0:T(128)S(1)} %pad_add_fusion.info_ref, bf16[32,3072]{1,0:T(8,128)(2,1)S(1)} %bitcast.18, bf16[32,3072]{1,0:T(8,128)(2,1)S(1)} %collective-permute-done.2.refs_1_, bf16[32,3072]{1,0:T(8,128)(2,1)S(1)} %collective-permute-done.4.refs_2_, ...), custom_call_target="tpu_custom_call" | custom-call | flops 2415919104 | bytes 9437184 | tf_op jit(solution)/shard_map/pallas_call | solution.py:104
  40.2 3.4 %shard_map.76.own_ref = f32[256,1536]{1,0:T(8,128)S(1)} custom-call(s32[3]{0:T(128)S(1)} %pad_add_fusion.info_ref, bf16[256,3072]{1,0:T(8,128)(2,1)S(1)} %get-tuple-element.33.tokens_ref, bf16[1536,3072]{1,0:T(8,128)(2,1)S(1)} %shard_map.73.refs_8_.upper_ref, bf16[1536,3072]{1,0:T(8,128)(2,1)S(1)} %shard_map.74.refs_9_.lower_ref), custom_call_target="tpu_custom_call" | custom-call | flops 2415919104 | bytes 9437184 | tf_op jit(solution)/shard_map/pallas_call | solution.py:137
  43.6 4.3 %shard_map.77 = (bf16[256,1536]{1,0:T(8,128)(2,1)S(1)}, bf16[1536,3072]{1,0:T(8,128)(2,1)S(1)}) custom-call(s32[3]{0:T(128)S(1)} %pad_add_fusion.info_ref, f32[256,1536]{1,0:T(8,128)S(1)} %shard_map.76.own_ref, bf16[256,1536]{1,0:T(8,128)(2,1)S(1)} %collective-permute-done.8.received_ref, f32[1,3072]{1,0:T(1,128)S(1)} %bitcast.19, ...), custom_call_target="tpu_custom_call" | custom-call | flops 23592960 | bytes 3145728 | tf_op jit(solution)/shard_map/pallas_call | solution.py:207
  48.5 4.3 %shard_map.78 = (f32[256,3072]{1,0:T(8,128)S(1)}, bf16[1536,3072]{1,0:T(8,128)(2,1)S(1)}) custom-call(s32[3]{0:T(128)S(1)} %pad_add_fusion.info_ref, bf16[256,1536]{1,0:T(8,128)(2,1)S(1)} %get-tuple-element.35.mixed_ref, bf16[1536,3072]{1,0:T(8,128)(2,1)S(1)} %get-tuple-element.36.weight_ref, bf16[3072,3072]{1,0:T(8,128)(2,1)} %later_ref.3), custom_call_target="tpu_custom_call" | custom-call | flops 2415919104 | bytes 9437184 | tf_op jit(solution)/shard_map/pallas_call | solution.py:240
  52.9 3.0 %shard_map.79 = (f32[128,3072]{1,0:T(8,128)S(1)}, bf16[128,3072]{1,0:T(8,128)(2,1)S(1)}) custom-call(bf16[256,1536]{1,0:T(8,128)(2,1)S(1)} %collective-permute-done.9.mixed_ref, bf16[1536,3072]{1,0:T(8,128)(2,1)S(1)} %get-tuple-element.37.weight_ref, f32[256,3072]{1,0:T(8,128)S(1)} %get-tuple-element.38.partial_ref), custom_call_target="tpu_custom_call" | custom-call | flops 2415919104 | bytes 9437184 | tf_op jit(solution)/shard_map/pallas_call | solution.py:277
  56.7 1.3 %collective-permute-start.12 = (bf16[32,3072]{1,0:T(8,128)(2,1)S(1)}, bf16[32,3072]{1,0:T(8,128)(2,1)S(1)}, u32[]{:S(2)}, u32[]{:S(2)}) collective-permute-start(bf16[32,3072]{1,0:T(8,128)(2,1)S(1)} %get-tuple-element.43), channel_id=1, source_target_pairs={{0,1},{1,0},{2,3},{3,2},{4,5},{5,4},{6,7},{7,6},{8,9},{9,8},{10,11... | collective-permute-start | bytes 589832 | tf_op jit(solution)/shard_map/ppermute | solution.py:376
  58.0 5.7 %collective-permute-done.13 = bf16[32,3072]{1,0:T(8,128)(2,1)S(1)} collective-permute-done((bf16[32,3072]{1,0:T(8,128)(2,1)S(1)}, bf16[32,3072]{1,0:T(8,128)(2,1)S(1)}, u32[]{:S(2)}, u32[]{:S(2)}) %collective-permute-start.13) | collective-permute-done | bytes 196640 | tf_op jit(solution)/shard_map/ppermute | solution.py:376
  64.7 3.3 %collective-permute-done.12 = bf16[32,3072]{1,0:T(8,128)(2,1)S(1)} collective-permute-done((bf16[32,3072]{1,0:T(8,128)(2,1)S(1)}, bf16[32,3072]{1,0:T(8,128)(2,1)S(1)}, u32[]{:S(2)}, u32[]{:S(2)}) %collective-permute-start.12) | collective-permute-done | bytes 196640 | tf_op jit(solution)/shard_map/ppermute | solution.py:376
  68.0 3.4 %collective-permute-done.14 = bf16[32,3072]{1,0:T(8,128)(2,1)S(1)} collective-permute-done((bf16[32,3072]{1,0:T(8,128)(2,1)S(1)}, bf16[32,3072]{1,0:T(8,128)(2,1)S(1)}, u32[]{:S(2)}, u32[]{:S(2)}) %collective-permute-start.14) | collective-permute-done | bytes 196640 | tf_op jit(solution)/shard_map/ppermute | solution.py:380
  72.3 6.7 %collective-permute-done.15 = bf16[32,3072]{1,0:T(8,128)(2,1)S(1)} collective-permute-done((bf16[32,3072]{1,0:T(8,128)(2,1)S(1)}, bf16[32,3072]{1,0:T(8,128)(2,1)S(1)}, u32[]{:S(2)}, u32[]{:S(2)}) %collective-permute-start.15) | collective-permute-done | bytes 196640 | tf_op jit(solution)/shard_map/ppermute | solution.py:380
  79.1 7.4 %collective-permute-done.16 = bf16[32,3072]{1,0:T(8,128)(2,1)S(1)} collective-permute-done((bf16[32,3072]{1,0:T(8,128)(2,1)S(1)}, bf16[32,3072]{1,0:T(8,128)(2,1)S(1)}, u32[]{:S(2)}, u32[]{:S(2)}) %collective-permute-start.16) | collective-permute-done | bytes 196640 | tf_op jit(solution)/shard_map/ppermute | solution.py:380
  86.7 1.3 %collective-permute-done.17 = bf16[1,16,3072]{2,1,0:T(8,128)(2,1)S(1)} collective-permute-done((bf16[1,16,3072]{2,1,0:T(8,128)(2,1)S(1)}, bf16[1,16,3072]{2,1,0:T(8,128)(2,1)S(1)}, u32[]{:S(2)}, u32[]{:S(2)}) %collective-permute-start.17) | collective-permute-done | bytes 98336 | tf_op jit(solution)/shard_map/ppermute | solution.py:385
  (37 shorter events, 6.9 us)
Async XLA Ops:
  1.0 1.5 %collective-permute-start = (bf16[16,3072]{1,0:T(8,128)(2,1)S(1)}, bf16[16,3072]{1,0:T(8,128)(2,1)S(1)}, u32[]{:S(2)}, u32[]{:S(2)}) collective-permute-start(bf16[16,3072]{1,0:T(8,128)(2,1)S(1)} %get-tuple-element.48), channel_id=1, source_target_pairs={{0,8},{8,0},{1,9},{9,1},{2,10},{10,2},{3,11},{11,3},{4,12},{12,4},... | collective-permute-start | bytes 294920 | tf_op jit(solution)/shard_map/ppermute | solution.py:312
  2.4 8.9 %collective-permute-start.1 = (bf16[32,3072]{1,0:T(8,128)(2,1)S(1)}, bf16[32,3072]{1,0:T(8,128)(2,1)S(1)}, u32[]{:S(2)}, u32[]{:S(2)}) collective-permute-start(bf16[32,3072]{1,0:T(8,128)(2,1)S(1)} %bitcast.16), channel_id=1, source_target_pairs={{0,1},{1,0},{2,3},{3,2},{4,5},{5,4},{6,7},{7,6},{8,9},{9,8},{10,11... | collective-permute-start | bytes 589832 | tf_op jit(solution)/shard_map/ppermute | solution.py:332
  5.4 8.5 %collective-permute-start.2 = (bf16[32,3072]{1,0:T(8,128)(2,1)S(1)}, bf16[32,3072]{1,0:T(8,128)(2,1)S(1)}, u32[]{:S(2)}, u32[]{:S(2)}) collective-permute-start(bf16[32,3072]{1,0:T(8,128)(2,1)S(1)} %bitcast.17), channel_id=1, source_target_pairs={{0,2},{1,3},{2,4},{3,5},{4,6},{5,7},{6,0},{7,1},{8,10},{9,11},{10,... | collective-permute-start | bytes 589832 | tf_op jit(solution)/shard_map/ppermute | solution.py:334
  13.9 5.9 %collective-permute-start.3 = (bf16[32,3072]{1,0:T(8,128)(2,1)S(1)}, bf16[32,3072]{1,0:T(8,128)(2,1)S(1)}, u32[]{:S(2)}, u32[]{:S(2)}) collective-permute-start(bf16[32,3072]{1,0:T(8,128)(2,1)S(1)} %collective-permute-done.2.refs_1_), channel_id=1, source_target_pairs={{0,1},{1,0},{2,3},{3,2},{4,5},{5,4},{6,7},{7,6},{8,9},{9,8},{10,11... | collective-permute-start | bytes 589832 | tf_op jit(solution)/shard_map/ppermute | solution.py:332
  14.4 7.7 %collective-permute-start.4 = (bf16[32,3072]{1,0:T(8,128)(2,1)S(1)}, bf16[32,3072]{1,0:T(8,128)(2,1)S(1)}, u32[]{:S(2)}, u32[]{:S(2)}) collective-permute-start(bf16[32,3072]{1,0:T(8,128)(2,1)S(1)} %collective-permute-done.2.refs_1_), channel_id=1, source_target_pairs={{0,2},{1,3},{2,4},{3,5},{4,6},{5,7},{6,0},{7,1},{8,10},{9,11},{10,... | collective-permute-start | bytes 589832 | tf_op jit(solution)/shard_map/ppermute | solution.py:334
  22.1 5.7 %collective-permute-start.5 = (bf16[32,3072]{1,0:T(8,128)(2,1)S(1)}, bf16[32,3072]{1,0:T(8,128)(2,1)S(1)}, u32[]{:S(2)}, u32[]{:S(2)}) collective-permute-start(bf16[32,3072]{1,0:T(8,128)(2,1)S(1)} %collective-permute-done.4.refs_2_), channel_id=1, source_target_pairs={{0,1},{1,0},{2,3},{3,2},{4,5},{5,4},{6,7},{7,6},{8,9},{9,8},{10,11... | collective-permute-start | bytes 589832 | tf_op jit(solution)/shard_map/ppermute | solution.py:332
  23.4 7.5 %collective-permute-start.6 = (bf16[32,3072]{1,0:T(8,128)(2,1)S(1)}, bf16[32,3072]{1,0:T(8,128)(2,1)S(1)}, u32[]{:S(2)}, u32[]{:S(2)}) collective-permute-start(bf16[32,3072]{1,0:T(8,128)(2,1)S(1)} %collective-permute-done.4.refs_2_), channel_id=1, source_target_pairs={{0,2},{1,3},{2,4},{3,5},{4,6},{5,7},{6,0},{7,1},{8,10},{9,11},{10,... | collective-permute-start | bytes 589832 | tf_op jit(solution)/shard_map/ppermute | solution.py:334
  30.9 5.7 %collective-permute-start.7 = (bf16[32,3072]{1,0:T(8,128)(2,1)S(1)}, bf16[32,3072]{1,0:T(8,128)(2,1)S(1)}, u32[]{:S(2)}, u32[]{:S(2)}) collective-permute-start(bf16[32,3072]{1,0:T(8,128)(2,1)S(1)} %collective-permute-done.6.refs_3_), channel_id=1, source_target_pairs={{0,1},{1,0},{2,3},{3,2},{4,5},{5,4},{6,7},{7,6},{8,9},{9,8},{10,11... | collective-permute-start | bytes 589832 | tf_op jit(solution)/shard_map/ppermute | solution.py:332
  40.1 3.5 %collective-permute-start.8 = (bf16[256,1536]{1,0:T(8,128)(2,1)S(1)}, bf16[256,1536]{1,0:T(8,128)(2,1)S(1)}, u32[]{:S(2)}, u32[]{:S(2)}) collective-permute-start(bf16[256,1536]{1,0:T(8,128)(2,1)S(1)} %get-tuple-element.34), channel_id=1, source_target_pairs={{0,8},{8,0},{1,9},{9,1},{2,10},{10,2},{3,11},{11,3},{4,12},{12,4},... | collective-permute-start | bytes 2359304 | tf_op jit(solution)/shard_map/ppermute | solution.py:350
  40.1 3.4 %copy-start = (f32[3,3,3072]{2,1,0:T(4,128)S(1)}, f32[3,3,3072]{2,1,0:T(4,128)}, u32[]{:S(2)}) copy-start(f32[3,3,3072]{2,1,0:T(4,128)} %weight_ref.5) | copy-start | bytes 331780
  40.1 3.4 %copy-start.1 = (f32[3072]{0:T(1024)S(1)}, f32[3072]{0:T(1024)}, u32[]{:S(2)}) copy-start(f32[3072]{0:T(1024)} %param.9) | copy-start | bytes 36868
  40.2 3.4 %copy-start.2 = (f32[3072]{0:T(1024)S(1)}, f32[3072]{0:T(1024)}, u32[]{:S(2)}) copy-start(f32[3072]{0:T(1024)} %param.11) | copy-start | bytes 36868
  47.9 4.9 %collective-permute-start.9 = (bf16[256,1536]{1,0:T(8,128)(2,1)S(1)}, bf16[256,1536]{1,0:T(8,128)(2,1)S(1)}, u32[]{:S(2)}, u32[]{:S(2)}) collective-permute-start(bf16[256,1536]{1,0:T(8,128)(2,1)S(1)} %get-tuple-element.35.mixed_ref), channel_id=1, source_target_pairs={{0,8},{8,0},{1,9},{9,1},{2,10},{10,2},{3,11},{11,3},{4,12},{12,4},... | collective-permute-start | bytes 2359304 | tf_op jit(solution)/shard_map/ppermute | solution.py:364
  55.9 30.7 %dynamic-slice-start = ((f32[6144]{0:T(1024)}, s32[]{:T(128)}), f32[3072]{0:T(1024)S(1)}, s32[]{:S(2)}) async-start(f32[6144]{0:T(1024)} %param.13, s32[]{:T(128)} %select_n.57), calls=%async_computation | async-start | bytes 25088 | tf_op jit(solution)/shard_map/dynamic_slice | solution.py:381
  56.0 7.8 %collective-permute-start.13 = (bf16[32,3072]{1,0:T(8,128)(2,1)S(1)}, bf16[32,3072]{1,0:T(8,128)(2,1)S(1)}, u32[]{:S(2)}, u32[]{:S(2)}) collective-permute-start(bf16[32,3072]{1,0:T(8,128)(2,1)S(1)} %get-tuple-element.42), channel_id=1, source_target_pairs={{0,1},{1,0},{2,3},{3,2},{4,5},{5,4},{6,7},{7,6},{8,9},{9,8},{10,11... | collective-permute-start | bytes 589832 | tf_op jit(solution)/shard_map/ppermute | solution.py:376
  56.7 11.3 %collective-permute-start.12 = (bf16[32,3072]{1,0:T(8,128)(2,1)S(1)}, bf16[32,3072]{1,0:T(8,128)(2,1)S(1)}, u32[]{:S(2)}, u32[]{:S(2)}) collective-permute-start(bf16[32,3072]{1,0:T(8,128)(2,1)S(1)} %get-tuple-element.43), channel_id=1, source_target_pairs={{0,1},{1,0},{2,3},{3,2},{4,5},{5,4},{6,7},{7,6},{8,9},{9,8},{10,11... | collective-permute-start | bytes 589832 | tf_op jit(solution)/shard_map/ppermute | solution.py:376
  63.8 7.5 %collective-permute-start.14 = (bf16[32,3072]{1,0:T(8,128)(2,1)S(1)}, bf16[32,3072]{1,0:T(8,128)(2,1)S(1)}, u32[]{:S(2)}, u32[]{:S(2)}) collective-permute-start(bf16[32,3072]{1,0:T(8,128)(2,1)S(1)} %add_convert_fusion.3), channel_id=1, source_target_pairs={{0,2},{1,3},{2,4},{3,5},{4,6},{5,7},{6,0},{7,1},{8,10},{9,11},{10,... | collective-permute-start | bytes 589832 | tf_op jit(solution)/shard_map/ppermute | solution.py:380
  63.9 8.4 %collective-permute-start.11 = (bf16[32,3072]{1,0:T(8,128)(2,1)S(1)}, bf16[32,3072]{1,0:T(8,128)(2,1)S(1)}, u32[]{:S(2)}, u32[]{:S(2)}) collective-permute-start(bf16[32,3072]{1,0:T(8,128)(2,1)S(1)} %get-tuple-element.44), channel_id=1, source_target_pairs={{0,1},{1,0},{2,3},{3,2},{4,5},{5,4},{6,7},{7,6},{8,9},{9,8},{10,11... | collective-permute-start | bytes 589832 | tf_op jit(solution)/shard_map/ppermute | solution.py:376
  71.4 7.5 %collective-permute-start.15 = (bf16[32,3072]{1,0:T(8,128)(2,1)S(1)}, bf16[32,3072]{1,0:T(8,128)(2,1)S(1)}, u32[]{:S(2)}, u32[]{:S(2)}) collective-permute-start(bf16[32,3072]{1,0:T(8,128)(2,1)S(1)} %add_convert_fusion.2), channel_id=1, source_target_pairs={{0,2},{1,3},{2,4},{3,5},{4,6},{5,7},{6,0},{7,1},{8,10},{9,11},{10,... | collective-permute-start | bytes 589832 | tf_op jit(solution)/shard_map/ppermute | solution.py:380
  71.5 7.6 %collective-permute-start.10 = (bf16[32,3072]{1,0:T(8,128)(2,1)S(1)}, bf16[32,3072]{1,0:T(8,128)(2,1)S(1)}, u32[]{:S(2)}, u32[]{:S(2)}) collective-permute-start(bf16[32,3072]{1,0:T(8,128)(2,1)S(1)} %get-tuple-element.41), channel_id=1, source_target_pairs={{0,1},{1,0},{2,3},{3,2},{4,5},{5,4},{6,7},{7,6},{8,9},{9,8},{10,11... | collective-permute-start | bytes 589832 | tf_op jit(solution)/shard_map/ppermute | solution.py:376
  79.0 7.5 %collective-permute-start.16 = (bf16[32,3072]{1,0:T(8,128)(2,1)S(1)}, bf16[32,3072]{1,0:T(8,128)(2,1)S(1)}, u32[]{:S(2)}, u32[]{:S(2)}) collective-permute-start(bf16[32,3072]{1,0:T(8,128)(2,1)S(1)} %add_convert_fusion.1), channel_id=1, source_target_pairs={{0,2},{1,3},{2,4},{3,5},{4,6},{5,7},{6,0},{7,1},{8,10},{9,11},{10,... | collective-permute-start | bytes 589832 | tf_op jit(solution)/shard_map/ppermute | solution.py:380
  86.7 1.4 %collective-permute-start.17 = (bf16[1,16,3072]{2,1,0:T(8,128)(2,1)S(1)}, bf16[1,16,3072]{2,1,0:T(8,128)(2,1)S(1)}, u32[]{:S(2)}, u32[]{:S(2)}) collective-permute-start(bf16[1,16,3072]{2,1,0:T(8,128)(2,1)S(1)} %get-tuple-element.46), channel_id=1, source_target_pairs={{0,8},{8,0},{1,9},{9,1},{2,10},{10,2},{3,11},{11,3},{4,12},{12,4},... | collective-permute-start | bytes 294920 | tf_op jit(solution)/shard_map/ppermute | solution.py:385

commit v2 on v1

--- a/solution.py
+++ b/solution.py
@@ -1,5 +1,3 @@
-import functools
-
 import jax
 import jax.numpy as jnp
 from jax import lax
@@ -74,65 +72,91 @@
     )(info, weight)
 
 
-def up_other(info, slots, upper, lower, width):
-    rows = slots[0].shape[0]
-    depth = slots[0].shape[1]
+def gathered_rows(slot_refs, tokens_ref):
+    rows = slot_refs[0].shape[0]
+    for index, ref in enumerate(slot_refs):
+        tokens_ref[index * rows : (index + 1) * rows, :] = ref[...]
+
+
+def tiles(total, width, most, body):
+    tile = tile_of(width, most)
+    high = tile_of(total, 256)
+
+    def step_body(step, carry):
+        row, col = step // (width // tile), step % (width // tile)
+        body(pl.ds(pl.multiple_of(row * high, high), high), pl.multiple_of(col * tile, tile), tile)
+        return carry
+
+    lax.fori_loop(0, (total // high) * (width // tile), step_body, 0)
+
+
+def up_first(slots, weight):
+    rows, depth = slots[0].shape
     total = rows * len(slots)
-    split = upper.shape[0]
-    tile = tile_of(width, 768)
-    high = tile_of(total, 256)
+    width = weight.shape[1]
+
+    def kernel(*refs):
+        weight_ref, out_ref, tokens_ref = refs[len(slots) :]
+        gathered_rows(refs[: len(slots)], tokens_ref)
+
+        def body(down, col, tile):
+            out_ref[down, pl.ds(col, tile)] = jnp.dot(
+                tokens_ref[down, :], weight_ref[:, pl.ds(col, tile)], preferred_element_type=F32
+            )
+
+        tiles(total, width, 1024, body)
+
+    return pl.pallas_call(
+        kernel,
+        out_shape=pltpu.VMEM((total, width), F32),
+        in_specs=[VMEM] * (len(slots) + 1),
+        out_specs=VMEM,
+        scratch_shapes=[pltpu.VMEM((total, depth), BF16)],
+        cost_estimate=cost(2 * total * depth * width, 2 * depth * width),
+        compiler_params=params(12),
+    )(*slots, weight)
+
+
+def up_other(info, slots, weight, partial):
+    rows, depth = slots[0].shape
+    total = rows * len(slots)
+    width = weight.shape[1] // 2
 
     def kernel(info_ref, *refs):
-        slot_refs = refs[: len(slots)]
-        upper_ref, lower_ref, out_ref, tokens_ref = refs[len(slots) :]
-        for index, ref in enumerate(slot_refs):
-            tokens_ref[index * rows : (index + 1) * rows, :] = ref[...]
+        weight_ref, partial_ref, out_ref, tokens_ref = refs[len(slots) :]
+        gathered_rows(refs[: len(slots)], tokens_ref)
         base = (1 - info_ref[0]) * width
 
-        def body(step, carry):
-            row, col = step // (width // tile), step % (width // tile)
-            down = pl.ds(pl.multiple_of(row * high, high), high)
-            across = pl.ds(pl.multiple_of(base + col * tile, 128), tile)
-            product = jnp.dot(tokens_ref[down, :split], upper_ref[:, across], preferred_element_type=F32) + jnp.dot(
-                tokens_ref[down, split:], lower_ref[:, across], preferred_element_type=F32
-            )
-            out_ref[down, pl.ds(pl.multiple_of(col * tile, 128), tile)] = product.astype(BF16)
-            return carry
-
-        lax.fori_loop(0, (total // high) * (width // tile), body, 0)
-
-    return pl.pallas_call(
-        kernel,
-        out_shape=(
-            pltpu.VMEM((total, width), BF16),
-            pltpu.VMEM((total, depth), BF16),
-        ),
+        def body(down, col, tile):
+            across = pl.ds(pl.multiple_of(base + col, 128), tile)
+            product = jnp.dot(tokens_ref[down, :], weight_ref[:, across], preferred_element_type=F32)
+            out_ref[down, pl.ds(col, tile)] = (partial_ref[down, across] + product).astype(BF16)
+
+        tiles(total, width, 768, body)
+
+    return pl.pallas_call(
+        kernel,
+        out_shape=(pltpu.VMEM((total, width), BF16), pltpu.VMEM((total, depth), BF16)),
         in_specs=[SMEM] + [VMEM] * (len(slots) + 2),
         out_specs=(VMEM, VMEM),
         cost_estimate=cost(2 * total * depth * width, 2 * depth * width),
         compiler_params=params(12),
-    )(info, *slots, upper, lower)
-
-
-def up_own(info, tokens, upper, lower, width):
+    )(info, *slots, weight, partial)
+
+
+def up_own(info, tokens, weight, partial):
     total, depth = tokens.shape
-    split = upper.shape[0]
-    tile = tile_of(width, 768)
-    high = tile_of(total, 256)
-
-    def kernel(info_ref, tokens_ref, upper_ref, lower_ref, out_ref):
+    width = weight.shape[1] // 2
+
+    def kernel(info_ref, tokens_ref, weight_ref, partial_ref, out_ref):
         base = info_ref[0] * width
 
-        def body(step, carry):
-            row, col = step // (width // tile), step % (width // tile)
-            down = pl.ds(pl.multiple_of(row * high, high), high)
-            across = pl.ds(pl.multiple_of(base + col * tile, 128), tile)
-            out_ref[down, pl.ds(pl.multiple_of(col * tile, 128), tile)] = jnp.dot(
-                tokens_ref[down, :split], upper_ref[:, across], preferred_element_type=F32
-            ) + jnp.dot(tokens_ref[down, split:], lower_ref[:, across], preferred_element_type=F32)
-            return carry
-
-        lax.fori_loop(0, (total // high) * (width // tile), body, 0)
+        def body(down, col, tile):
+            across = pl.ds(pl.multiple_of(base + col, 128), tile)
+            product = jnp.dot(tokens_ref[down, :], weight_ref[:, across], preferred_element_type=F32)
+            out_ref[down, pl.ds(col, tile)] = partial_ref[down, across] + product
+
+        tiles(total, width, 768, body)
 
     return pl.pallas_call(
         kernel,
@@ -141,7 +165,7 @@
         out_specs=VMEM,
         cost_estimate=cost(2 * total * depth * width, 2 * depth * width),
         compiler_params=params(12),
-    )(info, tokens, upper, lower)
+    )(info, tokens, weight, partial)
 
 
 def gelu(value):
@@ -248,63 +272,169 @@
     )(info, mixed, weight, later)
 
 
-def down_other(mixed, weight, partial, kept):
+def down_other(mixed, weight, partial, blocks, kept, start, width):
     total, depth = mixed.shape
-    width = weight.shape[1]
-    tile = tile_of(width, 1024)
-
-    def kernel(mixed_ref, weight_ref, partial_ref, keep_ref, *send_refs):
-        def body(col, carry):
-            across = pl.ds(pl.multiple_of(col * tile, tile), tile)
+    rows = total // blocks
+    tile = tile_of(width, 768)
+
+    def kernel(mixed_ref, weight_ref, partial_ref, *out_refs):
+        def body(step, carry):
+            col = pl.multiple_of(step * tile, tile)
+            across = pl.ds(pl.multiple_of(start + col, 128), tile)
+            here = pl.ds(col, tile)
             for first in range(0, total, 256):
                 high = min(256, total - first)
                 value = partial_ref[first : first + high, across] + jnp.dot(
                     mixed_ref[first : first + high, :], weight_ref[:, across], preferred_element_type=F32
                 )
-                inside = max(0, min(high, kept - first))
-                if inside:
-                    keep_ref[first : first + inside, across] = value[:inside]
-                if inside < high:
-                    low = first + inside - kept
-                    send_refs[0][low : low + high - inside, across] = value[inside:].astype(BF16)
+                for low in range(0, high, rows):
+                    out_ref = out_refs[(first + low) // rows]
+                    out_ref[:, here] = value[low : low + rows].astype(out_ref.dtype)
             return carry
 
         lax.fori_loop(0, width // tile, body, 0)
 
-    shapes = [pltpu.VMEM((kept, width), F32)]
-    if kept < total:
-        shapes.append(pltpu.VMEM((total - kept, width), BF16))
-    return pl.pallas_call(
-        kernel,
-        out_shape=tuple(shapes),
+    return pl.pallas_call(
+        kernel,
+        out_shape=tuple(pltpu.VMEM((rows, width), F32 if block < kept else BF16) for block in range(blocks)),
         in_specs=[VMEM] * 3,
-        out_specs=(VMEM,) * len(shapes),
+        out_specs=(VMEM,) * blocks,
         cost_estimate=cost(2 * total * depth * width, 2 * depth * width),
         compiler_params=params(12),
     )(mixed, weight, partial)
 
 
+def finish(info, totals, bias, cols, grid_half):
+    width = totals[0].shape[1]
+    half = width * len(totals)
+
+    def kernel(info_ref, *refs):
+        bias_ref, stay_ref, leave_ref = refs[len(totals) :]
+        core = info_ref[0]
+        for index in range(len(totals)):
+            shift = bias_ref[:, pl.ds(pl.multiple_of(core * half + index * width, 128), width)]
+            for col in range(cols):
+                for out_ref, side in ((stay_ref, core), (leave_ref, 1 - core)):
+                    source = pl.ds(pl.multiple_of((2 * col + side) * grid_half, 8), grid_half)
+                    out_ref[col, :, index * width : (index + 1) * width] = (refs[index][source, :] + shift).astype(BF16)
+
+    return pl.pallas_call(
+        kernel,
+        out_shape=(pltpu.VMEM((cols, grid_half, half), BF16),) * 2,
+        in_specs=[SMEM] + [VMEM] * (len(totals) + 1),
+        out_specs=(VMEM, VMEM),
+        cost_estimate=cost(4 * cols * grid_half * half, 8 * cols * grid_half * half),
+        compiler_params=params(4),
+    )(info, *totals, bias)
+
+
 def tie(*values):
     return lax.optimization_barrier(values)
+
+
+class Links:
+    def __init__(self, count):
+        self.lanes = 2 if count % 2 == 0 else 1
+        self.ring = count // self.lanes
+        self.upward = [(t, (t + self.lanes) % count) for t in range(count)]
+        self.downward = [(t, s) for s, t in self.upward]
+        self.pairs = [(t, t ^ 1) for t in range(count)]
+
+    def up(self, value):
+        return lax.ppermute(value, "tp", self.upward)
+
+    def down(self, value):
+        return lax.ppermute(value, "tp", self.downward)
+
+    def cross(self, value):
+        return lax.ppermute(value, "tp", self.pairs)
+
+
+def gather_steps(links, block, tree, extras):
+    ring = links.ring
+    tree = tree and links.lanes > 1 and ring > 2
+    column, beside = {0: block}, {}
+    for step in range(1, ring + 1):
+        moves = []
+        if step < ring:
+            moves.append((column, step, links.up(column[step - 1])))
+        if links.lanes > 1 and not (tree and step == ring):
+            moves.append((beside, step - 1, links.cross(column[step - 1])))
+        if tree and step == 2:
+            moves.append((beside, ring - 1, links.down(beside[0])))
+        made = extras.get(step)
+        yield
+        values = [value for _, _, value in moves]
+        if made is not None:
+            values.append(made())
+        if not values:
+            continue
+        done = tie(*values)
+        for (where, slot, _), value in zip(moves, done):
+            where[slot] = value
+        if made is not None:
+            extras[step] = done[-1]
+    yield [column[j] for j in range(ring)] + [beside[j] for j in range(ring) if links.lanes > 1]
+
+
+def scatter_steps(links, kept, sent, tree):
+    ring = links.ring
+    sent = list(sent)
+    if tree and links.lanes > 1 and ring > 2:
+        total = kept[ring - 1]
+        for slot in range(ring - 2, -1, -1):
+            moves = [links.down(total.astype(BF16)), links.cross(sent[slot])]
+            if slot == 1:
+                moves.append(links.up(sent[ring - 1]))
+            yield
+            count = len(moves)
+            arrived = tie(*moves, *sent)
+            moves, sent = arrived[:count], list(arrived[count:])
+            total = kept[slot] + moves[0].astype(F32) + moves[1].astype(F32)
+            if slot == 1:
+                sent[0] = (sent[0].astype(F32) + moves[2].astype(F32)).astype(BF16)
+    else:
+        total = None
+        for slot in list(range(1, ring)) + [0]:
+            moves = [links.cross(sent[slot])] if links.lanes > 1 else []
+            if total is not None:
+                moves.append(links.up(total.astype(BF16)))
+            yield
+            count = len(moves)
+            arrived = tie(*moves, *sent) if moves else tuple(sent)
+            moves, sent = arrived[:count], list(arrived[count:])
+            total = kept[slot]
+            for value in moves:
+                total = total + value.astype(F32)
+    yield total
+
+
+def interleave(streams):
+    results = [None] * len(streams)
+    live = list(range(len(streams)))
+    while live:
+        for index in list(live):
+            try:
+                results[index] = next(streams[index])
+            except StopIteration:
+                live.remove(index)
+    return results
 
 
 def local(tokens, up_weight, up_bias, conv_weight, conv_bias, down_weight, down_bias):
     cols, grid_half, width_model = tokens.shape
     half = width_model // 2
+    part = half // 2
     units = up_weight.shape[1]
     units_half = units // 2
     grid_y = grid_half * 2
     rows = cols * grid_y
 
-    count = lax.axis_size("tp")
-    lanes = 2 if count % 2 == 0 else 1
-    ring_size = count // lanes
+    links = Links(lax.axis_size("tp"))
     core = lax.axis_index("sp")
     mine = lax.axis_index("tp")
-    ring_at, lane_at = mine // lanes, mine % lanes
-    ring = [(t, (t + lanes) % count) for t in range(count)]
-    cross = [(t, t ^ 1) for t in range(count)]
     swap = [(0, 1), (1, 0)]
+    info = jnp.stack([core, mine // links.lanes, mine % links.lanes]).astype(jnp.int32)
 
     flat = tokens.reshape(cols * grid_half, width_model)
     keep = lax.dynamic_slice_in_dim(flat, core * half, half, axis=1)
@@ -313,42 +443,23 @@
     keep, take = (x.reshape(cols, 1, grid_half, half) for x in (keep, take))
     block = jnp.where(core == 0, jnp.concatenate([keep, take], 1), jnp.concatenate([take, keep], 1))
     block = block.reshape(rows, half)
-
-    info = jnp.stack([core, ring_at, lane_at]).astype(jnp.int32)
-    block, info = tie(block, info)
-
-    up_split = half // 2
-    up_bytes = up_split * units * 2
-    fetches = [
-        lambda: fetch(info, up_weight, lambda c: 0 * c, up_split, 0),
-        lambda: fetch(info, up_weight, lambda c: 0 * c + up_split, up_split, up_bytes),
-    ]
-
-    column, beside, fetched = [block], [], []
-    for step in range(ring_size):
-        current = column[-1]
-        pending = []
-        if lanes > 1:
-            pending.append(lax.ppermute(current, "tp", cross))
-        if step < ring_size - 1:
-            pending.append(lax.ppermute(current, "tp", ring))
-        if fetches:
-            fetched.append(fetches.pop(0)())
-            pending.append(fetched[-1])
-        done = list(tie(*pending))
-        if lanes > 1:
-            beside.append(done.pop(0))
-        if step < ring_size - 1:
-            column.append(done.pop(0))
-        if done:
-            fetched[-1] = done.pop(0)
-    fetched += [make() for make in fetches]
-    upper, lower = fetched
-    slots = column + beside
-
-    partial_other, gathered = up_other(info, slots, upper, lower, units_half)
+    block_a, block_b, info = tie(block[:, :part], block[:, part:], info)
+
+    part_bytes = part * units * 2
+    extras_a = {}
+    extras_b = {
+        1: lambda: fetch(info, up_weight, lambda c: 0 * c, part, 0),
+        2: lambda: fetch(info, up_weight, lambda c: 0 * c + part, part, part_bytes),
+    }
+    slots_a, slots_b = interleave(
+        [gather_steps(links, block_a, False, extras_a), gather_steps(links, block_b, True, extras_b)]
+    )
+    upper, lower = (made if not callable(made) else made() for made in (extras_b[1], extras_b[2]))
+
+    first = up_first(slots_a, upper)
+    partial_other, tokens_b = up_other(info, slots_b, lower, first)
     partial_received = lax.ppermute(partial_other, "sp", swap)
-    partial_own = up_own(info, gathered, upper, lower, units_half)
+    partial_own = up_own(info, tokens_b, lower, first)
     mixed, down_mine = conv(
         info,
         partial_own,
@@ -357,31 +468,20 @@
         conv_weight,
         conv_bias.reshape(1, units),
         down_weight,
-        ring_size,
-        lanes,
+        links.ring,
+        links.lanes,
         grid_y,
     )
     mixed_received = lax.ppermute(mixed, "sp", swap)
     product, down_theirs = down_own(info, mixed, down_mine, down_weight)
-    sums = down_other(mixed_received, down_theirs, product, ring_size * rows)
-    kept = sums[0].reshape(ring_size, rows, half)
-
-    order = list(range(1, ring_size)) + [0]
-    if lanes > 1:
-        sent = sums[1].reshape(ring_size, rows, half)
-    travelling = None
-    for position, j in enumerate(order):
-        value = kept[j]
-        if lanes > 1:
-            value = value + lax.ppermute(sent[j], "tp", cross).astype(F32)
-        if travelling is not None:
-            value = value + travelling.astype(F32)
-        if position < ring_size - 1:
-            travelling = lax.ppermute(value.astype(BF16), "tp", ring)
-    bias = lax.dynamic_slice_in_dim(down_bias, core * half, half)
-    final = (value + bias).astype(BF16).reshape(cols, 2, grid_half, half)
-    stay = lax.dynamic_index_in_dim(final, core, 1, keepdims=False)
-    leave = lax.dynamic_index_in_dim(final, 1 - core, 1, keepdims=False)
+
+    streams = []
+    for start, tree in ((0, False), (part, True)):
+        sums = down_other(mixed_received, down_theirs, product, len(slots_a), links.ring, start, part)
+        streams.append(scatter_steps(links, sums[: links.ring], sums[links.ring :], tree))
+    totals = interleave(streams)
+
+    stay, leave = finish(info, totals, down_bias.reshape(1, width_model), cols, grid_half)
     arrive = lax.ppermute(leave, "sp", swap)
     return jnp.where(core == 0, jnp.concatenate([stay, arrive], -1), jnp.concatenate([arrive, stay], -1))
 

time: 88.9 us -> 85.8 us (0.965)
  waiting for transfers between devices: 47.1 us -> 20.2 us
  starting transfers between devices: 12.1 us -> 34.4 us
  Pallas kernels: 27.2 us -> 28.7 us
    ppermute x14 -> x28, waiting for transfers between devices: 44.9 us -> 18 us  [the longest x10 10.8 us: up(): return lax.ppermute(value, 'tp', self.upward)]
    ppermute x14 -> x28, starting transfers between devices: 10.8 us -> 33.2 us  [the longest x14 15.5 us: cross(): return lax.ppermute(value, 'tp', self.pairs)]
    pallas_call x1 -> x4, Pallas kernels: 2.99 us -> 6.9 us  [the longest x2 3.23 us: down_other(): pl.pallas_call(kernel, out_shape=tuple((pltpu.VMEM((rows, width), F32 if...]
    pallas_call x1, Pallas kernels: 3.49 us -> 2.24 us  [up_other(): pl.pallas_call(kernel, out_shape=(pltpu.VMEM((total, width), BF16), pltpu...]
    pallas_call x1, Pallas kernels: 3.36 us -> 2.17 us  [up_own(): pl.pallas_call(kernel, out_shape=pltpu.VMEM((total, width), F32), in_spec...]
  transfers between devices with their start and end apart: 18 -> 32, of which waited for: 13 -> 14; matrix products, arithmetic and copies ran while one was open for 0% -> 0% of each run, Pallas kernels for 18% -> 20%
where the time goes in v2:
time: 85.8 us; the launch traced here: 85.7 us
  starting transfers between devices  34.4 us (40%)
  Pallas kernels  28.7 us (33%)
  waiting for transfers between devices  20.2 us (24%)
  other arithmetic  1.1 us (1%)
  local copies, waits for them, and re-layouts  0.99 us (1%)
    ppermute x14, starting transfers between devices, cross(): return lax.ppermute(value, 'tp', self.pairs)  15.5 us
    ppermute x10, waiting for transfers between devices, up(): return lax.ppermute(value, 'tp', self.upward)  10.8 us
    ppermute x10, starting transfers between devices, up(): return lax.ppermute(value, 'tp', self.upward)  10.2 us
    pallas_call x2, Pallas kernels, fetch(): pl.pallas_call(kernel, out_shape=pltpu.VMEM((count, weight.shape[1]), wei...  8.68 us
    ppermute x4, starting transfers between devices, down(): return lax.ppermute(value, 'tp', self.downward)  7.44 us
    ppermute x14, waiting for transfers between devices, cross(): return lax.ppermute(value, 'tp', self.pairs)  4.99 us
    pallas_call x1, Pallas kernels, conv(): pl.pallas_call(kernel, out_shape=(pltpu.VMEM((total, width), BF16), pltpu...  4.35 us
    pallas_call x1, Pallas kernels, down_own(): pl.pallas_call(kernel, out_shape=(pltpu.VMEM((total, width), F32), pltpu....  4.35 us
  transfers between devices with their start and end apart: 32, of which 14 were waited for; matrix products, arithmetic and copies ran while one was open for 0% of the time, Pallas kernels for 20%

profile of v2, /device:TPU:0, one launch (start us, length us, event | category | flops | bytes accessed | tf_op | source)
XLA Modules:
  0.0 85.7 jit_solution(3557668619732622722)
XLA Ops:
  2.5 3.0 %collective-permute-start.8 = (bf16[32,1536]{1,0:T(8,128)(2,1)S(1)}, bf16[32,1536]{1,0:T(8,128)(2,1)S(1)}, u32[]{:S(2)}, u32[]{:S(2)}) collective-permute-start(bf16[32,1536]{1,0:T(8,128)(2,1)S(1)} %get-tuple-element.81.refs_0_), channel_id=1, source_target_pairs={{0,2},{1,3},{2,4},{3,5},{4,6},{5,7},{6,0},{7,1},{8,10},{9,11},{10,... | collective-permute-start | bytes 294920 | tf_op jit(solution)/shard_map/ppermute | solution.py:344
  7.0 1.6 %collective-permute-start.1 = (bf16[32,1536]{1,0:T(8,128)(2,1)S(1)}, bf16[32,1536]{1,0:T(8,128)(2,1)S(1)}, u32[]{:S(2)}, u32[]{:S(2)}) collective-permute-start(bf16[32,1536]{1,0:T(8,128)(2,1)S(1)} %get-tuple-element.72.refs_0_), channel_id=1, source_target_pairs={{0,2},{1,3},{2,4},{3,5},{4,6},{5,7},{6,0},{7,1},{8,10},{9,11},{10,... | collective-permute-start | bytes 294920 | tf_op jit(solution)/shard_map/ppermute | solution.py:344
  11.6 2.2 %collective-permute-start.11 = (bf16[32,1536]{1,0:T(8,128)(2,1)S(1)}, bf16[32,1536]{1,0:T(8,128)(2,1)S(1)}, u32[]{:S(2)}, u32[]{:S(2)}) collective-permute-start(bf16[32,1536]{1,0:T(8,128)(2,1)S(1)} %collective-permute-done.8.refs_1_), channel_id=1, source_target_pairs={{0,1},{1,0},{2,3},{3,2},{4,5},{5,4},{6,7},{7,6},{8,9},{9,8},{10,11... | collective-permute-start | bytes 294920 | tf_op jit(solution)/shard_map/ppermute | solution.py:350
  13.9 4.3 %shard_map.73.refs_8_ = bf16[1536,3072]{1,0:T(8,128)(2,1)S(1)} custom-call(s32[3]{0:T(128)S(1)} %pad_add_fusion.info_ref, bf16[3072,3072]{1,0:T(8,128)(2,1)} %weight_ref.4), custom_call_target="tpu_custom_call" | custom-call | bytes 18874368 | tf_op jit(solution)/shard_map/pallas_call | solution.py:64
  18.2 1.9 %collective-permute-start.3 = (bf16[32,1536]{1,0:T(8,128)(2,1)S(1)}, bf16[32,1536]{1,0:T(8,128)(2,1)S(1)}, u32[]{:S(2)}, u32[]{:S(2)}) collective-permute-start(bf16[32,1536]{1,0:T(8,128)(2,1)S(1)} %collective-permute-done.1.refs_1_), channel_id=1, source_target_pairs={{0,2},{1,3},{2,4},{3,5},{4,6},{5,7},{6,0},{7,1},{8,10},{9,11},{10,... | collective-permute-start | bytes 294920 | tf_op jit(solution)/shard_map/ppermute | solution.py:344
  20.5 1.6 %collective-permute-start.5 = (bf16[32,1536]{1,0:T(8,128)(2,1)S(1)}, bf16[32,1536]{1,0:T(8,128)(2,1)S(1)}, u32[]{:S(2)}, u32[]{:S(2)}) collective-permute-start(bf16[32,1536]{1,0:T(8,128)(2,1)S(1)} %collective-permute-done.2.refs_4_), channel_id=1, source_target_pairs={{2,0},{3,1},{4,2},{5,3},{6,4},{7,5},{0,6},{1,7},{10,8},{11,9},{12,... | collective-permute-start | bytes 294920 | tf_op jit(solution)/shard_map/ppermute | solution.py:347
  22.5 1.7 %collective-permute-start.13 = (bf16[32,1536]{1,0:T(8,128)(2,1)S(1)}, bf16[32,1536]{1,0:T(8,128)(2,1)S(1)}, u32[]{:S(2)}, u32[]{:S(2)}) collective-permute-start(bf16[32,1536]{1,0:T(8,128)(2,1)S(1)} %collective-permute-done.10.refs_2_), channel_id=1, source_target_pairs={{0,1},{1,0},{2,3},{3,2},{4,5},{5,4},{6,7},{7,6},{8,9},{9,8},{10,11... | collective-permute-start | bytes 294920 | tf_op jit(solution)/shard_map/ppermute | solution.py:350
  24.2 4.3 %shard_map.74.refs_8_.weight_ref = bf16[1536,3072]{1,0:T(8,128)(2,1)S(1)} custom-call(s32[3]{0:T(128)S(1)} %pad_add_fusion.info_ref, bf16[3072,3072]{1,0:T(8,128)(2,1)} %weight_ref.4), custom_call_target="tpu_custom_call" | custom-call | bytes 18874368 | tf_op jit(solution)/shard_map/pallas_call | solution.py:64
  29.2 1.9 %collective-permute-start.14 = (bf16[32,1536]{1,0:T(8,128)(2,1)S(1)}, bf16[32,1536]{1,0:T(8,128)(2,1)S(1)}, u32[]{:S(2)}, u32[]{:S(2)}) collective-permute-start(bf16[32,1536]{1,0:T(8,128)(2,1)S(1)} %collective-permute-done.12.refs_3_), channel_id=1, source_target_pairs={{0,1},{1,0},{2,3},{3,2},{4,5},{5,4},{6,7},{7,6},{8,9},{9,8},{10,11... | collective-permute-start | bytes 294920 | tf_op jit(solution)/shard_map/ppermute | solution.py:350
  31.1 4.0 %collective-permute-done.6.refs_3_ = bf16[32,1536]{1,0:T(8,128)(2,1)S(1)} collective-permute-done((bf16[32,1536]{1,0:T(8,128)(2,1)S(1)}, bf16[32,1536]{1,0:T(8,128)(2,1)S(1)}, u32[]{:S(2)}, u32[]{:S(2)}) %collective-permute-start.6) | collective-permute-done | bytes 98336 | tf_op jit(solution)/shard_map/ppermute | solution.py:344
  35.1 3.1 %shard_map.75.refs_9_.partial_ref = f32[256,3072]{1,0:T(8,128)S(1)} custom-call(bf16[32,1536]{1,0:T(8,128)(2,1)S(1)} %get-tuple-element.81.refs_0_, bf16[32,1536]{1,0:T(8,128)(2,1)S(1)} %collective-permute-done.8.refs_1_, bf16[32,1536]{1,0:T(8,128)(2,1)S(1)} %collective-permute-done.10.refs_2_, bf16[32,1536]{1,0:T(8,128)(2,1)S(1)} %collective-permute-done.12.refs_3_, ...), custom_call_target="tpu_custom_call" | custom-call | flops 2415919104 | bytes 9437184 | tf_op jit(solution)/shard_map/pallas_call | solution.py:109
  38.2 2.2 %shard_map.76 = (bf16[256,1536]{1,0:T(8,128)(2,1)S(1)}, bf16[256,1536]{1,0:T(8,128)(2,1)S(1)}) custom-call(s32[3]{0:T(128)S(1)} %pad_add_fusion.info_ref, bf16[32,1536]{1,0:T(8,128)(2,1)S(1)} %get-tuple-element.72.refs_0_, bf16[32,1536]{1,0:T(8,128)(2,1)S(1)} %collective-permute-done.1.refs_1_, bf16[32,1536]{1,0:T(8,128)(2,1)S(1)} %collective-permute-done.3.refs_2_, ...), custom_call_target="tpu_custom_call" | custom-call | flops 1207959552 | bytes 4718592 | tf_op jit(solution)/shard_map/pallas_call | solution.py:137
  40.5 2.2 %shard_map.77.own_ref = f32[256,1536]{1,0:T(8,128)S(1)} custom-call(s32[3]{0:T(128)S(1)} %pad_add_fusion.info_ref, bf16[256,1536]{1,0:T(8,128)(2,1)S(1)} %get-tuple-element.89.tokens_ref, bf16[1536,3072]{1,0:T(8,128)(2,1)S(1)} %shard_map.74.refs_8_.weight_ref, f32[256,3072]{1,0:T(8,128)S(1)} %shard_map.75.refs_9_.partial_ref), custom_call_target="tpu_custom_call" | custom-call | flops 1207959552 | bytes 4718592 | tf_op jit(solution)/shard_map/pallas_call | solution.py:161
  42.8 4.3 %shard_map.78 = (bf16[256,1536]{1,0:T(8,128)(2,1)S(1)}, bf16[1536,3072]{1,0:T(8,128)(2,1)S(1)}) custom-call(s32[3]{0:T(128)S(1)} %pad_add_fusion.info_ref, f32[256,1536]{1,0:T(8,128)S(1)} %shard_map.77.own_ref, bf16[256,1536]{1,0:T(8,128)(2,1)S(1)} %collective-permute-done.15.received_ref, f32[1,3072]{1,0:T(1,128)S(1)} %bitcast.13, ...), custom_call_target="tpu_custom_call" | custom-call | flops 23592960 | bytes 3145728 | tf_op jit(solution)/shard_map/pallas_call | solution.py:231
  47.7 4.3 %shard_map.79 = (f32[256,3072]{1,0:T(8,128)S(1)}, bf16[1536,3072]{1,0:T(8,128)(2,1)S(1)}) custom-call(s32[3]{0:T(128)S(1)} %pad_add_fusion.info_ref, bf16[256,1536]{1,0:T(8,128)(2,1)S(1)} %get-tuple-element.91.mixed_ref, bf16[1536,3072]{1,0:T(8,128)(2,1)S(1)} %get-tuple-element.92.weight_ref, bf16[3072,3072]{1,0:T(8,128)(2,1)} %later_ref.3), custom_call_target="tpu_custom_call" | custom-call | flops 2415919104 | bytes 9437184 | tf_op jit(solution)/shard_map/pallas_call | solution.py:264
  52.1 1.6 %shard_map.80 = (f32[32,1536]{1,0:T(8,128)S(1)}, f32[32,1536]{1,0:T(8,128)S(1)}, f32[32,1536]{1,0:T(8,128)S(1)}, f32[32,1536]{1,0:T(8,128)S(1)}, bf16[32,1536]{1...) custom-call(bf16[256,1536]{1,0:T(8,128)(2,1)S(1)} %collective-permute, ...), custom_call_target="tpu_custom_call" | custom-call | flops 1207959552 | bytes 4718592 | tf_op jit(solution)/shard_map/pallas_call | solution.py:297
  54.3 1.6 %shard_map.81 = (f32[32,1536]{1,0:T(8,128)S(1)}, f32[32,1536]{1,0:T(8,128)S(1)}, f32[32,1536]{1,0:T(8,128)S(1)}, f32[32,1536]{1,0:T(8,128)S(1)}, bf16[32,1536]{1...) custom-call(bf16[256,1536]{1,0:T(8,128)(2,1)S(1)} %collective-permute, ...), custom_call_target="tpu_custom_call" | custom-call | flops 1207959552 | bytes 4718592 | tf_op jit(solution)/shard_map/pallas_call | solution.py:297
  56.0 3.5 %collective-permute-start.24 = (bf16[32,1536]{1,0:T(8,128)(2,1)S(1)}, bf16[32,1536]{1,0:T(8,128)(2,1)S(1)}, u32[]{:S(2)}, u32[]{:S(2)}) collective-permute-start(bf16[32,1536]{1,0:T(8,128)(2,1)S(1)} %convert_element_type.76), channel_id=1, source_target_pairs={{2,0},{3,1},{4,2},{5,3},{6,4},{7,5},{0,6},{1,7},{10,8},{11,9},{12,... | collective-permute-start | bytes 294920 | tf_op jit(solution)/shard_map/ppermute | solution.py:347
  62.6 2.2 %collective-permute-done.25 = bf16[32,1536]{1,0:T(8,128)(2,1)S(1)} collective-permute-done((bf16[32,1536]{1,0:T(8,128)(2,1)S(1)}, bf16[32,1536]{1,0:T(8,128)(2,1)S(1)}, u32[]{:S(2)}, u32[]{:S(2)}) %collective-permute-start.25) | collective-permute-done | bytes 98336 | tf_op jit(solution)/shard_map/ppermute | solution.py:350
  64.8 2.2 %collective-permute-start.26 = (bf16[32,1536]{1,0:T(8,128)(2,1)S(1)}, bf16[32,1536]{1,0:T(8,128)(2,1)S(1)}, u32[]{:S(2)}, u32[]{:S(2)}) collective-permute-start(bf16[32,1536]{1,0:T(8,128)(2,1)S(1)} %add_convert_fusion.2), channel_id=1, source_target_pairs={{2,0},{3,1},{4,2},{5,3},{6,4},{7,5},{0,6},{1,7},{10,8},{11,9},{12,... | collective-permute-start | bytes 294920 | tf_op jit(solution)/shard_map/ppermute | solution.py:347
  69.5 2.2 %collective-permute-done.27 = bf16[32,1536]{1,0:T(8,128)(2,1)S(1)} collective-permute-done((bf16[32,1536]{1,0:T(8,128)(2,1)S(1)}, bf16[32,1536]{1,0:T(8,128)(2,1)S(1)}, u32[]{:S(2)}, u32[]{:S(2)}) %collective-permute-start.27) | collective-permute-done | bytes 98336 | tf_op jit(solution)/shard_map/ppermute | solution.py:350
  71.7 3.4 %collective-permute-done.28 = bf16[32,1536]{1,0:T(8,128)(2,1)S(1)} collective-permute-done((bf16[32,1536]{1,0:T(8,128)(2,1)S(1)}, bf16[32,1536]{1,0:T(8,128)(2,1)S(1)}, u32[]{:S(2)}, u32[]{:S(2)}) %collective-permute-start.28) | collective-permute-done | bytes 98336 | tf_op jit(solution)/shard_map/ppermute | solution.py:344
  76.3 2.1 %collective-permute-start.23 = (bf16[32,1536]{1,0:T(8,128)(2,1)S(1)}, bf16[32,1536]{1,0:T(8,128)(2,1)S(1)}, u32[]{:S(2)}, u32[]{:S(2)}) collective-permute-start(bf16[32,1536]{1,0:T(8,128)(2,1)S(1)} %add_convert_fusion.3), channel_id=1, source_target_pairs={{0,2},{1,3},{2,4},{3,5},{4,6},{5,7},{6,0},{7,1},{8,10},{9,11},{10,... | collective-permute-start | bytes 294920 | tf_op jit(solution)/shard_map/ppermute | solution.py:344
  80.8 1.9 %collective-permute-done.23 = bf16[32,1536]{1,0:T(8,128)(2,1)S(1)} collective-permute-done((bf16[32,1536]{1,0:T(8,128)(2,1)S(1)}, bf16[32,1536]{1,0:T(8,128)(2,1)S(1)}, u32[]{:S(2)}, u32[]{:S(2)}) %collective-permute-start.23) | collective-permute-done | bytes 98336 | tf_op jit(solution)/shard_map/ppermute | solution.py:344
  (71 shorter events, 21.9 us)
Async XLA Ops:
  2.5 8.1 %collective-permute-start.8 = (bf16[32,1536]{1,0:T(8,128)(2,1)S(1)}, bf16[32,1536]{1,0:T(8,128)(2,1)S(1)}, u32[]{:S(2)}, u32[]{:S(2)}) collective-permute-start(bf16[32,1536]{1,0:T(8,128)(2,1)S(1)} %get-tuple-element.81.refs_0_), channel_id=1, source_target_pairs={{0,2},{1,3},{2,4},{3,5},{4,6},{5,7},{6,0},{7,1},{8,10},{9,11},{10,... | collective-permute-start | bytes 294920 | tf_op jit(solution)/shard_map/ppermute | solution.py:344
  5.4 5.1 %collective-permute-start.9 = (bf16[32,1536]{1,0:T(8,128)(2,1)S(1)}, bf16[32,1536]{1,0:T(8,128)(2,1)S(1)}, u32[]{:S(2)}, u32[]{:S(2)}) collective-permute-start(bf16[32,1536]{1,0:T(8,128)(2,1)S(1)} %get-tuple-element.81.refs_0_), channel_id=1, source_target_pairs={{0,1},{1,0},{2,3},{3,2},{4,5},{5,4},{6,7},{7,6},{8,9},{9,8},{10,11... | collective-permute-start | bytes 294920 | tf_op jit(solution)/shard_map/ppermute | solution.py:350
  7.0 11.3 %collective-permute-start.1 = (bf16[32,1536]{1,0:T(8,128)(2,1)S(1)}, bf16[32,1536]{1,0:T(8,128)(2,1)S(1)}, u32[]{:S(2)}, u32[]{:S(2)}) collective-permute-start(bf16[32,1536]{1,0:T(8,128)(2,1)S(1)} %get-tuple-element.72.refs_0_), channel_id=1, source_target_pairs={{0,2},{1,3},{2,4},{3,5},{4,6},{5,7},{6,0},{7,1},{8,10},{9,11},{10,... | collective-permute-start | bytes 294920 | tf_op jit(solution)/shard_map/ppermute | solution.py:344
  8.5 9.7 %collective-permute-start.2 = (bf16[32,1536]{1,0:T(8,128)(2,1)S(1)}, bf16[32,1536]{1,0:T(8,128)(2,1)S(1)}, u32[]{:S(2)}, u32[]{:S(2)}) collective-permute-start(bf16[32,1536]{1,0:T(8,128)(2,1)S(1)} %get-tuple-element.72.refs_0_), channel_id=1, source_target_pairs={{0,1},{1,0},{2,3},{3,2},{4,5},{5,4},{6,7},{7,6},{8,9},{9,8},{10,11... | collective-permute-start | bytes 294920 | tf_op jit(solution)/shard_map/ppermute | solution.py:350
  10.6 11.5 %collective-permute-start.10 = (bf16[32,1536]{1,0:T(8,128)(2,1)S(1)}, bf16[32,1536]{1,0:T(8,128)(2,1)S(1)}, u32[]{:S(2)}, u32[]{:S(2)}) collective-permute-start(bf16[32,1536]{1,0:T(8,128)(2,1)S(1)} %collective-permute-done.8.refs_1_), channel_id=1, source_target_pairs={{0,2},{1,3},{2,4},{3,5},{4,6},{5,7},{6,0},{7,1},{8,10},{9,11},{10,... | collective-permute-start | bytes 294920 | tf_op jit(solution)/shard_map/ppermute | solution.py:344
  11.6 10.5 %collective-permute-start.11 = (bf16[32,1536]{1,0:T(8,128)(2,1)S(1)}, bf16[32,1536]{1,0:T(8,128)(2,1)S(1)}, u32[]{:S(2)}, u32[]{:S(2)}) collective-permute-start(bf16[32,1536]{1,0:T(8,128)(2,1)S(1)} %collective-permute-done.8.refs_1_), channel_id=1, source_target_pairs={{0,1},{1,0},{2,3},{3,2},{4,5},{5,4},{6,7},{7,6},{8,9},{9,8},{10,11... | collective-permute-start | bytes 294920 | tf_op jit(solution)/shard_map/ppermute | solution.py:350
  18.2 10.3 %collective-permute-start.3 = (bf16[32,1536]{1,0:T(8,128)(2,1)S(1)}, bf16[32,1536]{1,0:T(8,128)(2,1)S(1)}, u32[]{:S(2)}, u32[]{:S(2)}) collective-permute-start(bf16[32,1536]{1,0:T(8,128)(2,1)S(1)} %collective-permute-done.1.refs_1_), channel_id=1, source_target_pairs={{0,2},{1,3},{2,4},{3,5},{4,6},{5,7},{6,0},{7,1},{8,10},{9,11},{10,... | collective-permute-start | bytes 294920 | tf_op jit(solution)/shard_map/ppermute | solution.py:344
  20.2 8.4 %collective-permute-start.4 = (bf16[32,1536]{1,0:T(8,128)(2,1)S(1)}, bf16[32,1536]{1,0:T(8,128)(2,1)S(1)}, u32[]{:S(2)}, u32[]{:S(2)}) collective-permute-start(bf16[32,1536]{1,0:T(8,128)(2,1)S(1)} %collective-permute-done.1.refs_1_), channel_id=1, source_target_pairs={{0,1},{1,0},{2,3},{3,2},{4,5},{5,4},{6,7},{7,6},{8,9},{9,8},{10,11... | collective-permute-start | bytes 294920 | tf_op jit(solution)/shard_map/ppermute | solution.py:350
  20.5 8.1 %collective-permute-start.5 = (bf16[32,1536]{1,0:T(8,128)(2,1)S(1)}, bf16[32,1536]{1,0:T(8,128)(2,1)S(1)}, u32[]{:S(2)}, u32[]{:S(2)}) collective-permute-start(bf16[32,1536]{1,0:T(8,128)(2,1)S(1)} %collective-permute-done.2.refs_4_), channel_id=1, source_target_pairs={{2,0},{3,1},{4,2},{5,3},{6,4},{7,5},{0,6},{1,7},{10,8},{11,9},{12,... | collective-permute-start | bytes 294920 | tf_op jit(solution)/shard_map/ppermute | solution.py:347
  22.1 7.1 %collective-permute-start.12 = (bf16[32,1536]{1,0:T(8,128)(2,1)S(1)}, bf16[32,1536]{1,0:T(8,128)(2,1)S(1)}, u32[]{:S(2)}, u32[]{:S(2)}) collective-permute-start(bf16[32,1536]{1,0:T(8,128)(2,1)S(1)} %collective-permute-done.10.refs_2_), channel_id=1, source_target_pairs={{0,2},{1,3},{2,4},{3,5},{4,6},{5,7},{6,0},{7,1},{8,10},{9,11},{10,... | collective-permute-start | bytes 294920 | tf_op jit(solution)/shard_map/ppermute | solution.py:344
  22.5 6.7 %collective-permute-start.13 = (bf16[32,1536]{1,0:T(8,128)(2,1)S(1)}, bf16[32,1536]{1,0:T(8,128)(2,1)S(1)}, u32[]{:S(2)}, u32[]{:S(2)}) collective-permute-start(bf16[32,1536]{1,0:T(8,128)(2,1)S(1)} %collective-permute-done.10.refs_2_), channel_id=1, source_target_pairs={{0,1},{1,0},{2,3},{3,2},{4,5},{5,4},{6,7},{7,6},{8,9},{9,8},{10,11... | collective-permute-start | bytes 294920 | tf_op jit(solution)/shard_map/ppermute | solution.py:350
  28.6 6.5 %collective-permute-start.6 = (bf16[32,1536]{1,0:T(8,128)(2,1)S(1)}, bf16[32,1536]{1,0:T(8,128)(2,1)S(1)}, u32[]{:S(2)}, u32[]{:S(2)}) collective-permute-start(bf16[32,1536]{1,0:T(8,128)(2,1)S(1)} %collective-permute-done.3.refs_2_), channel_id=1, source_target_pairs={{0,2},{1,3},{2,4},{3,5},{4,6},{5,7},{6,0},{7,1},{8,10},{9,11},{10,... | collective-permute-start | bytes 294920 | tf_op jit(solution)/shard_map/ppermute | solution.py:344
  28.7 6.3 %collective-permute-start.7 = (bf16[32,1536]{1,0:T(8,128)(2,1)S(1)}, bf16[32,1536]{1,0:T(8,128)(2,1)S(1)}, u32[]{:S(2)}, u32[]{:S(2)}) collective-permute-start(bf16[32,1536]{1,0:T(8,128)(2,1)S(1)} %collective-permute-done.3.refs_2_), channel_id=1, source_target_pairs={{0,1},{1,0},{2,3},{3,2},{4,5},{5,4},{6,7},{7,6},{8,9},{9,8},{10,11... | collective-permute-start | bytes 294920 | tf_op jit(solution)/shard_map/ppermute | solution.py:350
  29.2 5.9 %collective-permute-start.14 = (bf16[32,1536]{1,0:T(8,128)(2,1)S(1)}, bf16[32,1536]{1,0:T(8,128)(2,1)S(1)}, u32[]{:S(2)}, u32[]{:S(2)}) collective-permute-start(bf16[32,1536]{1,0:T(8,128)(2,1)S(1)} %collective-permute-done.12.refs_3_), channel_id=1, source_target_pairs={{0,1},{1,0},{2,3},{3,2},{4,5},{5,4},{6,7},{7,6},{8,9},{9,8},{10,11... | collective-permute-start | bytes 294920 | tf_op jit(solution)/shard_map/ppermute | solution.py:350
  47.2 4.9 %collective-permute-start.16 = (bf16[256,1536]{1,0:T(8,128)(2,1)S(1)}, bf16[256,1536]{1,0:T(8,128)(2,1)S(1)}, u32[]{:S(2)}, u32[]{:S(2)}) collective-permute-start(bf16[256,1536]{1,0:T(8,128)(2,1)S(1)} %get-tuple-element.91.mixed_ref), channel_id=1, source_target_pairs={{0,8},{8,0},{1,9},{9,1},{2,10},{10,2},{3,11},{11,3},{4,12},{12,4},... | collective-permute-start | bytes 2359304 | tf_op jit(solution)/shard_map/ppermute | solution.py:475
  53.7 6.9 %collective-permute-start.17 = (bf16[32,1536]{1,0:T(8,128)(2,1)S(1)}, bf16[32,1536]{1,0:T(8,128)(2,1)S(1)}, u32[]{:S(2)}, u32[]{:S(2)}) collective-permute-start(bf16[32,1536]{1,0:T(8,128)(2,1)S(1)} %get-tuple-element.96), channel_id=1, source_target_pairs={{0,1},{1,0},{2,3},{3,2},{4,5},{5,4},{6,7},{7,6},{8,9},{9,8},{10,11... | collective-permute-start | bytes 294920 | tf_op jit(solution)/shard_map/ppermute | solution.py:350
  56.0 6.6 %collective-permute-start.24 = (bf16[32,1536]{1,0:T(8,128)(2,1)S(1)}, bf16[32,1536]{1,0:T(8,128)(2,1)S(1)}, u32[]{:S(2)}, u32[]{:S(2)}) collective-permute-start(bf16[32,1536]{1,0:T(8,128)(2,1)S(1)} %convert_element_type.76), channel_id=1, source_target_pairs={{2,0},{3,1},{4,2},{5,3},{6,4},{7,5},{0,6},{1,7},{10,8},{11,9},{12,... | collective-permute-start | bytes 294920 | tf_op jit(solution)/shard_map/ppermute | solution.py:347
  59.5 5.3 %collective-permute-start.25 = (bf16[32,1536]{1,0:T(8,128)(2,1)S(1)}, bf16[32,1536]{1,0:T(8,128)(2,1)S(1)}, u32[]{:S(2)}, u32[]{:S(2)}) collective-permute-start(bf16[32,1536]{1,0:T(8,128)(2,1)S(1)} %get-tuple-element.120), channel_id=1, source_target_pairs={{0,1},{1,0},{2,3},{3,2},{4,5},{5,4},{6,7},{7,6},{8,9},{9,8},{10,11... | collective-permute-start | bytes 294920 | tf_op jit(solution)/shard_map/ppermute | solution.py:350
  60.6 7.5 %collective-permute-start.19 = (bf16[32,1536]{1,0:T(8,128)(2,1)S(1)}, bf16[32,1536]{1,0:T(8,128)(2,1)S(1)}, u32[]{:S(2)}, u32[]{:S(2)}) collective-permute-start(bf16[32,1536]{1,0:T(8,128)(2,1)S(1)} %add_convert_fusion.5), channel_id=1, source_target_pairs={{0,2},{1,3},{2,4},{3,5},{4,6},{5,7},{6,0},{7,1},{8,10},{9,11},{10,... | collective-permute-start | bytes 294920 | tf_op jit(solution)/shard_map/ppermute | solution.py:344
  60.7 7.5 %collective-permute-start.18 = (bf16[32,1536]{1,0:T(8,128)(2,1)S(1)}, bf16[32,1536]{1,0:T(8,128)(2,1)S(1)}, u32[]{:S(2)}, u32[]{:S(2)}) collective-permute-start(bf16[32,1536]{1,0:T(8,128)(2,1)S(1)} %get-tuple-element.100), channel_id=1, source_target_pairs={{0,1},{1,0},{2,3},{3,2},{4,5},{5,4},{6,7},{7,6},{8,9},{9,8},{10,11... | collective-permute-start | bytes 294920 | tf_op jit(solution)/shard_map/ppermute | solution.py:350
  68.1 6.9 %collective-permute-start.28 = (bf16[32,1536]{1,0:T(8,128)(2,1)S(1)}, bf16[32,1536]{1,0:T(8,128)(2,1)S(1)}, u32[]{:S(2)}, u32[]{:S(2)}) collective-permute-start(bf16[32,1536]{1,0:T(8,128)(2,1)S(1)} %get-tuple-element.127), channel_id=1, source_target_pairs={{0,2},{1,3},{2,4},{3,5},{4,6},{5,7},{6,0},{7,1},{8,10},{9,11},{10,... | collective-permute-start | bytes 294920 | tf_op jit(solution)/shard_map/ppermute | solution.py:344
  68.2 8.0 %collective-permute-start.21 = (bf16[32,1536]{1,0:T(8,128)(2,1)S(1)}, bf16[32,1536]{1,0:T(8,128)(2,1)S(1)}, u32[]{:S(2)}, u32[]{:S(2)}) collective-permute-start(bf16[32,1536]{1,0:T(8,128)(2,1)S(1)} %add_convert_fusion.4), channel_id=1, source_target_pairs={{0,2},{1,3},{2,4},{3,5},{4,6},{5,7},{6,0},{7,1},{8,10},{9,11},{10,... | collective-permute-start | bytes 294920 | tf_op jit(solution)/shard_map/ppermute | solution.py:344
  68.2 8.0 %collective-permute-start.20 = (bf16[32,1536]{1,0:T(8,128)(2,1)S(1)}, bf16[32,1536]{1,0:T(8,128)(2,1)S(1)}, u32[]{:S(2)}, u32[]{:S(2)}) collective-permute-start(bf16[32,1536]{1,0:T(8,128)(2,1)S(1)} %get-tuple-element.105), channel_id=1, source_target_pairs={{0,1},{1,0},{2,3},{3,2},{4,5},{5,4},{6,7},{7,6},{8,9},{9,8},{10,11... | collective-permute-start | bytes 294920 | tf_op jit(solution)/shard_map/ppermute | solution.py:350
  76.3 6.5 %collective-permute-start.23 = (bf16[32,1536]{1,0:T(8,128)(2,1)S(1)}, bf16[32,1536]{1,0:T(8,128)(2,1)S(1)}, u32[]{:S(2)}, u32[]{:S(2)}) collective-permute-start(bf16[32,1536]{1,0:T(8,128)(2,1)S(1)} %add_convert_fusion.3), channel_id=1, source_target_pairs={{0,2},{1,3},{2,4},{3,5},{4,6},{5,7},{6,0},{7,1},{8,10},{9,11},{10,... | collective-permute-start | bytes 294920 | tf_op jit(solution)/shard_map/ppermute | solution.py:344
  (12 other events, 64.9 us)

commit v3 on v2

--- a/solution.py
+++ b/solution.py
@@ -90,49 +90,51 @@
     lax.fori_loop(0, (total // high) * (width // tile), step_body, 0)
 
 
-def up_first(slots, weight):
+def up_near(info, slots, upper, lower):
     rows, depth = slots[0].shape
     total = rows * len(slots)
-    width = weight.shape[1]
-
-    def kernel(*refs):
-        weight_ref, out_ref, tokens_ref = refs[len(slots) :]
+    split = upper.shape[0]
+    width = upper.shape[1] // 2
+
+    def kernel(info_ref, *refs):
+        upper_ref, lower_ref, other_ref, own_ref, tokens_ref = refs[len(slots) :]
         gathered_rows(refs[: len(slots)], tokens_ref)
-
-        def body(down, col, tile):
-            out_ref[down, pl.ds(col, tile)] = jnp.dot(
-                tokens_ref[down, :], weight_ref[:, pl.ds(col, tile)], preferred_element_type=F32
-            )
-
-        tiles(total, width, 1024, body)
-
-    return pl.pallas_call(
-        kernel,
-        out_shape=pltpu.VMEM((total, width), F32),
-        in_specs=[VMEM] * (len(slots) + 1),
-        out_specs=VMEM,
+        for side, out_ref in ((1 - info_ref[0], other_ref), (info_ref[0], own_ref)):
+            product_tiles(tokens_ref, upper_ref, lower_ref, side * width, out_ref)
+
+    return pl.pallas_call(
+        kernel,
+        out_shape=(pltpu.VMEM((total, width), BF16), pltpu.VMEM((total, width), F32)),
+        in_specs=[SMEM] + [VMEM] * (len(slots) + 2),
+        out_specs=(VMEM, VMEM),
         scratch_shapes=[pltpu.VMEM((total, depth), BF16)],
-        cost_estimate=cost(2 * total * depth * width, 2 * depth * width),
-        compiler_params=params(12),
-    )(*slots, weight)
-
-
-def up_other(info, slots, weight, partial):
+        cost_estimate=cost(4 * total * depth * width, 2 * depth * width),
+        compiler_params=params(10),
+    )(info, *slots, upper, lower)
+
+
+def product_tiles(tokens_ref, upper_ref, lower_ref, base, out_ref):
+    split = upper_ref.shape[0]
+
+    def body(down, col, tile):
+        across = pl.ds(pl.multiple_of(base + col, 128), tile)
+        product = jnp.dot(tokens_ref[down, :split], upper_ref[:, across], preferred_element_type=F32) + jnp.dot(
+            tokens_ref[down, split:], lower_ref[:, across], preferred_element_type=F32
+        )
+        out_ref[down, pl.ds(col, tile)] = product.astype(out_ref.dtype)
+
+    tiles(*out_ref.shape, 768, body)
+
+
+def up_other(info, slots, upper, lower):
     rows, depth = slots[0].shape
     total = rows * len(slots)
-    width = weight.shape[1] // 2
+    width = upper.shape[1] // 2
 
     def kernel(info_ref, *refs):
-        weight_ref, partial_ref, out_ref, tokens_ref = refs[len(slots) :]
+        upper_ref, lower_ref, out_ref, tokens_ref = refs[len(slots) :]
         gathered_rows(refs[: len(slots)], tokens_ref)
-        base = (1 - info_ref[0]) * width
-
-        def body(down, col, tile):
-            across = pl.ds(pl.multiple_of(base + col, 128), tile)
-            product = jnp.dot(tokens_ref[down, :], weight_ref[:, across], preferred_element_type=F32)
-            out_ref[down, pl.ds(col, tile)] = (partial_ref[down, across] + product).astype(BF16)
-
-        tiles(total, width, 768, body)
+        product_tiles(tokens_ref, upper_ref, lower_ref, (1 - info_ref[0]) * width, out_ref)
 
     return pl.pallas_call(
         kernel,
@@ -140,23 +142,16 @@
         in_specs=[SMEM] + [VMEM] * (len(slots) + 2),
         out_specs=(VMEM, VMEM),
         cost_estimate=cost(2 * total * depth * width, 2 * depth * width),
-        compiler_params=params(12),
-    )(info, *slots, weight, partial)
-
-
-def up_own(info, tokens, weight, partial):
+        compiler_params=params(10),
+    )(info, *slots, upper, lower)
+
+
+def up_own(info, tokens, upper, lower):
     total, depth = tokens.shape
-    width = weight.shape[1] // 2
-
-    def kernel(info_ref, tokens_ref, weight_ref, partial_ref, out_ref):
-        base = info_ref[0] * width
-
-        def body(down, col, tile):
-            across = pl.ds(pl.multiple_of(base + col, 128), tile)
-            product = jnp.dot(tokens_ref[down, :], weight_ref[:, across], preferred_element_type=F32)
-            out_ref[down, pl.ds(col, tile)] = partial_ref[down, across] + product
-
-        tiles(total, width, 768, body)
+    width = upper.shape[1] // 2
+
+    def kernel(info_ref, tokens_ref, upper_ref, lower_ref, out_ref):
+        product_tiles(tokens_ref, upper_ref, lower_ref, info_ref[0] * width, out_ref)
 
     return pl.pallas_call(
         kernel,
@@ -164,8 +159,8 @@
         in_specs=[SMEM] + [VMEM] * 3,
         out_specs=VMEM,
         cost_estimate=cost(2 * total * depth * width, 2 * depth * width),
-        compiler_params=params(12),
-    )(info, tokens, weight, partial)
+        compiler_params=params(10),
+    )(info, tokens, upper, lower)
 
 
 def gelu(value):
@@ -181,13 +176,16 @@
 
 
 def conv(info, own, received, up_bias, conv_weight, conv_bias, later, ring_size, lanes_of, grid_y):
-    total, width = own.shape
+    width = own[0].shape[1]
+    rows = own[0].shape[0] // ring_size
     blocks = ring_size * lanes_of
-    rows = total // blocks
+    total = rows * blocks
     lanes = 128
     extent_x = total // grid_y
 
-    def kernel(info_ref, own_ref, received_ref, up_bias_ref, weight_ref, bias_ref, later_ref, out_ref, later_out, hidden, sems):
+    def kernel(info_ref, *refs):
+        own_refs, received_refs = refs[:lanes_of], refs[lanes_of : 2 * lanes_of]
+        up_bias_ref, weight_ref, bias_ref, later_ref, out_ref, later_out, hidden, sems = refs[2 * lanes_of :]
         copies = row_copies(later_ref, pl.multiple_of(info_ref[0] * width, 16), later_out, sems)
         for copy in copies:
             copy.start()
@@ -207,8 +205,9 @@
             absolute = pl.ds(pl.multiple_of(base + col * lanes, lanes), lanes)
             shift = up_bias_ref[:, absolute]
             for slot in range(blocks):
-                down = slice(slot * rows, (slot + 1) * rows)
-                value = own_ref[down, across] + received_ref[down, across].astype(F32) + shift
+                q, j = slot // ring_size, slot % ring_size
+                down = slice(j * rows, (j + 1) * rows)
+                value = own_refs[q][down, across] + received_refs[q][down, across].astype(F32) + shift
                 target = pl.multiple_of(places[slot] * rows + grid_y, grid_y)
                 hidden[pl.ds(target, rows), :] = value.astype(BF16).astype(F32)
             weights = [[weight_ref[a, b : b + 1, absolute] for b in range(3)] for a in range(3)]
@@ -231,12 +230,12 @@
     return pl.pallas_call(
         kernel,
         out_shape=(pltpu.VMEM((total, width), BF16), pltpu.VMEM((width, later.shape[1]), BF16)),
-        in_specs=[SMEM] + [VMEM] * 5 + [HBM],
+        in_specs=[SMEM] + [VMEM] * (2 * lanes_of + 3) + [HBM],
         out_specs=(VMEM, VMEM),
         scratch_shapes=[pltpu.VMEM(((extent_x + 2) * grid_y, lanes), F32), pltpu.SemaphoreType.DMA((4,))],
         cost_estimate=cost(60 * total * width, 8 * total * width),
         compiler_params=params(33),
-    )(info, own, received, up_bias, conv_weight, conv_bias, later)
+    )(info, *own, *received, up_bias, conv_weight, conv_bias, later)
 
 
 def down_own(info, mixed, weight, later):
@@ -272,35 +271,34 @@
     )(info, mixed, weight, later)
 
 
-def down_other(mixed, weight, partial, blocks, kept, start, width):
-    total, depth = mixed.shape
-    rows = total // blocks
-    tile = tile_of(width, 768)
+def down_other(mixed, weight, partial, rows, first, blocks, kind):
+    depth = mixed.shape[1]
+    width = weight.shape[1]
+    total = rows * blocks
+    tile = tile_of(width, 1024)
+    high = rows * max(n for n in range(1, blocks + 1) if blocks % n == 0 and rows * n <= max(256, rows))
 
     def kernel(mixed_ref, weight_ref, partial_ref, *out_refs):
         def body(step, carry):
-            col = pl.multiple_of(step * tile, tile)
-            across = pl.ds(pl.multiple_of(start + col, 128), tile)
-            here = pl.ds(col, tile)
-            for first in range(0, total, 256):
-                high = min(256, total - first)
-                value = partial_ref[first : first + high, across] + jnp.dot(
-                    mixed_ref[first : first + high, :], weight_ref[:, across], preferred_element_type=F32
+            across = pl.ds(pl.multiple_of(step * tile, tile), tile)
+            for start in range(0, total, high):
+                down = slice(first + start, first + start + high)
+                value = partial_ref[down, across] + jnp.dot(
+                    mixed_ref[down, :], weight_ref[:, across], preferred_element_type=F32
                 )
                 for low in range(0, high, rows):
-                    out_ref = out_refs[(first + low) // rows]
-                    out_ref[:, here] = value[low : low + rows].astype(out_ref.dtype)
+                    out_refs[(start + low) // rows][:, across] = value[low : low + rows].astype(kind)
             return carry
 
         lax.fori_loop(0, width // tile, body, 0)
 
     return pl.pallas_call(
         kernel,
-        out_shape=tuple(pltpu.VMEM((rows, width), F32 if block < kept else BF16) for block in range(blocks)),
+        out_shape=(pltpu.VMEM((rows, width), kind),) * blocks,
         in_specs=[VMEM] * 3,
         out_specs=(VMEM,) * blocks,
         cost_estimate=cost(2 * total * depth * width, 2 * depth * width),
-        compiler_params=params(12),
+        compiler_params=params(10),
     )(mixed, weight, partial)
 
 
@@ -350,75 +348,76 @@
         return lax.ppermute(value, "tp", self.pairs)
 
 
-def gather_steps(links, block, tree, extras):
+def gather(links, block, fetches):
     ring = links.ring
-    tree = tree and links.lanes > 1 and ring > 2
+    half_way = ring // 2
     column, beside = {0: block}, {}
-    for step in range(1, ring + 1):
-        moves = []
-        if step < ring:
-            moves.append((column, step, links.up(column[step - 1])))
-        if links.lanes > 1 and not (tree and step == ring):
-            moves.append((beside, step - 1, links.cross(column[step - 1])))
-        if tree and step == 2:
-            moves.append((beside, ring - 1, links.down(beside[0])))
-        made = extras.get(step)
-        yield
-        values = [value for _, _, value in moves]
-        if made is not None:
-            values.append(made())
-        if not values:
-            continue
-        done = tie(*values)
-        for (where, slot, _), value in zip(moves, done):
-            where[slot] = value
-        if made is not None:
-            extras[step] = done[-1]
-    yield [column[j] for j in range(ring)] + [beside[j] for j in range(ring) if links.lanes > 1]
-
-
-def scatter_steps(links, kept, sent, tree):
+    first, second = fetches
+
+    def hand(slot):
+        if links.lanes > 1:
+            beside[slot] = links.cross(column[slot])
+
+    if ring > 1:
+        column[1] = links.up(block)
+    hand(0)
+    upper = first()
+    if ring > 2:
+        if links.lanes > 1:
+            late, upper, beside[0] = tie(block, upper, beside[0])
+        else:
+            late, upper = tie(block, upper)
+        column[ring - 1] = links.down(late)
+    if ring > 1:
+        hand(1)
+    if half_way > 1:
+        column[2] = links.up(column[1])
+    lower = second(column[1] if ring > 1 else block)
+    for distance in range(1, half_way + 1):
+        if distance > 2:
+            column[distance] = links.up(column[distance - 1])
+        if distance > 1:
+            hand(distance)
+        if 1 < distance < ring - half_way:
+            column[ring - distance] = links.down(column[ring - distance + 1])
+        if distance < ring - half_way:
+            hand(ring - distance)
+    return [column[j] for j in range(ring)], [beside[j] for j in range(ring) if links.lanes > 1], upper, lower
+
+
+def scatter(links, far, make_near):
     ring = links.ring
-    sent = list(sent)
-    if tree and links.lanes > 1 and ring > 2:
-        total = kept[ring - 1]
-        for slot in range(ring - 2, -1, -1):
-            moves = [links.down(total.astype(BF16)), links.cross(sent[slot])]
-            if slot == 1:
-                moves.append(links.up(sent[ring - 1]))
-            yield
-            count = len(moves)
-            arrived = tie(*moves, *sent)
-            moves, sent = arrived[:count], list(arrived[count:])
-            total = kept[slot] + moves[0].astype(F32) + moves[1].astype(F32)
-            if slot == 1:
-                sent[0] = (sent[0].astype(F32) + moves[2].astype(F32)).astype(BF16)
-    else:
-        total = None
-        for slot in list(range(1, ring)) + [0]:
-            moves = [links.cross(sent[slot])] if links.lanes > 1 else []
-            if total is not None:
-                moves.append(links.up(total.astype(BF16)))
-            yield
-            count = len(moves)
-            arrived = tie(*moves, *sent) if moves else tuple(sent)
-            moves, sent = arrived[:count], list(arrived[count:])
-            total = kept[slot]
-            for value in moves:
-                total = total + value.astype(F32)
-    yield total
-
-
-def interleave(streams):
-    results = [None] * len(streams)
-    live = list(range(len(streams)))
-    while live:
-        for index in list(live):
-            try:
-                results[index] = next(streams[index])
-            except StopIteration:
-                live.remove(index)
-    return results
+    half_way = ring // 2
+    upper_chain = list(range(half_way, 0, -1))
+    lower_chain = list(range(half_way + 1, ring))
+    order = [slot for pair in zip(upper_chain, lower_chain) for slot in pair]
+    order += [slot for slot in upper_chain + lower_chain if slot not in order] + [0]
+    far = list(far)
+    crossed, arrived, ready = {}, {slot: [] for slot in range(ring)}, {}
+    if links.lanes > 1:
+        crossed[order[0]] = links.cross(far[order[0]])
+    near = make_near()
+    for position, slot in enumerate(order):
+        if links.lanes > 1 and position + 1 < ring:
+            after = order[position + 1]
+            token = near[0] if position == 0 else ready[order[position - 1]]
+            far[after], token = tie(far[after], token)
+            if position == 0:
+                near[0] = token
+            else:
+                ready[order[position - 1]] = token
+            crossed[after] = links.cross(far[after])
+        terms = arrived[slot] + ([crossed[slot]] if links.lanes > 1 else [])
+        total = near[slot]
+        for term in terms:
+            total = total + term.astype(F32)
+        if slot == 0:
+            return total
+        ready[slot] = total.astype(BF16)
+        if slot <= half_way:
+            arrived[slot - 1].append(links.down(ready[slot]))
+        else:
+            arrived[(slot + 1) % ring].append(links.up(ready[slot]))
 
 
 def local(tokens, up_weight, up_bias, conv_weight, conv_bias, down_weight, down_bias):
@@ -443,27 +442,28 @@
     keep, take = (x.reshape(cols, 1, grid_half, half) for x in (keep, take))
     block = jnp.where(core == 0, jnp.concatenate([keep, take], 1), jnp.concatenate([take, keep], 1))
     block = block.reshape(rows, half)
-    block_a, block_b, info = tie(block[:, :part], block[:, part:], info)
+    block, info = tie(block, info)
 
     part_bytes = part * units * 2
-    extras_a = {}
-    extras_b = {
-        1: lambda: fetch(info, up_weight, lambda c: 0 * c, part, 0),
-        2: lambda: fetch(info, up_weight, lambda c: 0 * c + part, part, part_bytes),
-    }
-    slots_a, slots_b = interleave(
-        [gather_steps(links, block_a, False, extras_a), gather_steps(links, block_b, True, extras_b)]
+
+    def fetch_lower(token):
+        late, _ = tie(info, token)
+        return fetch(late, up_weight, lambda c: 0 * c + part, part, part_bytes)
+
+    near, far, upper, lower = gather(
+        links, block, (lambda: fetch(info, up_weight, lambda c: 0 * c, part, 0), fetch_lower)
     )
-    upper, lower = (made if not callable(made) else made() for made in (extras_b[1], extras_b[2]))
-
-    first = up_first(slots_a, upper)
-    partial_other, tokens_b = up_other(info, slots_b, lower, first)
-    partial_received = lax.ppermute(partial_other, "sp", swap)
-    partial_own = up_own(info, tokens_b, lower, first)
+
+    near_other, near_own = up_near(info, near, upper, lower)
+    own, received = [near_own], [lax.ppermute(near_other, "sp", swap)]
+    if far:
+        far_other, tokens_far = up_other(info, far, upper, lower)
+        received.append(lax.ppermute(far_other, "sp", swap))
+        own.append(up_own(info, tokens_far, upper, lower))
     mixed, down_mine = conv(
         info,
-        partial_own,
-        partial_received,
+        own,
+        received,
         up_bias.reshape(1, units),
         conv_weight,
         conv_bias.reshape(1, units),
@@ -475,11 +475,13 @@
     mixed_received = lax.ppermute(mixed, "sp", swap)
     product, down_theirs = down_own(info, mixed, down_mine, down_weight)
 
-    streams = []
-    for start, tree in ((0, False), (part, True)):
-        sums = down_other(mixed_received, down_theirs, product, len(slots_a), links.ring, start, part)
-        streams.append(scatter_steps(links, sums[: links.ring], sums[links.ring :], tree))
-    totals = interleave(streams)
+    sent = []
+    if far:
+        sent = down_other(mixed_received, down_theirs, product, rows, links.ring * rows, links.ring, BF16)
+    total = scatter(
+        links, sent, lambda: list(down_other(mixed_received, down_theirs, product, rows, 0, links.ring, F32))
+    )
+    totals = [total]
 
     stay, leave = finish(info, totals, down_bias.reshape(1, width_model), cols, grid_half)
     arrive = lax.ppermute(leave, "sp", swap)

time: 85.8 us -> 75.9 us (0.88)
  starting transfers between devices: 34.4 us -> 22.3 us
  waiting for transfers between devices: 20.2 us -> 21.4 us
  Pallas kernels: 28.7 us -> 29.8 us
    ppermute x10 -> x3, starting transfers between devices: 10.2 us -> 1.64 us  [up(): return lax.ppermute(value, 'tp', self.upward)]
    ppermute x14 -> x8, waiting for transfers between devices: 4.99 us -> 13.1 us  [cross(): return lax.ppermute(value, 'tp', self.pairs)]
    ppermute x10 -> x3, waiting for transfers between devices: 10.8 us -> 3.96 us  [up(): return lax.ppermute(value, 'tp', self.upward)]
    ppermute x14 -> x8, starting transfers between devices: 15.5 us -> 10.4 us  [cross(): return lax.ppermute(value, 'tp', self.pairs)]
    ppermute x4 -> x3, starting transfers between devices: 7.44 us -> 8.98 us  [down(): return lax.ppermute(value, 'tp', self.downward)]
    pallas_call x3, Pallas kernels: 6.33 us -> 7.41 us  [the longest x1 3.84 us: up_near(): pl.pallas_call(kernel, out_shape=(pltpu.VMEM((total, width), BF16), pltpu...]
    ppermute x4 -> x3, waiting for transfers between devices: 2.16 us -> 2.19 us  [down(): return lax.ppermute(value, 'tp', self.downward)]
  transfers between devices with their start and end apart: 32 -> 19, of which waited for: 14 -> 9; matrix products, arithmetic and copies ran while one was open for 0% -> 0% of each run, Pallas kernels for 20% -> 30%
where the time goes in v3:
time: 75.9 us; the launch traced here: 75.8 us
  Pallas kernels  29.8 us (39%)
  starting transfers between devices  22.3 us (29%)
  waiting for transfers between devices  21.4 us (28%)
  other arithmetic  1.06 us (1%)
  local copies, waits for them, and re-layouts  0.98 us (1%)
    ppermute x8, waiting for transfers between devices, cross(): return lax.ppermute(value, 'tp', self.pairs)  13.1 us
    ppermute x8, starting transfers between devices, cross(): return lax.ppermute(value, 'tp', self.pairs)  10.4 us
    ppermute x3, starting transfers between devices, down(): return lax.ppermute(value, 'tp', self.downward)  8.98 us
    pallas_call x2, Pallas kernels, fetch(): pl.pallas_call(kernel, out_shape=pltpu.VMEM((count, weight.shape[1]), wei...  8.68 us
    pallas_call x1, Pallas kernels, conv(): pl.pallas_call(kernel, out_shape=(pltpu.VMEM((total, width), BF16), pltpu...  4.35 us
    pallas_call x1, Pallas kernels, down_own(): pl.pallas_call(kernel, out_shape=(pltpu.VMEM((total, width), F32), pltpu....  4.35 us
    ppermute x3, waiting for transfers between devices, up(): return lax.ppermute(value, 'tp', self.upward)  3.96 us
    pallas_call x1, Pallas kernels, up_near(): pl.pallas_call(kernel, out_shape=(pltpu.VMEM((total, width), BF16), pltpu...  3.84 us
  transfers between devices with their start and end apart: 19, of which 9 were waited for; matrix products, arithmetic and copies ran while one was open for 0% of the time, Pallas kernels for 30%

profile of v3, /device:TPU:0, one launch (start us, length us, event | category | flops | bytes accessed | tf_op | source)
XLA Modules:
  0.0 75.8 jit_solution(11291912532925432612)
XLA Ops:
  2.4 2.9 %collective-permute-start.3 = (bf16[32,3072]{1,0:T(8,128)(2,1)S(1)}, bf16[32,3072]{1,0:T(8,128)(2,1)S(1)}, u32[]{:S(2)}, u32[]{:S(2)}) collective-permute-start(bf16[32,3072]{1,0:T(8,128)(2,1)S(1)} %bitcast.12), channel_id=1, source_target_pairs={{0,1},{1,0},{2,3},{3,2},{4,5},{5,4},{6,7},{7,6},{8,9},{9,8},{10,11... | collective-permute-start | bytes 589832 | tf_op jit(solution)/shard_map/ppermute | solution.py:348
  5.4 1.6 %collective-permute-start.1 = (bf16[32,3072]{1,0:T(8,128)(2,1)S(1)}, bf16[32,3072]{1,0:T(8,128)(2,1)S(1)}, u32[]{:S(2)}, u32[]{:S(2)}) collective-permute-start(bf16[32,3072]{1,0:T(8,128)(2,1)S(1)} %bitcast.13), channel_id=1, source_target_pairs={{0,2},{1,3},{2,4},{3,5},{4,6},{5,7},{6,0},{7,1},{8,10},{9,11},{10,... | collective-permute-start | bytes 589832 | tf_op jit(solution)/shard_map/ppermute | solution.py:342
  7.0 4.3 %shard_map.73.refs_4_.upper_ref = bf16[1536,3072]{1,0:T(8,128)(2,1)S(1)} custom-call(s32[3]{0:T(128)S(1)} %pad_add_fusion.info_ref, bf16[3072,3072]{1,0:T(8,128)(2,1)} %weight_ref.3), custom_call_target="tpu_custom_call" | custom-call | bytes 18874368 | tf_op jit(solution)/shard_map/pallas_call | solution.py:64
  11.3 3.1 %collective-permute-start.4 = (bf16[32,3072]{1,0:T(8,128)(2,1)S(1)}, bf16[32,3072]{1,0:T(8,128)(2,1)S(1)}, u32[]{:S(2)}, u32[]{:S(2)}) collective-permute-start(bf16[32,3072]{1,0:T(8,128)(2,1)S(1)} %bitcast.14), channel_id=1, source_target_pairs={{2,0},{3,1},{4,2},{5,3},{6,4},{7,5},{0,6},{1,7},{10,8},{11,9},{12,... | collective-permute-start | bytes 589832 | tf_op jit(solution)/shard_map/ppermute | solution.py:345
  14.4 4.3 %shard_map.74.refs_5_.lower_ref = bf16[1536,3072]{1,0:T(8,128)(2,1)S(1)} custom-call(s32[3]{0:T(128)S(1)} %pad_add_fusion.info_ref, bf16[3072,3072]{1,0:T(8,128)(2,1)} %weight_ref.3), custom_call_target="tpu_custom_call" | custom-call | bytes 18874368 | tf_op jit(solution)/shard_map/pallas_call | solution.py:64
  18.8 1.6 %collective-permute-start.5 = (bf16[32,3072]{1,0:T(8,128)(2,1)S(1)}, bf16[32,3072]{1,0:T(8,128)(2,1)S(1)}, u32[]{:S(2)}, u32[]{:S(2)}) collective-permute-start(bf16[32,3072]{1,0:T(8,128)(2,1)S(1)} %collective-permute-done.1.refs_1_), channel_id=1, source_target_pairs={{0,1},{1,0},{2,3},{3,2},{4,5},{5,4},{6,7},{7,6},{8,9},{9,8},{10,11... | collective-permute-start | bytes 589832 | tf_op jit(solution)/shard_map/ppermute | solution.py:348
  21.3 2.7 %collective-permute-done.2.refs_2_ = bf16[32,3072]{1,0:T(8,128)(2,1)S(1)} collective-permute-done((bf16[32,3072]{1,0:T(8,128)(2,1)S(1)}, bf16[32,3072]{1,0:T(8,128)(2,1)S(1)}, u32[]{:S(2)}, u32[]{:S(2)}) %collective-permute-start.2) | collective-permute-done | bytes 196640 | tf_op jit(solution)/shard_map/ppermute | solution.py:342
  24.7 3.8 %shard_map.75 = (bf16[128,1536]{1,0:T(8,128)(2,1)S(1)}, f32[128,1536]{1,0:T(8,128)S(1)}) custom-call(s32[3]{0:T(128)S(1)} %pad_add_fusion.info_ref, bf16[32,3072]{1,0:T(8,128)(2,1)S(1)} %bitcast.15, bf16[32,3072]{1,0:T(8,128)(2,1)S(1)} %collective-permute-done.1.refs_1_, bf16[32,3072]{1,0:T(8,128)(2,1)S(1)} %collective-permute-done.2.refs_2_, ...), custom_call_target="tpu_custom_call" | custom-call | flops 2415919104 | bytes 9437184 | tf_op jit(solution)/shard_map/pallas_call | solution.py:105
  28.6 2.3 %collective-permute-done.7.refs_3_ = bf16[32,3072]{1,0:T(8,128)(2,1)S(1)} collective-permute-done((bf16[32,3072]{1,0:T(8,128)(2,1)S(1)}, bf16[32,3072]{1,0:T(8,128)(2,1)S(1)}, u32[]{:S(2)}, u32[]{:S(2)}) %collective-permute-start.7) | collective-permute-done | bytes 196640 | tf_op jit(solution)/shard_map/ppermute | solution.py:348
  30.9 2.2 %collective-permute-done.6.refs_2_ = bf16[32,3072]{1,0:T(8,128)(2,1)S(1)} collective-permute-done((bf16[32,3072]{1,0:T(8,128)(2,1)S(1)}, bf16[32,3072]{1,0:T(8,128)(2,1)S(1)}, u32[]{:S(2)}, u32[]{:S(2)}) %collective-permute-start.6) | collective-permute-done | bytes 196640 | tf_op jit(solution)/shard_map/ppermute | solution.py:348
  33.1 2.2 %shard_map.76 = (bf16[128,1536]{1,0:T(8,128)(2,1)S(1)}, bf16[128,3072]{1,0:T(8,128)(2,1)S(1)}) custom-call(s32[3]{0:T(128)S(1)} %pad_add_fusion.info_ref, bf16[32,3072]{1,0:T(8,128)(2,1)S(1)} %collective-permute-done.3.refs_0_, bf16[32,3072]{1,0:T(8,128)(2,1)S(1)} %collective-permute-done.5.refs_1_, bf16[32,3072]{1,0:T(8,128)(2,1)S(1)} %collective-permute-done.6.refs_2_, ...), custom_call_target="tpu_custom_call" | custom-call | flops 1207959552 | bytes 9437184 | tf_op jit(solution)/shard_map/pallas_call | solution.py:139
  35.5 2.2 %shard_map.77.refs_1_ = f32[128,1536]{1,0:T(8,128)S(1)} custom-call(s32[3]{0:T(128)S(1)} %pad_add_fusion.info_ref, bf16[128,3072]{1,0:T(8,128)(2,1)S(1)} %get-tuple-element.40.tokens_ref, bf16[1536,3072]{1,0:T(8,128)(2,1)S(1)} %shard_map.73.refs_4_.upper_ref, bf16[1536,3072]{1,0:T(8,128)(2,1)S(1)} %shard_map.74.refs_5_.lower_ref), custom_call_target="tpu_custom_call" | custom-call | flops 1207959552 | bytes 9437184 | tf_op jit(solution)/shard_map/pallas_call | solution.py:156
  37.7 4.4 %shard_map.78 = (bf16[256,1536]{1,0:T(8,128)(2,1)S(1)}, bf16[1536,3072]{1,0:T(8,128)(2,1)S(1)}) custom-call(s32[3]{0:T(128)S(1)} %pad_add_fusion.info_ref, f32[128,1536]{1,0:T(8,128)S(1)} %get-tuple-element.38.refs_0_, f32[128,1536]{1,0:T(8,128)S(1)} %shard_map.77.refs_1_, bf16[128,1536]{1,0:T(8,128)(2,1)S(1)} %collective-permute-done.8.refs_2_, ...), custom_call_target="tpu_custom_call" | custom-call | flops 23592960 | bytes 3145728 | tf_op jit(solution)/shard_map/pallas_call | solution.py:230
  42.6 4.3 %shard_map.79 = (f32[256,3072]{1,0:T(8,128)S(1)}, bf16[1536,3072]{1,0:T(8,128)(2,1)S(1)}) custom-call(s32[3]{0:T(128)S(1)} %pad_add_fusion.info_ref, bf16[256,1536]{1,0:T(8,128)(2,1)S(1)} %get-tuple-element.43.mixed_ref, bf16[1536,3072]{1,0:T(8,128)(2,1)S(1)} %get-tuple-element.44.weight_ref, bf16[3072,3072]{1,0:T(8,128)(2,1)} %later_ref.1), custom_call_target="tpu_custom_call" | custom-call | flops 2415919104 | bytes 9437184 | tf_op jit(solution)/shard_map/pallas_call | solution.py:263
  47.0 1.8 %shard_map.80 = (bf16[32,3072]{1,0:T(8,128)(2,1)S(1)}, bf16[32,3072]{1,0:T(8,128)(2,1)S(1)}, bf16[32,3072]{1,0:T(8,128)(2,1)S(1)}, bf16[32,3072]{1,0:T(8,128)(2,1)S(1)}) custom-call(bf16[256,1536]{1,0:T(8,128)(2,1)S(1)} %collective-permute-done.10.mixed_ref, bf16[1536,3072]{1,0:T(8,128)(2,1)S(1)} %get-tuple-element.45.weight_ref, ...), custom_call_target="tpu_custom_call" | custom-call | flops 1207959552 | bytes 9437184 | tf_op jit(solution)/shard_map/pallas_call | solution.py:295
  48.8 1.6 %collective-permute-start.13 = (bf16[32,3072]{1,0:T(8,128)(2,1)S(1)}, bf16[32,3072]{1,0:T(8,128)(2,1)S(1)}, u32[]{:S(2)}, u32[]{:S(2)}) collective-permute-start(bf16[32,3072]{1,0:T(8,128)(2,1)S(1)} %get-tuple-element.54), channel_id=1, source_target_pairs={{0,1},{1,0},{2,3},{3,2},{4,5},{5,4},{6,7},{7,6},{8,9},{9,8},{10,11... | collective-permute-start | bytes 589832 | tf_op jit(solution)/shard_map/ppermute | solution.py:348
  50.3 1.8 %shard_map.81 = (f32[32,3072]{1,0:T(8,128)S(1)}, f32[32,3072]{1,0:T(8,128)S(1)}, f32[32,3072]{1,0:T(8,128)S(1)}, f32[32,3072]{1,0:T(8,128)S(1)}) custom-call(bf16[256,1536]{1,0:T(8,128)(2,1)S(1)} %collective-permute-done.10.mixed_ref, bf16[1536,3072]{1,0:T(8,128)(2,1)S(1)} %get-tuple-element.45.weight_ref, f32[256,3072]{1,0:T(8,128)S(1)} %get-tuple-element.46.partial_ref), custom_call_target="tpu_custom_call" | custom-call | flops 1207959552 | bytes 9437184 | tf_op jit(solution)/shard_map/pallas_call | solution.py:295
  52.7 3.9 %collective-permute-done.13 = bf16[32,3072]{1,0:T(8,128)(2,1)S(1)} collective-permute-done((bf16[32,3072]{1,0:T(8,128)(2,1)S(1)}, bf16[32,3072]{1,0:T(8,128)(2,1)S(1)}, u32[]{:S(2)}, u32[]{:S(2)}) %collective-permute-start.13) | collective-permute-done | bytes 196640 | tf_op jit(solution)/shard_map/ppermute | solution.py:348
  56.7 3.6 %collective-permute-start.14 = (bf16[32,3072]{1,0:T(8,128)(2,1)S(1)}, bf16[32,3072]{1,0:T(8,128)(2,1)S(1)}, u32[]{:S(2)}, u32[]{:S(2)}) collective-permute-start(bf16[32,3072]{1,0:T(8,128)(2,1)S(1)} %add_convert_fusion.1), channel_id=1, source_target_pairs={{2,0},{3,1},{4,2},{5,3},{6,4},{7,5},{0,6},{1,7},{10,8},{11,9},{12,... | collective-permute-start | bytes 589832 | tf_op jit(solution)/shard_map/ppermute | solution.py:345
  60.2 1.5 %collective-permute-start.15 = (bf16[32,3072]{1,0:T(8,128)(2,1)S(1)}, bf16[32,3072]{1,0:T(8,128)(2,1)S(1)}, u32[]{:S(2)}, u32[]{:S(2)}) collective-permute-start(bf16[32,3072]{1,0:T(8,128)(2,1)S(1)} %get-tuple-element.56), channel_id=1, source_target_pairs={{0,1},{1,0},{2,3},{3,2},{4,5},{5,4},{6,7},{7,6},{8,9},{9,8},{10,11... | collective-permute-start | bytes 589832 | tf_op jit(solution)/shard_map/ppermute | solution.py:348
  62.5 4.7 %collective-permute-done.15 = bf16[32,3072]{1,0:T(8,128)(2,1)S(1)} collective-permute-done((bf16[32,3072]{1,0:T(8,128)(2,1)S(1)}, bf16[32,3072]{1,0:T(8,128)(2,1)S(1)}, u32[]{:S(2)}, u32[]{:S(2)}) %collective-permute-start.15) | collective-permute-done | bytes 196640 | tf_op jit(solution)/shard_map/ppermute | solution.py:348
  67.3 2.3 %collective-permute-start.16 = (bf16[32,3072]{1,0:T(8,128)(2,1)S(1)}, bf16[32,3072]{1,0:T(8,128)(2,1)S(1)}, u32[]{:S(2)}, u32[]{:S(2)}) collective-permute-start(bf16[32,3072]{1,0:T(8,128)(2,1)S(1)} %add_convert_fusion), channel_id=1, source_target_pairs={{2,0},{3,1},{4,2},{5,3},{6,4},{7,5},{0,6},{1,7},{10,8},{11,9},{12,... | collective-permute-start | bytes 589832 | tf_op jit(solution)/shard_map/ppermute | solution.py:345
  70.8 2.2 %collective-permute-done.16 = bf16[32,3072]{1,0:T(8,128)(2,1)S(1)} collective-permute-done((bf16[32,3072]{1,0:T(8,128)(2,1)S(1)}, bf16[32,3072]{1,0:T(8,128)(2,1)S(1)}, u32[]{:S(2)}, u32[]{:S(2)}) %collective-permute-start.16) | collective-permute-done | bytes 196640 | tf_op jit(solution)/shard_map/ppermute | solution.py:345
  73.8 1.3 %collective-permute-done.18 = bf16[1,16,3072]{2,1,0:T(8,128)(2,1)S(1)} collective-permute-done((bf16[1,16,3072]{2,1,0:T(8,128)(2,1)S(1)}, bf16[1,16,3072]{2,1,0:T(8,128)(2,1)S(1)}, u32[]{:S(2)}, u32[]{:S(2)}) %collective-permute-start.18) | collective-permute-done | bytes 98336 | tf_op jit(solution)/shard_map/ppermute | solution.py:487
  (40 shorter events, 8.9 us)
Async XLA Ops:
  1.0 1.5 %collective-permute-start = (bf16[16,3072]{1,0:T(8,128)(2,1)S(1)}, bf16[16,3072]{1,0:T(8,128)(2,1)S(1)}, u32[]{:S(2)}, u32[]{:S(2)}) collective-permute-start(bf16[16,3072]{1,0:T(8,128)(2,1)S(1)} %get-tuple-element.62), channel_id=1, source_target_pairs={{0,8},{8,0},{1,9},{9,1},{2,10},{10,2},{3,11},{11,3},{4,12},{12,4},... | collective-permute-start | bytes 294920 | tf_op jit(solution)/shard_map/ppermute | solution.py:441
  2.4 8.9 %collective-permute-start.3 = (bf16[32,3072]{1,0:T(8,128)(2,1)S(1)}, bf16[32,3072]{1,0:T(8,128)(2,1)S(1)}, u32[]{:S(2)}, u32[]{:S(2)}) collective-permute-start(bf16[32,3072]{1,0:T(8,128)(2,1)S(1)} %bitcast.12), channel_id=1, source_target_pairs={{0,1},{1,0},{2,3},{3,2},{4,5},{5,4},{6,7},{7,6},{8,9},{9,8},{10,11... | collective-permute-start | bytes 589832 | tf_op jit(solution)/shard_map/ppermute | solution.py:348
  5.4 9.0 %collective-permute-start.1 = (bf16[32,3072]{1,0:T(8,128)(2,1)S(1)}, bf16[32,3072]{1,0:T(8,128)(2,1)S(1)}, u32[]{:S(2)}, u32[]{:S(2)}) collective-permute-start(bf16[32,3072]{1,0:T(8,128)(2,1)S(1)} %bitcast.13), channel_id=1, source_target_pairs={{0,2},{1,3},{2,4},{3,5},{4,6},{5,7},{6,0},{7,1},{8,10},{9,11},{10,... | collective-permute-start | bytes 589832 | tf_op jit(solution)/shard_map/ppermute | solution.py:342
  11.3 9.1 %collective-permute-start.4 = (bf16[32,3072]{1,0:T(8,128)(2,1)S(1)}, bf16[32,3072]{1,0:T(8,128)(2,1)S(1)}, u32[]{:S(2)}, u32[]{:S(2)}) collective-permute-start(bf16[32,3072]{1,0:T(8,128)(2,1)S(1)} %bitcast.14), channel_id=1, source_target_pairs={{2,0},{3,1},{4,2},{5,3},{6,4},{7,5},{0,6},{1,7},{10,8},{11,9},{12,... | collective-permute-start | bytes 589832 | tf_op jit(solution)/shard_map/ppermute | solution.py:345
  14.4 9.6 %collective-permute-start.2 = (bf16[32,3072]{1,0:T(8,128)(2,1)S(1)}, bf16[32,3072]{1,0:T(8,128)(2,1)S(1)}, u32[]{:S(2)}, u32[]{:S(2)}) collective-permute-start(bf16[32,3072]{1,0:T(8,128)(2,1)S(1)} %collective-permute-done.1.refs_1_), channel_id=1, source_target_pairs={{0,2},{1,3},{2,4},{3,5},{4,6},{5,7},{6,0},{7,1},{8,10},{9,11},{10,... | collective-permute-start | bytes 589832 | tf_op jit(solution)/shard_map/ppermute | solution.py:342
  18.8 9.9 %collective-permute-start.5 = (bf16[32,3072]{1,0:T(8,128)(2,1)S(1)}, bf16[32,3072]{1,0:T(8,128)(2,1)S(1)}, u32[]{:S(2)}, u32[]{:S(2)}) collective-permute-start(bf16[32,3072]{1,0:T(8,128)(2,1)S(1)} %collective-permute-done.1.refs_1_), channel_id=1, source_target_pairs={{0,1},{1,0},{2,3},{3,2},{4,5},{5,4},{6,7},{7,6},{8,9},{9,8},{10,11... | collective-permute-start | bytes 589832 | tf_op jit(solution)/shard_map/ppermute | solution.py:348
  20.4 10.5 %collective-permute-start.7 = (bf16[32,3072]{1,0:T(8,128)(2,1)S(1)}, bf16[32,3072]{1,0:T(8,128)(2,1)S(1)}, u32[]{:S(2)}, u32[]{:S(2)}) collective-permute-start(bf16[32,3072]{1,0:T(8,128)(2,1)S(1)} %collective-permute-done.4.refs_3_), channel_id=1, source_target_pairs={{0,1},{1,0},{2,3},{3,2},{4,5},{5,4},{6,7},{7,6},{8,9},{9,8},{10,11... | collective-permute-start | bytes 589832 | tf_op jit(solution)/shard_map/ppermute | solution.py:348
  24.0 9.1 %collective-permute-start.6 = (bf16[32,3072]{1,0:T(8,128)(2,1)S(1)}, bf16[32,3072]{1,0:T(8,128)(2,1)S(1)}, u32[]{:S(2)}, u32[]{:S(2)}) collective-permute-start(bf16[32,3072]{1,0:T(8,128)(2,1)S(1)} %collective-permute-done.2.refs_2_), channel_id=1, source_target_pairs={{0,1},{1,0},{2,3},{3,2},{4,5},{5,4},{6,7},{7,6},{8,9},{9,8},{10,11... | collective-permute-start | bytes 589832 | tf_op jit(solution)/shard_map/ppermute | solution.py:348
  28.6 9.1 %collective-permute-start.8 = (bf16[128,1536]{1,0:T(8,128)(2,1)S(1)}, bf16[128,1536]{1,0:T(8,128)(2,1)S(1)}, u32[]{:S(2)}, u32[]{:S(2)}) collective-permute-start(bf16[128,1536]{1,0:T(8,128)(2,1)S(1)} %get-tuple-element.41), channel_id=1, source_target_pairs={{0,8},{8,0},{1,9},{9,1},{2,10},{10,2},{3,11},{11,3},{4,12},{12,4},... | collective-permute-start | bytes 1179656 | tf_op jit(solution)/shard_map/ppermute | solution.py:458
  35.4 2.3 %collective-permute-start.9 = (bf16[128,1536]{1,0:T(8,128)(2,1)S(1)}, bf16[128,1536]{1,0:T(8,128)(2,1)S(1)}, u32[]{:S(2)}, u32[]{:S(2)}) collective-permute-start(bf16[128,1536]{1,0:T(8,128)(2,1)S(1)} %get-tuple-element.42), channel_id=1, source_target_pairs={{0,8},{8,0},{1,9},{9,1},{2,10},{10,2},{3,11},{11,3},{4,12},{12,4},... | collective-permute-start | bytes 1179656 | tf_op jit(solution)/shard_map/ppermute | solution.py:461
  35.4 2.2 %copy-start = (f32[3,3,3072]{2,1,0:T(4,128)S(1)}, f32[3,3,3072]{2,1,0:T(4,128)}, u32[]{:S(2)}) copy-start(f32[3,3,3072]{2,1,0:T(4,128)} %refs_5_.1) | copy-start | bytes 331780
  35.5 2.2 %copy-start.2 = (f32[3072]{0:T(1024)S(1)}, f32[3072]{0:T(1024)}, u32[]{:S(2)}) copy-start(f32[3072]{0:T(1024)} %param.9) | copy-start | bytes 36868
  35.5 2.2 %copy-start.3 = (f32[3072]{0:T(1024)S(1)}, f32[3072]{0:T(1024)}, u32[]{:S(2)}) copy-start(f32[3072]{0:T(1024)} %param.11) | copy-start | bytes 36868
  42.1 4.9 %collective-permute-start.10 = (bf16[256,1536]{1,0:T(8,128)(2,1)S(1)}, bf16[256,1536]{1,0:T(8,128)(2,1)S(1)}, u32[]{:S(2)}, u32[]{:S(2)}) collective-permute-start(bf16[256,1536]{1,0:T(8,128)(2,1)S(1)} %get-tuple-element.43.mixed_ref), channel_id=1, source_target_pairs={{0,8},{8,0},{1,9},{9,1},{2,10},{10,2},{3,11},{11,3},{4,12},{12,4},... | collective-permute-start | bytes 2359304 | tf_op jit(solution)/shard_map/ppermute | solution.py:475
  48.8 24.3 %copy-start.1 = (f32[6144]{0:T(1024)S(1)}, f32[6144]{0:T(1024)}, u32[]{:S(2)}) copy-start(f32[6144]{0:T(1024)} %param.13) | copy-start | bytes 73732
  48.8 7.8 %collective-permute-start.13 = (bf16[32,3072]{1,0:T(8,128)(2,1)S(1)}, bf16[32,3072]{1,0:T(8,128)(2,1)S(1)}, u32[]{:S(2)}, u32[]{:S(2)}) collective-permute-start(bf16[32,3072]{1,0:T(8,128)(2,1)S(1)} %get-tuple-element.54), channel_id=1, source_target_pairs={{0,1},{1,0},{2,3},{3,2},{4,5},{5,4},{6,7},{7,6},{8,9},{9,8},{10,11... | collective-permute-start | bytes 589832 | tf_op jit(solution)/shard_map/ppermute | solution.py:348
  52.2 9.6 %collective-permute-start.11 = (bf16[32,3072]{1,0:T(8,128)(2,1)S(1)}, bf16[32,3072]{1,0:T(8,128)(2,1)S(1)}, u32[]{:S(2)}, u32[]{:S(2)}) collective-permute-start(bf16[32,3072]{1,0:T(8,128)(2,1)S(1)} %get-tuple-element.51), channel_id=1, source_target_pairs={{0,1},{1,0},{2,3},{3,2},{4,5},{5,4},{6,7},{7,6},{8,9},{9,8},{10,11... | collective-permute-start | bytes 589832 | tf_op jit(solution)/shard_map/ppermute | solution.py:348
  56.7 10.5 %collective-permute-start.14 = (bf16[32,3072]{1,0:T(8,128)(2,1)S(1)}, bf16[32,3072]{1,0:T(8,128)(2,1)S(1)}, u32[]{:S(2)}, u32[]{:S(2)}) collective-permute-start(bf16[32,3072]{1,0:T(8,128)(2,1)S(1)} %add_convert_fusion.1), channel_id=1, source_target_pairs={{2,0},{3,1},{4,2},{5,3},{6,4},{7,5},{0,6},{1,7},{10,8},{11,9},{12,... | collective-permute-start | bytes 589832 | tf_op jit(solution)/shard_map/ppermute | solution.py:345
  60.2 7.0 %collective-permute-start.15 = (bf16[32,3072]{1,0:T(8,128)(2,1)S(1)}, bf16[32,3072]{1,0:T(8,128)(2,1)S(1)}, u32[]{:S(2)}, u32[]{:S(2)}) collective-permute-start(bf16[32,3072]{1,0:T(8,128)(2,1)S(1)} %get-tuple-element.56), channel_id=1, source_target_pairs={{0,1},{1,0},{2,3},{3,2},{4,5},{5,4},{6,7},{7,6},{8,9},{9,8},{10,11... | collective-permute-start | bytes 589832 | tf_op jit(solution)/shard_map/ppermute | solution.py:348
  61.8 9.0 %collective-permute-start.12 = (bf16[32,3072]{1,0:T(8,128)(2,1)S(1)}, bf16[32,3072]{1,0:T(8,128)(2,1)S(1)}, u32[]{:S(2)}, u32[]{:S(2)}) collective-permute-start(bf16[32,3072]{1,0:T(8,128)(2,1)S(1)} %add_convert_fusion.2), channel_id=1, source_target_pairs={{0,2},{1,3},{2,4},{3,5},{4,6},{5,7},{6,0},{7,1},{8,10},{9,11},{10,... | collective-permute-start | bytes 589832 | tf_op jit(solution)/shard_map/ppermute | solution.py:342
  61.9 7.7 %collective-permute-start.17 = (bf16[32,3072]{1,0:T(8,128)(2,1)S(1)}, bf16[32,3072]{1,0:T(8,128)(2,1)S(1)}, u32[]{:S(2)}, u32[]{:S(2)}) collective-permute-start(bf16[32,3072]{1,0:T(8,128)(2,1)S(1)} %get-tuple-element.58), channel_id=1, source_target_pairs={{0,1},{1,0},{2,3},{3,2},{4,5},{5,4},{6,7},{7,6},{8,9},{9,8},{10,11... | collective-permute-start | bytes 589832 | tf_op jit(solution)/shard_map/ppermute | solution.py:348
  67.3 5.7 %collective-permute-start.16 = (bf16[32,3072]{1,0:T(8,128)(2,1)S(1)}, bf16[32,3072]{1,0:T(8,128)(2,1)S(1)}, u32[]{:S(2)}, u32[]{:S(2)}) collective-permute-start(bf16[32,3072]{1,0:T(8,128)(2,1)S(1)} %add_convert_fusion), channel_id=1, source_target_pairs={{2,0},{3,1},{4,2},{5,3},{6,4},{7,5},{0,6},{1,7},{10,8},{11,9},{12,... | collective-permute-start | bytes 589832 | tf_op jit(solution)/shard_map/ppermute | solution.py:345
  73.7 1.4 %collective-permute-start.18 = (bf16[1,16,3072]{2,1,0:T(8,128)(2,1)S(1)}, bf16[1,16,3072]{2,1,0:T(8,128)(2,1)S(1)}, u32[]{:S(2)}, u32[]{:S(2)}) collective-permute-start(bf16[1,16,3072]{2,1,0:T(8,128)(2,1)S(1)} %get-tuple-element.60), channel_id=1, source_target_pairs={{0,8},{8,0},{1,9},{9,1},{2,10},{10,2},{3,11},{11,3},{4,12},{12,4},... | collective-permute-start | bytes 294920 | tf_op jit(solution)/shard_map/ppermute | solution.py:487

commit v4 on v3

--- a/solution.py
+++ b/solution.py
@@ -11,17 +11,6 @@
 HBM = pl.BlockSpec(memory_space=pltpu.HBM)
 SMEM = pl.BlockSpec(memory_space=pltpu.SMEM)
 MIB = 1 << 20
-
-ERF_NUM = (0.00022905065861350646, 0.0034082910107109506, 0.050955695062380861, 0.18520832239976145, 1.128379143519084)
-ERF_DEN = (
-    -1.1791602954361697e-7,
-    0.000023547966471313185,
-    0.0010179625278914885,
-    0.014070470171167667,
-    0.11098505178285362,
-    0.49746925110067538,
-    1.0,
-)
 
 
 def tile_of(size, most):
@@ -73,14 +62,15 @@
 
 
 def gathered_rows(slot_refs, tokens_ref):
-    rows = slot_refs[0].shape[0]
-    for index, ref in enumerate(slot_refs):
-        tokens_ref[index * rows : (index + 1) * rows, :] = ref[...]
+    start = 0
+    for ref in slot_refs:
+        tokens_ref[start : start + ref.shape[0], :] = ref[...]
+        start += ref.shape[0]
 
 
 def tiles(total, width, most, body):
     tile = tile_of(width, most)
-    high = tile_of(total, 256)
+    high = tile_of(total, 256) if total > 256 else total
 
     def step_body(step, carry):
         row, col = step // (width // tile), step % (width // tile)
@@ -90,27 +80,86 @@
     lax.fori_loop(0, (total // high) * (width // tile), step_body, 0)
 
 
-def up_near(info, slots, upper, lower):
-    rows, depth = slots[0].shape
-    total = rows * len(slots)
-    split = upper.shape[0]
-    width = upper.shape[1] // 2
+def up_early(info, slots, upper, weight):
+    depth = slots[0].shape[1]
+    total = sum(slot.shape[0] for slot in slots)
+    split, units = upper.shape
+    width = units // 2
+    parts = 2
+    step = (depth - split) // parts
 
     def kernel(info_ref, *refs):
-        upper_ref, lower_ref, other_ref, own_ref, tokens_ref = refs[len(slots) :]
+        upper_ref, weight_ref, other_ref, own_ref, lower_ref, tokens_ref, sums_ref, sems = refs[len(slots) :]
+        copies = row_copies(weight_ref, split, lower_ref, sems)
+        for copy in copies:
+            copy.start()
         gathered_rows(refs[: len(slots)], tokens_ref)
-        for side, out_ref in ((1 - info_ref[0], other_ref), (info_ref[0], own_ref)):
-            product_tiles(tokens_ref, upper_ref, lower_ref, side * width, out_ref)
-
-    return pl.pallas_call(
-        kernel,
-        out_shape=(pltpu.VMEM((total, width), BF16), pltpu.VMEM((total, width), F32)),
-        in_specs=[SMEM] + [VMEM] * (len(slots) + 2),
-        out_specs=(VMEM, VMEM),
-        scratch_shapes=[pltpu.VMEM((total, depth), BF16)],
+
+        def first(down, col, tile):
+            across = pl.ds(col, tile)
+            sums_ref[down, across] = jnp.dot(tokens_ref[down, :split], upper_ref[:, across], preferred_element_type=F32)
+
+        tiles(total, units, 768, first)
+        for part, copy in enumerate(copies):
+            copy.wait()
+            deep = slice(part * step, (part + 1) * step)
+            features = slice(split + part * step, split + (part + 1) * step)
+
+            def more(down, col, tile):
+                across = pl.ds(col, tile)
+                sums_ref[down, across] += jnp.dot(
+                    tokens_ref[down, features], lower_ref[deep, across], preferred_element_type=F32
+                )
+
+            def last(out_ref, base):
+                def body(down, col, tile):
+                    across = pl.ds(pl.multiple_of(base + col, 128), tile)
+                    value = sums_ref[down, across] + jnp.dot(
+                        tokens_ref[down, features], lower_ref[deep, across], preferred_element_type=F32
+                    )
+                    out_ref[down, pl.ds(col, tile)] = value.astype(out_ref.dtype)
+
+                return body
+
+            if part < parts - 1:
+                tiles(total, units, 768, more)
+            else:
+                tiles(total, width, 768, last(other_ref, (1 - info_ref[0]) * width))
+                tiles(total, width, 768, last(own_ref, info_ref[0] * width))
+
+    return pl.pallas_call(
+        kernel,
+        out_shape=(
+            pltpu.VMEM((total, width), BF16),
+            pltpu.VMEM((total, width), F32),
+            pltpu.VMEM((depth - split, units), BF16),
+        ),
+        in_specs=[SMEM] + [VMEM] * (len(slots) + 1) + [HBM],
+        out_specs=(VMEM,) * 3,
+        scratch_shapes=[
+            pltpu.VMEM((total, depth), BF16),
+            pltpu.VMEM((total, units), F32),
+            pltpu.SemaphoreType.DMA((parts,)),
+        ],
         cost_estimate=cost(4 * total * depth * width, 2 * depth * width),
-        compiler_params=params(10),
-    )(info, *slots, upper, lower)
+        compiler_params=params(26),
+    )(info, *slots, upper, weight)
+
+
+def join(parts):
+    rows = sum(part.shape[0] for part in parts)
+
+    def kernel(*refs):
+        gathered_rows(refs[:-1], refs[-1])
+
+    return pl.pallas_call(
+        kernel,
+        out_shape=pltpu.VMEM((rows, parts[0].shape[1]), parts[0].dtype),
+        in_specs=[VMEM] * len(parts),
+        out_specs=VMEM,
+        cost_estimate=cost(0, 4 * rows * parts[0].shape[1]),
+        compiler_params=params(1),
+    )(*parts)
 
 
 def product_tiles(tokens_ref, upper_ref, lower_ref, base, out_ref):
@@ -127,8 +176,8 @@
 
 
 def up_other(info, slots, upper, lower):
-    rows, depth = slots[0].shape
-    total = rows * len(slots)
+    depth = slots[0].shape[1]
+    total = sum(slot.shape[0] for slot in slots)
     width = upper.shape[1] // 2
 
     def kernel(info_ref, *refs):
@@ -164,28 +213,21 @@
 
 
 def gelu(value):
-    arg = jnp.clip(value * 0.7071067811865476, -3.832506856900711, 3.832506856900711)
-    square = arg * arg
-    num = jnp.full_like(square, ERF_NUM[0])
-    for coefficient in ERF_NUM[1:]:
-        num = num * square + coefficient
-    den = jnp.full_like(square, ERF_DEN[0])
-    for coefficient in ERF_DEN[1:]:
-        den = den * square + coefficient
-    return 0.5 * value * (1.0 + arg * num / den)
-
-
-def conv(info, own, received, up_bias, conv_weight, conv_bias, later, ring_size, lanes_of, grid_y):
+    return 0.5 * value * (1.0 + lax.erf(value * 0.7071067811865476))
+
+
+def conv(info, own, received, up_bias, conv_weight, conv_bias, later, groups, links, rows, grid_y):
     width = own[0].shape[1]
-    rows = own[0].shape[0] // ring_size
-    blocks = ring_size * lanes_of
+    slots = [(group, index) + slot for group, members in enumerate(groups) for index, slot in enumerate(members)]
+    blocks = len(slots)
     total = rows * blocks
+    count = len(groups)
     lanes = 128
     extent_x = total // grid_y
 
     def kernel(info_ref, *refs):
-        own_refs, received_refs = refs[:lanes_of], refs[lanes_of : 2 * lanes_of]
-        up_bias_ref, weight_ref, bias_ref, later_ref, out_ref, later_out, hidden, sems = refs[2 * lanes_of :]
+        own_refs, received_refs = refs[:count], refs[count : 2 * count]
+        up_bias_ref, weight_ref, bias_ref, later_ref, out_ref, later_out, hidden, sems = refs[2 * count :]
         copies = row_copies(later_ref, pl.multiple_of(info_ref[0] * width, 16), later_out, sems)
         for copy in copies:
             copy.start()
@@ -195,9 +237,8 @@
         first, last = at_y == 0, at_y == grid_y - 1
         base = info_ref[0] * width
         places = [
-            lax.rem(info_ref[1] + (ring_size - j), ring_size) * lanes_of + lax.rem(info_ref[2] + q, lanes_of)
-            for q in range(lanes_of)
-            for j in range(ring_size)
+            lax.rem(info_ref[1] + (links.ring - j), links.ring) * links.lanes + lax.rem(info_ref[2] + q, links.lanes)
+            for _, _, q, j in slots
         ]
 
         def body(col, carry):
@@ -205,9 +246,9 @@
             absolute = pl.ds(pl.multiple_of(base + col * lanes, lanes), lanes)
             shift = up_bias_ref[:, absolute]
             for slot in range(blocks):
-                q, j = slot // ring_size, slot % ring_size
-                down = slice(j * rows, (j + 1) * rows)
-                value = own_refs[q][down, across] + received_refs[q][down, across].astype(F32) + shift
+                group, index, _, _ = slots[slot]
+                down = slice(index * rows, (index + 1) * rows)
+                value = own_refs[group][down, across] + received_refs[group][down, across].astype(F32) + shift
                 target = pl.multiple_of(places[slot] * rows + grid_y, grid_y)
                 hidden[pl.ds(target, rows), :] = value.astype(BF16).astype(F32)
             weights = [[weight_ref[a, b : b + 1, absolute] for b in range(3)] for a in range(3)]
@@ -230,7 +271,7 @@
     return pl.pallas_call(
         kernel,
         out_shape=(pltpu.VMEM((total, width), BF16), pltpu.VMEM((width, later.shape[1]), BF16)),
-        in_specs=[SMEM] + [VMEM] * (2 * lanes_of + 3) + [HBM],
+        in_specs=[SMEM] + [VMEM] * (2 * count + 3) + [HBM],
         out_specs=(VMEM, VMEM),
         scratch_shapes=[pltpu.VMEM(((extent_x + 2) * grid_y, lanes), F32), pltpu.SemaphoreType.DMA((4,))],
         cost_estimate=cost(60 * total * width, 8 * total * width),
@@ -271,32 +312,43 @@
     )(info, mixed, weight, later)
 
 
-def down_other(mixed, weight, partial, rows, first, blocks, kind):
+def down_other(mixed, weight, partial, first, outs):
     depth = mixed.shape[1]
     width = weight.shape[1]
-    total = rows * blocks
+    total = sum(rows for rows, _ in outs)
     tile = tile_of(width, 1024)
-    high = rows * max(n for n in range(1, blocks + 1) if blocks % n == 0 and rows * n <= max(256, rows))
 
     def kernel(mixed_ref, weight_ref, partial_ref, *out_refs):
         def body(step, carry):
             across = pl.ds(pl.multiple_of(step * tile, tile), tile)
-            for start in range(0, total, high):
-                down = slice(first + start, first + start + high)
+            start = 0
+            pieces = []
+            for out_ref in out_refs:
+                rows = out_ref.shape[0]
+                pieces.append((out_ref, start, rows))
+                start += rows
+            while pieces:
+                take = 1
+                while take < len(pieces) and sum(rows for _, _, rows in pieces[: take + 1]) <= 256:
+                    take += 1
+                low = pieces[0][1]
+                high = sum(rows for _, _, rows in pieces[:take])
+                down = slice(first + low, first + low + high)
                 value = partial_ref[down, across] + jnp.dot(
                     mixed_ref[down, :], weight_ref[:, across], preferred_element_type=F32
                 )
-                for low in range(0, high, rows):
-                    out_refs[(start + low) // rows][:, across] = value[low : low + rows].astype(kind)
+                for out_ref, at, rows in pieces[:take]:
+                    out_ref[:, across] = value[at - low : at - low + rows].astype(out_ref.dtype)
+                pieces = pieces[take:]
             return carry
 
         lax.fori_loop(0, width // tile, body, 0)
 
     return pl.pallas_call(
         kernel,
-        out_shape=(pltpu.VMEM((rows, width), kind),) * blocks,
+        out_shape=tuple(pltpu.VMEM((rows, width), kind) for rows, kind in outs),
         in_specs=[VMEM] * 3,
-        out_specs=(VMEM,) * blocks,
+        out_specs=(VMEM,) * len(outs),
         cost_estimate=cost(2 * total * depth * width, 2 * depth * width),
         compiler_params=params(10),
     )(mixed, weight, partial)
@@ -334,6 +386,7 @@
     def __init__(self, count):
         self.lanes = 2 if count % 2 == 0 else 1
         self.ring = count // self.lanes
+        self.half = self.ring // 2
         self.upward = [(t, (t + self.lanes) % count) for t in range(count)]
         self.downward = [(t, s) for s, t in self.upward]
         self.pairs = [(t, t ^ 1) for t in range(count)]
@@ -348,76 +401,75 @@
         return lax.ppermute(value, "tp", self.pairs)
 
 
-def gather(links, block, fetches):
-    ring = links.ring
-    half_way = ring // 2
-    column, beside = {0: block}, {}
-    first, second = fetches
-
-    def hand(slot):
+def gather(links, block, fetch_upper):
+    column, beside = [block], []
+    if links.lanes > 1:
+        beside.append(links.cross(block))
+    if links.half:
+        column.append(links.up(block))
+    upper = fetch_upper()
+    start = block
+    if links.lanes > 1:
+        if links.half:
+            upper, beside[0], column[1] = tie(upper, beside[0], column[1])
+        if links.half + 1 < links.ring:
+            start = join([block, beside[0]])
+    for slot in range(1, links.half + 1):
+        if slot > 1:
+            column.append(links.up(column[slot - 1]))
         if links.lanes > 1:
-            beside[slot] = links.cross(column[slot])
-
-    if ring > 1:
-        column[1] = links.up(block)
-    hand(0)
-    upper = first()
-    if ring > 2:
-        if links.lanes > 1:
-            late, upper, beside[0] = tie(block, upper, beside[0])
-        else:
-            late, upper = tie(block, upper)
-        column[ring - 1] = links.down(late)
-    if ring > 1:
-        hand(1)
-    if half_way > 1:
-        column[2] = links.up(column[1])
-    lower = second(column[1] if ring > 1 else block)
-    for distance in range(1, half_way + 1):
-        if distance > 2:
-            column[distance] = links.up(column[distance - 1])
-        if distance > 1:
-            hand(distance)
-        if 1 < distance < ring - half_way:
-            column[ring - distance] = links.down(column[ring - distance + 1])
-        if distance < ring - half_way:
-            hand(ring - distance)
-    return [column[j] for j in range(ring)], [beside[j] for j in range(ring) if links.lanes > 1], upper, lower
-
-
-def scatter(links, far, make_near):
-    ring = links.ring
-    half_way = ring // 2
-    upper_chain = list(range(half_way, 0, -1))
-    lower_chain = list(range(half_way + 1, ring))
-    order = [slot for pair in zip(upper_chain, lower_chain) for slot in pair]
-    order += [slot for slot in upper_chain + lower_chain if slot not in order] + [0]
-    far = list(far)
+            beside.append(links.cross(column[slot]))
+    if links.half > 1 and links.half + 1 < links.ring:
+        start, column[-1] = tie(start, column[-1])
+    both = []
+    for _ in range(links.half + 1, links.ring):
+        start = links.down(start)
+        both.append(start)
+    early = column + beside[: links.half]
+    late = beside[links.half :] + both
+    names_early = [(0, j) for j in range(links.half + 1)] + [(1, j) for j in range(len(beside[: links.half]))]
+    names_late = [(1, links.half)] * len(beside[links.half :])
+    names_late += [(q, j) for j in range(links.ring - 1, links.half, -1) for q in range(links.lanes)]
+    return early, late, [names_early] + ([names_late] if late else []), upper
+
+
+def scatter(links, rows, names, late, early):
+    ring, half = links.ring, links.half
+    terms = {}
+
+    def bring(make, members):
+        terms.update(zip(members, make([(rows, BF16 if q else F32) for q, _ in members])))
+
+    up_slots, down_slots = list(range(half + 1, ring)), list(range(half, 0, -1))
+    order = [slot for both in zip(down_slots, up_slots) for slot in both]
+    order += [slot for slot in down_slots + up_slots if slot not in order] + [0]
     crossed, arrived, ready = {}, {slot: [] for slot in range(ring)}, {}
-    if links.lanes > 1:
-        crossed[order[0]] = links.cross(far[order[0]])
-    near = make_near()
+    if len(names) > 1:
+        bring(late, names[1])
+    if links.lanes > 1 and half:
+        crossed[half] = links.cross(terms[1, half])
+    bring(early, names[0])
+    if links.lanes > 1 and not half:
+        crossed[0] = links.cross(terms[1, 0])
     for position, slot in enumerate(order):
         if links.lanes > 1 and position + 1 < ring:
             after = order[position + 1]
-            token = near[0] if position == 0 else ready[order[position - 1]]
-            far[after], token = tie(far[after], token)
             if position == 0:
-                near[0] = token
+                terms[1, after], terms[0, 0] = tie(terms[1, after], terms[0, 0])
             else:
-                ready[order[position - 1]] = token
-            crossed[after] = links.cross(far[after])
-        terms = arrived[slot] + ([crossed[slot]] if links.lanes > 1 else [])
-        total = near[slot]
-        for term in terms:
+                before = order[position - 1]
+                terms[1, after], ready[before] = tie(terms[1, after], ready[before])
+            crossed[after] = links.cross(terms[1, after])
+        total = terms[0, slot]
+        for term in arrived[slot] + ([crossed[slot]] if links.lanes > 1 else []):
             total = total + term.astype(F32)
-        if slot == 0:
-            return total
-        ready[slot] = total.astype(BF16)
-        if slot <= half_way:
-            arrived[slot - 1].append(links.down(ready[slot]))
-        else:
-            arrived[(slot + 1) % ring].append(links.up(ready[slot]))
+        if slot:
+            ready[slot] = total.astype(BF16)
+            if slot <= half:
+                arrived[slot - 1].append(links.down(ready[slot]))
+            else:
+                arrived[(slot + 1) % ring].append(links.up(ready[slot]))
+    return total
 
 
 def local(tokens, up_weight, up_bias, conv_weight, conv_bias, down_weight, down_bias):
@@ -444,22 +496,14 @@
     block = block.reshape(rows, half)
     block, info = tie(block, info)
 
-    part_bytes = part * units * 2
-
-    def fetch_lower(token):
-        late, _ = tie(info, token)
-        return fetch(late, up_weight, lambda c: 0 * c + part, part, part_bytes)
-
-    near, far, upper, lower = gather(
-        links, block, (lambda: fetch(info, up_weight, lambda c: 0 * c, part, 0), fetch_lower)
-    )
-
-    near_other, near_own = up_near(info, near, upper, lower)
-    own, received = [near_own], [lax.ppermute(near_other, "sp", swap)]
-    if far:
-        far_other, tokens_far = up_other(info, far, upper, lower)
-        received.append(lax.ppermute(far_other, "sp", swap))
-        own.append(up_own(info, tokens_far, upper, lower))
+    early, late, groups, upper = gather(links, block, lambda: fetch(info, up_weight, lambda c: 0 * c, part, 0))
+
+    early_other, early_own, lower = up_early(info, early, upper, up_weight)
+    own, received = [early_own], [lax.ppermute(early_other, "sp", swap)]
+    if late:
+        late_other, late_tokens = up_other(info, late, upper, lower)
+        received.append(lax.ppermute(late_other, "sp", swap))
+        own.append(up_own(info, late_tokens, upper, lower))
     mixed, down_mine = conv(
         info,
         own,
@@ -468,22 +512,24 @@
         conv_weight,
         conv_bias.reshape(1, units),
         down_weight,
-        links.ring,
-        links.lanes,
+        groups,
+        links,
+        rows,
         grid_y,
     )
     mixed_received = lax.ppermute(mixed, "sp", swap)
     product, down_theirs = down_own(info, mixed, down_mine, down_weight)
 
-    sent = []
-    if far:
-        sent = down_other(mixed_received, down_theirs, product, rows, links.ring * rows, links.ring, BF16)
+    early_rows = rows * len(groups[0])
     total = scatter(
-        links, sent, lambda: list(down_other(mixed_received, down_theirs, product, rows, 0, links.ring, F32))
+        links,
+        rows,
+        groups,
+        lambda outs: down_other(mixed_received, down_theirs, product, early_rows, outs),
+        lambda outs: down_other(mixed_received, down_theirs, product, 0, outs),
     )
-    totals = [total]
-
-    stay, leave = finish(info, totals, down_bias.reshape(1, width_model), cols, grid_half)
+
+    stay, leave = finish(info, [total], down_bias.reshape(1, width_model), cols, grid_half)
     arrive = lax.ppermute(leave, "sp", swap)
     return jnp.where(core == 0, jnp.concatenate([stay, arrive], -1), jnp.concatenate([arrive, stay], -1))
 

time: 75.9 us -> 73.1 us (0.963)
  starting transfers between devices: 22.3 us -> 16 us
  waiting for transfers between devices: 21.4 us -> 26.5 us
  Pallas kernels: 29.8 us -> 28.3 us
    ppermute x3, waiting for transfers between devices: 3.96 us -> 12 us  [up(): return lax.ppermute(value, 'tp', self.upward)]
    ppermute x3, starting transfers between devices: 8.98 us -> 3.6 us  [down(): return lax.ppermute(value, 'tp', self.downward)]
    ppermute x8 -> x7, waiting for transfers between devices: 13.1 us -> 8.67 us  [cross(): return lax.ppermute(value, 'tp', self.pairs)]
    pallas_call x2 -> x1, Pallas kernels: 8.68 us -> 4.34 us  [fetch(): pl.pallas_call(kernel, out_shape=pltpu.VMEM((count, weight.shape[1]), wei...]
    pallas_call x3 -> x4, Pallas kernels: 7.41 us -> 9.96 us  [the longest x1 5.96 us: up_early(): pl.pallas_call(kernel, out_shape=(pltpu.VMEM((total, width), BF16), pltpu...]
    ppermute x8 -> x7, starting transfers between devices: 10.4 us -> 8.65 us  [cross(): return lax.ppermute(value, 'tp', self.pairs)]
    ppermute x3, waiting for transfers between devices: 2.19 us -> 3.64 us  [down(): return lax.ppermute(value, 'tp', self.downward)]
    ppermute x3, starting transfers between devices: 1.64 us -> 2.45 us  [up(): return lax.ppermute(value, 'tp', self.upward)]
  transfers between devices with their start and end apart: 19 -> 18, of which waited for: 9 -> 11; matrix products, arithmetic and copies ran while one was open for 0% -> 0% of each run, Pallas kernels for 30% -> 29%
where the time goes in v4:
time: 73.1 us; the launch traced here: 73 us
  Pallas kernels  28.3 us (39%)
  waiting for transfers between devices  26.5 us (36%)
  starting transfers between devices  16 us (22%)
  other arithmetic  1.05 us (1%)
  local copies, waits for them, and re-layouts  0.98 us (1%)
    ppermute x3, waiting for transfers between devices, up(): return lax.ppermute(value, 'tp', self.upward)  12 us
    ppermute x7, waiting for transfers between devices, cross(): return lax.ppermute(value, 'tp', self.pairs)  8.67 us
    ppermute x7, starting transfers between devices, cross(): return lax.ppermute(value, 'tp', self.pairs)  8.65 us
    pallas_call x1, Pallas kernels, up_early(): pl.pallas_call(kernel, out_shape=(pltpu.VMEM((total, width), BF16), pltpu...  5.96 us
    pallas_call x1, Pallas kernels, conv(): pl.pallas_call(kernel, out_shape=(pltpu.VMEM((total, width), BF16), pltpu...  4.35 us
    pallas_call x1, Pallas kernels, down_own(): pl.pallas_call(kernel, out_shape=(pltpu.VMEM((total, width), F32), pltpu....  4.35 us
    pallas_call x1, Pallas kernels, fetch(): pl.pallas_call(kernel, out_shape=pltpu.VMEM((count, weight.shape[1]), wei...  4.34 us
    pallas_call x2, Pallas kernels, down_other(): pl.pallas_call(kernel, out_shape=tuple((pltpu.VMEM((rows, width), kind) f...  3.98 us
  transfers between devices with their start and end apart: 18, of which 11 were waited for; matrix products, arithmetic and copies ran while one was open for 0% of the time, Pallas kernels for 29%

profile of v4, /device:TPU:0, one launch (start us, length us, event | category | flops | bytes accessed | tf_op | source)
XLA Modules:
  0.0 73.0 jit_solution(13842437982295681014)
XLA Ops:
  2.4 2.9 %collective-permute-start.1 = (bf16[32,3072]{1,0:T(8,128)(2,1)S(1)}, bf16[32,3072]{1,0:T(8,128)(2,1)S(1)}, u32[]{:S(2)}, u32[]{:S(2)}) collective-permute-start(bf16[32,3072]{1,0:T(8,128)(2,1)S(1)} %bitcast.12), channel_id=1, source_target_pairs={{0,1},{1,0},{2,3},{3,2},{4,5},{5,4},{6,7},{7,6},{8,9},{9,8},{10,11... | collective-permute-start | bytes 589832 | tf_op jit(solution)/shard_map/ppermute | solution.py:401
  5.4 1.6 %collective-permute-start.2 = (bf16[32,3072]{1,0:T(8,128)(2,1)S(1)}, bf16[32,3072]{1,0:T(8,128)(2,1)S(1)}, u32[]{:S(2)}, u32[]{:S(2)}) collective-permute-start(bf16[32,3072]{1,0:T(8,128)(2,1)S(1)} %bitcast.13), channel_id=1, source_target_pairs={{0,2},{1,3},{2,4},{3,5},{4,6},{5,7},{6,0},{7,1},{8,10},{9,11},{10,... | collective-permute-start | bytes 589832 | tf_op jit(solution)/shard_map/ppermute | solution.py:395
  7.0 4.3 %shard_map.73.refs_5_.refs_2_.upper_ref = bf16[1536,3072]{1,0:T(8,128)(2,1)S(1)} custom-call(s32[3]{0:T(128)S(1)} %pad_add_fusion.info_ref, bf16[3072,3072]{1,0:T(8,128)(2,1)} %refs_6_.1), custom_call_target="tpu_custom_call" | custom-call | bytes 18874368 | tf_op jit(solution)/shard_map/pallas_call | solution.py:53
  11.3 2.6 %collective-permute-done.2.refs_1_ = bf16[32,3072]{1,0:T(8,128)(2,1)S(1)} collective-permute-done((bf16[32,3072]{1,0:T(8,128)(2,1)S(1)}, bf16[32,3072]{1,0:T(8,128)(2,1)S(1)}, u32[]{:S(2)}, u32[]{:S(2)}) %collective-permute-start.2) | collective-permute-done | bytes 196640 | tf_op jit(solution)/shard_map/ppermute | solution.py:395
  14.5 8.1 %collective-permute-done.3.refs_2_ = bf16[32,3072]{1,0:T(8,128)(2,1)S(1)} collective-permute-done((bf16[32,3072]{1,0:T(8,128)(2,1)S(1)}, bf16[32,3072]{1,0:T(8,128)(2,1)S(1)}, u32[]{:S(2)}, u32[]{:S(2)}) %collective-permute-start.3) | collective-permute-done | bytes 196640 | tf_op jit(solution)/shard_map/ppermute | solution.py:395
  23.4 6.0 %shard_map.75 = (bf16[160,1536]{1,0:T(8,128)(2,1)S(1)}, f32[160,1536]{1,0:T(8,128)S(1)}, bf16[1536,3072]{1,0:T(8,128)(2,1)S(1)}) custom-call(s32[3]{0:T(128)S(1)} %pad_add_fusion.info_ref, bf16[32,3072]{1,0:T(8,128)(2,1)S(1)} %bitcast.15, bf16[32,3072]{1,0:T(8,128)(2,1)S(1)} %collective-permute-done.2.refs_1_, ...), custom_call_target="tpu_custom_call" | custom-call | flops 3019898880 | bytes 9437184 | tf_op jit(solution)/shard_map/pallas_call | solution.py:130
  29.4 1.5 %collective-permute-done.6.refs_1_ = bf16[64,3072]{1,0:T(8,128)(2,1)S(1)} collective-permute-done((bf16[64,3072]{1,0:T(8,128)(2,1)S(1)}, bf16[64,3072]{1,0:T(8,128)(2,1)S(1)}, u32[]{:S(2)}, u32[]{:S(2)}) %collective-permute-start.6) | collective-permute-done | bytes 393248 | tf_op jit(solution)/shard_map/ppermute | solution.py:398
  30.9 2.4 %shard_map.76 = (bf16[96,1536]{1,0:T(8,128)(2,1)S(1)}, bf16[96,3072]{1,0:T(8,128)(2,1)S(1)}) custom-call(s32[3]{0:T(128)S(1)} %pad_add_fusion.info_ref, bf16[32,3072]{1,0:T(8,128)(2,1)S(1)} %collective-permute-done.5.refs_0_, bf16[64,3072]{1,0:T(8,128)(2,1)S(1)} %collective-permute-done.6.refs_1_, ...), custom_call_target="tpu_custom_call" | custom-call | flops 905969664 | bytes 9437184 | tf_op jit(solution)/shard_map/pallas_call | solution.py:188
  33.4 2.3 %shard_map.77.refs_1_ = f32[96,1536]{1,0:T(8,128)S(1)} custom-call(s32[3]{0:T(128)S(1)} %pad_add_fusion.info_ref, bf16[96,3072]{1,0:T(8,128)(2,1)S(1)} %get-tuple-element.44.tokens_ref, bf16[1536,3072]{1,0:T(8,128)(2,1)S(1)} %shard_map.73.refs_5_.refs_2_.upper_ref, bf16[1536,3072]{1,0:T(8,128)(2,1)S(1)} %get-tuple-element.43.refs_3_.lower_ref), custom_call_target="tpu_custom_call" | custom-call | flops 905969664 | bytes 9437184 | tf_op jit(solution)/shard_map/pallas_call | solution.py:205
  35.8 4.4 %shard_map.78 = (bf16[256,1536]{1,0:T(8,128)(2,1)S(1)}, bf16[1536,3072]{1,0:T(8,128)(2,1)S(1)}) custom-call(s32[3]{0:T(128)S(1)} %pad_add_fusion.info_ref, f32[160,1536]{1,0:T(8,128)S(1)} %get-tuple-element.41.refs_0_, f32[96,1536]{1,0:T(8,128)S(1)} %shard_map.77.refs_1_, bf16[160,1536]{1,0:T(8,128)(2,1)S(1)} %collective-permute-done.7.refs_2_, ...), custom_call_target="tpu_custom_call" | custom-call | flops 23592960 | bytes 3145728 | tf_op jit(solution)/shard_map/pallas_call | solution.py:271
  40.7 4.3 %shard_map.79 = (f32[256,3072]{1,0:T(8,128)S(1)}, bf16[1536,3072]{1,0:T(8,128)(2,1)S(1)}) custom-call(s32[3]{0:T(128)S(1)} %pad_add_fusion.info_ref, bf16[256,1536]{1,0:T(8,128)(2,1)S(1)} %get-tuple-element.47.mixed_ref, bf16[1536,3072]{1,0:T(8,128)(2,1)S(1)} %get-tuple-element.48.weight_ref, bf16[3072,3072]{1,0:T(8,128)(2,1)} %later_ref.1), custom_call_target="tpu_custom_call" | custom-call | flops 2415919104 | bytes 9437184 | tf_op jit(solution)/shard_map/pallas_call | solution.py:304
  45.0 1.9 %shard_map.80 = (bf16[32,3072]{1,0:T(8,128)(2,1)S(1)}, f32[32,3072]{1,0:T(8,128)S(1)}, bf16[32,3072]{1,0:T(8,128)(2,1)S(1)}) custom-call(bf16[256,1536]{1,0:T(8,128)(2,1)S(1)} %collective-permute-done.9.mixed_ref, bf16[1536,3072]{1,0:T(8,128)(2,1)S(1)} %get-tuple-element.49.weight_ref, f32[256,3072]{1,0:T(8,128)S(1)} %get-tuple-element.50.partial_ref), custom_call_target="tpu_custom_call" | custom-call | flops 905969664 | bytes 9437184 | tf_op jit(solution)/shard_map/pallas_call | solution.py:347
  47.9 2.1 %shard_map.81 = (f32[32,3072]{1,0:T(8,128)S(1)}, f32[32,3072]{1,0:T(8,128)S(1)}, f32[32,3072]{1,0:T(8,128)S(1)}, bf16[32,3072]{1,0:T(8,128)(2,1)S(1)}, bf16[32,3072]{1,0:T(8,128)(2,1)S(1)}) custom-call(bf16[256,1536]{1,0:T(8,128)(2,1)S(1)} %collective-permute-done.9.mixed_ref, bf16[1536,3072]{1,0:T(8,128)(2,1)S(1)} %get-tuple-element.49.weight_ref, ...), custom_call_target="tpu_custom_call" | custom-call | flops 1509949440 | bytes 9437184 | tf_op jit(solution)/shard_map/pallas_call | solution.py:347
  50.0 1.2 %collective-permute-start.10 = (bf16[32,3072]{1,0:T(8,128)(2,1)S(1)}, bf16[32,3072]{1,0:T(8,128)(2,1)S(1)}, u32[]{:S(2)}, u32[]{:S(2)}) collective-permute-start(bf16[32,3072]{1,0:T(8,128)(2,1)S(1)} %get-tuple-element.55), channel_id=1, source_target_pairs={{0,1},{1,0},{2,3},{3,2},{4,5},{5,4},{6,7},{7,6},{8,9},{9,8},{10,11... | collective-permute-start | bytes 589832 | tf_op jit(solution)/shard_map/ppermute | solution.py:401
  51.2 3.6 %collective-permute-done.12 = bf16[32,3072]{1,0:T(8,128)(2,1)S(1)} collective-permute-done((bf16[32,3072]{1,0:T(8,128)(2,1)S(1)}, bf16[32,3072]{1,0:T(8,128)(2,1)S(1)}, u32[]{:S(2)}, u32[]{:S(2)}) %collective-permute-start.12) | collective-permute-done | bytes 196640 | tf_op jit(solution)/shard_map/ppermute | solution.py:401
  54.9 2.0 %collective-permute-start.13 = (bf16[32,3072]{1,0:T(8,128)(2,1)S(1)}, bf16[32,3072]{1,0:T(8,128)(2,1)S(1)}, u32[]{:S(2)}, u32[]{:S(2)}) collective-permute-start(bf16[32,3072]{1,0:T(8,128)(2,1)S(1)} %add_convert_fusion.1), channel_id=1, source_target_pairs={{2,0},{3,1},{4,2},{5,3},{6,4},{7,5},{0,6},{1,7},{10,8},{11,9},{12,... | collective-permute-start | bytes 589832 | tf_op jit(solution)/shard_map/ppermute | solution.py:398
  56.9 1.0 %collective-permute-start.14 = (bf16[32,3072]{1,0:T(8,128)(2,1)S(1)}, bf16[32,3072]{1,0:T(8,128)(2,1)S(1)}, u32[]{:S(2)}, u32[]{:S(2)}) collective-permute-start(bf16[32,3072]{1,0:T(8,128)(2,1)S(1)} %get-tuple-element.60), channel_id=1, source_target_pairs={{0,1},{1,0},{2,3},{3,2},{4,5},{5,4},{6,7},{7,6},{8,9},{9,8},{10,11... | collective-permute-start | bytes 589832 | tf_op jit(solution)/shard_map/ppermute | solution.py:401
  59.6 1.2 %collective-permute-start.16 = (bf16[32,3072]{1,0:T(8,128)(2,1)S(1)}, bf16[32,3072]{1,0:T(8,128)(2,1)S(1)}, u32[]{:S(2)}, u32[]{:S(2)}) collective-permute-start(bf16[32,3072]{1,0:T(8,128)(2,1)S(1)} %get-tuple-element.62), channel_id=1, source_target_pairs={{0,1},{1,0},{2,3},{3,2},{4,5},{5,4},{6,7},{7,6},{8,9},{9,8},{10,11... | collective-permute-start | bytes 589832 | tf_op jit(solution)/shard_map/ppermute | solution.py:401
  60.8 3.1 %collective-permute-done.14 = bf16[32,3072]{1,0:T(8,128)(2,1)S(1)} collective-permute-done((bf16[32,3072]{1,0:T(8,128)(2,1)S(1)}, bf16[32,3072]{1,0:T(8,128)(2,1)S(1)}, u32[]{:S(2)}, u32[]{:S(2)}) %collective-permute-start.14) | collective-permute-done | bytes 196640 | tf_op jit(solution)/shard_map/ppermute | solution.py:401
  64.1 1.6 %collective-permute-start.15 = (bf16[32,3072]{1,0:T(8,128)(2,1)S(1)}, bf16[32,3072]{1,0:T(8,128)(2,1)S(1)}, u32[]{:S(2)}, u32[]{:S(2)}) collective-permute-start(bf16[32,3072]{1,0:T(8,128)(2,1)S(1)} %add_convert_fusion), channel_id=1, source_target_pairs={{2,0},{3,1},{4,2},{5,3},{6,4},{7,5},{0,6},{1,7},{10,8},{11,9},{12,... | collective-permute-start | bytes 589832 | tf_op jit(solution)/shard_map/ppermute | solution.py:398
  65.6 1.1 %collective-permute-done.16 = bf16[32,3072]{1,0:T(8,128)(2,1)S(1)} collective-permute-done((bf16[32,3072]{1,0:T(8,128)(2,1)S(1)}, bf16[32,3072]{1,0:T(8,128)(2,1)S(1)}, u32[]{:S(2)}, u32[]{:S(2)}) %collective-permute-start.16) | collective-permute-done | bytes 196640 | tf_op jit(solution)/shard_map/ppermute | solution.py:401
  66.8 1.3 %collective-permute-done.11 = bf16[32,3072]{1,0:T(8,128)(2,1)S(1)} collective-permute-done((bf16[32,3072]{1,0:T(8,128)(2,1)S(1)}, bf16[32,3072]{1,0:T(8,128)(2,1)S(1)}, u32[]{:S(2)}, u32[]{:S(2)}) %collective-permute-start.11) | collective-permute-done | bytes 196640 | tf_op jit(solution)/shard_map/ppermute | solution.py:395
  68.0 2.2 %collective-permute-done.15 = bf16[32,3072]{1,0:T(8,128)(2,1)S(1)} collective-permute-done((bf16[32,3072]{1,0:T(8,128)(2,1)S(1)}, bf16[32,3072]{1,0:T(8,128)(2,1)S(1)}, u32[]{:S(2)}, u32[]{:S(2)}) %collective-permute-start.15) | collective-permute-done | bytes 196640 | tf_op jit(solution)/shard_map/ppermute | solution.py:398
  71.0 1.3 %collective-permute-done.17 = bf16[1,16,3072]{2,1,0:T(8,128)(2,1)S(1)} collective-permute-done((bf16[1,16,3072]{2,1,0:T(8,128)(2,1)S(1)}, bf16[1,16,3072]{2,1,0:T(8,128)(2,1)S(1)}, u32[]{:S(2)}, u32[]{:S(2)}) %collective-permute-start.17) | collective-permute-done | bytes 98336 | tf_op jit(solution)/shard_map/ppermute | solution.py:533
  (38 shorter events, 8.7 us)
Async XLA Ops:
  1.0 1.5 %collective-permute-start = (bf16[16,3072]{1,0:T(8,128)(2,1)S(1)}, bf16[16,3072]{1,0:T(8,128)(2,1)S(1)}, u32[]{:S(2)}, u32[]{:S(2)}) collective-permute-start(bf16[16,3072]{1,0:T(8,128)(2,1)S(1)} %get-tuple-element.66), channel_id=1, source_target_pairs={{0,8},{8,0},{1,9},{9,1},{2,10},{10,2},{3,11},{11,3},{4,12},{12,4},... | collective-permute-start | bytes 294920 | tf_op jit(solution)/shard_map/ppermute | solution.py:493
  2.4 8.9 %collective-permute-start.1 = (bf16[32,3072]{1,0:T(8,128)(2,1)S(1)}, bf16[32,3072]{1,0:T(8,128)(2,1)S(1)}, u32[]{:S(2)}, u32[]{:S(2)}) collective-permute-start(bf16[32,3072]{1,0:T(8,128)(2,1)S(1)} %bitcast.12), channel_id=1, source_target_pairs={{0,1},{1,0},{2,3},{3,2},{4,5},{5,4},{6,7},{7,6},{8,9},{9,8},{10,11... | collective-permute-start | bytes 589832 | tf_op jit(solution)/shard_map/ppermute | solution.py:401
  5.4 8.5 %collective-permute-start.2 = (bf16[32,3072]{1,0:T(8,128)(2,1)S(1)}, bf16[32,3072]{1,0:T(8,128)(2,1)S(1)}, u32[]{:S(2)}, u32[]{:S(2)}) collective-permute-start(bf16[32,3072]{1,0:T(8,128)(2,1)S(1)} %bitcast.13), channel_id=1, source_target_pairs={{0,2},{1,3},{2,4},{3,5},{4,6},{5,7},{6,0},{7,1},{8,10},{9,11},{10,... | collective-permute-start | bytes 589832 | tf_op jit(solution)/shard_map/ppermute | solution.py:395
  13.9 8.7 %collective-permute-start.3 = (bf16[32,3072]{1,0:T(8,128)(2,1)S(1)}, bf16[32,3072]{1,0:T(8,128)(2,1)S(1)}, u32[]{:S(2)}, u32[]{:S(2)}) collective-permute-start(bf16[32,3072]{1,0:T(8,128)(2,1)S(1)} %collective-permute-done.2.refs_1_), channel_id=1, source_target_pairs={{0,2},{1,3},{2,4},{3,5},{4,6},{5,7},{6,0},{7,1},{8,10},{9,11},{10,... | collective-permute-start | bytes 589832 | tf_op jit(solution)/shard_map/ppermute | solution.py:395
  13.9 9.5 %collective-permute-start.4 = (bf16[32,3072]{1,0:T(8,128)(2,1)S(1)}, bf16[32,3072]{1,0:T(8,128)(2,1)S(1)}, u32[]{:S(2)}, u32[]{:S(2)}) collective-permute-start(bf16[32,3072]{1,0:T(8,128)(2,1)S(1)} %collective-permute-done.2.refs_1_), channel_id=1, source_target_pairs={{0,1},{1,0},{2,3},{3,2},{4,5},{5,4},{6,7},{7,6},{8,9},{9,8},{10,11... | collective-permute-start | bytes 589832 | tf_op jit(solution)/shard_map/ppermute | solution.py:401
  22.6 8.3 %collective-permute-start.6 = (bf16[64,3072]{1,0:T(8,128)(2,1)S(1)}, bf16[64,3072]{1,0:T(8,128)(2,1)S(1)}, u32[]{:S(2)}, u32[]{:S(2)}) collective-permute-start(bf16[64,3072]{1,0:T(8,128)(2,1)S(1)} %shard_map.74), channel_id=1, source_target_pairs={{2,0},{3,1},{4,2},{5,3},{6,4},{7,5},{0,6},{1,7},{10,8},{11,9},{12,... | collective-permute-start | bytes 1179656 | tf_op jit(solution)/shard_map/ppermute | solution.py:398
  22.6 6.8 %collective-permute-start.5 = (bf16[32,3072]{1,0:T(8,128)(2,1)S(1)}, bf16[32,3072]{1,0:T(8,128)(2,1)S(1)}, u32[]{:S(2)}, u32[]{:S(2)}) collective-permute-start(bf16[32,3072]{1,0:T(8,128)(2,1)S(1)} %collective-permute-done.3.refs_2_), channel_id=1, source_target_pairs={{0,1},{1,0},{2,3},{3,2},{4,5},{5,4},{6,7},{7,6},{8,9},{9,8},{10,11... | collective-permute-start | bytes 589832 | tf_op jit(solution)/shard_map/ppermute | solution.py:401
  29.3 6.4 %collective-permute-start.7 = (bf16[160,1536]{1,0:T(8,128)(2,1)S(1)}, bf16[160,1536]{1,0:T(8,128)(2,1)S(1)}, u32[]{:S(2)}, u32[]{:S(2)}) collective-permute-start(bf16[160,1536]{1,0:T(8,128)(2,1)S(1)} %get-tuple-element.45), channel_id=1, source_target_pairs={{0,8},{8,0},{1,9},{9,1},{2,10},{10,2},{3,11},{11,3},{4,12},{12,4},... | collective-permute-start | bytes 1474568 | tf_op jit(solution)/shard_map/ppermute | solution.py:502
  33.3 2.5 %collective-permute-start.8 = (bf16[96,1536]{1,0:T(8,128)(2,1)S(1)}, bf16[96,1536]{1,0:T(8,128)(2,1)S(1)}, u32[]{:S(2)}, u32[]{:S(2)}) collective-permute-start(bf16[96,1536]{1,0:T(8,128)(2,1)S(1)} %get-tuple-element.46), channel_id=1, source_target_pairs={{0,8},{8,0},{1,9},{9,1},{2,10},{10,2},{3,11},{11,3},{4,12},{12,4},... | collective-permute-start | bytes 884744 | tf_op jit(solution)/shard_map/ppermute | solution.py:505
  33.4 2.4 %copy-start = (f32[3,3,3072]{2,1,0:T(4,128)S(1)}, f32[3,3,3072]{2,1,0:T(4,128)}, u32[]{:S(2)}) copy-start(f32[3,3,3072]{2,1,0:T(4,128)} %refs_5_.1) | copy-start | bytes 331780
  33.4 2.4 %copy-start.2 = (f32[3072]{0:T(1024)S(1)}, f32[3072]{0:T(1024)}, u32[]{:S(2)}) copy-start(f32[3072]{0:T(1024)} %param.9) | copy-start | bytes 36868
  33.4 2.4 %copy-start.3 = (f32[3072]{0:T(1024)S(1)}, f32[3072]{0:T(1024)}, u32[]{:S(2)}) copy-start(f32[3072]{0:T(1024)} %param.11) | copy-start | bytes 36868
  40.2 4.9 %collective-permute-start.9 = (bf16[256,1536]{1,0:T(8,128)(2,1)S(1)}, bf16[256,1536]{1,0:T(8,128)(2,1)S(1)}, u32[]{:S(2)}, u32[]{:S(2)}) collective-permute-start(bf16[256,1536]{1,0:T(8,128)(2,1)S(1)} %get-tuple-element.47.mixed_ref), channel_id=1, source_target_pairs={{0,8},{8,0},{1,9},{9,1},{2,10},{10,2},{3,11},{11,3},{4,12},{12,4},... | collective-permute-start | bytes 2359304 | tf_op jit(solution)/shard_map/ppermute | solution.py:520
  47.0 23.3 %copy-start.1 = (f32[6144]{0:T(1024)S(1)}, f32[6144]{0:T(1024)}, u32[]{:S(2)}) copy-start(f32[6144]{0:T(1024)} %param.13) | copy-start | bytes 73732
  47.0 7.8 %collective-permute-start.12 = (bf16[32,3072]{1,0:T(8,128)(2,1)S(1)}, bf16[32,3072]{1,0:T(8,128)(2,1)S(1)}, u32[]{:S(2)}, u32[]{:S(2)}) collective-permute-start(bf16[32,3072]{1,0:T(8,128)(2,1)S(1)} %get-tuple-element.58), channel_id=1, source_target_pairs={{0,1},{1,0},{2,3},{3,2},{4,5},{5,4},{6,7},{7,6},{8,9},{9,8},{10,11... | collective-permute-start | bytes 589832 | tf_op jit(solution)/shard_map/ppermute | solution.py:401
  50.0 8.7 %collective-permute-start.10 = (bf16[32,3072]{1,0:T(8,128)(2,1)S(1)}, bf16[32,3072]{1,0:T(8,128)(2,1)S(1)}, u32[]{:S(2)}, u32[]{:S(2)}) collective-permute-start(bf16[32,3072]{1,0:T(8,128)(2,1)S(1)} %get-tuple-element.55), channel_id=1, source_target_pairs={{0,1},{1,0},{2,3},{3,2},{4,5},{5,4},{6,7},{7,6},{8,9},{9,8},{10,11... | collective-permute-start | bytes 589832 | tf_op jit(solution)/shard_map/ppermute | solution.py:401
  54.9 9.1 %collective-permute-start.13 = (bf16[32,3072]{1,0:T(8,128)(2,1)S(1)}, bf16[32,3072]{1,0:T(8,128)(2,1)S(1)}, u32[]{:S(2)}, u32[]{:S(2)}) collective-permute-start(bf16[32,3072]{1,0:T(8,128)(2,1)S(1)} %add_convert_fusion.1), channel_id=1, source_target_pairs={{2,0},{3,1},{4,2},{5,3},{6,4},{7,5},{0,6},{1,7},{10,8},{11,9},{12,... | collective-permute-start | bytes 589832 | tf_op jit(solution)/shard_map/ppermute | solution.py:398
  56.9 7.1 %collective-permute-start.14 = (bf16[32,3072]{1,0:T(8,128)(2,1)S(1)}, bf16[32,3072]{1,0:T(8,128)(2,1)S(1)}, u32[]{:S(2)}, u32[]{:S(2)}) collective-permute-start(bf16[32,3072]{1,0:T(8,128)(2,1)S(1)} %get-tuple-element.60), channel_id=1, source_target_pairs={{0,1},{1,0},{2,3},{3,2},{4,5},{5,4},{6,7},{7,6},{8,9},{9,8},{10,11... | collective-permute-start | bytes 589832 | tf_op jit(solution)/shard_map/ppermute | solution.py:401
  58.7 9.3 %collective-permute-start.11 = (bf16[32,3072]{1,0:T(8,128)(2,1)S(1)}, bf16[32,3072]{1,0:T(8,128)(2,1)S(1)}, u32[]{:S(2)}, u32[]{:S(2)}) collective-permute-start(bf16[32,3072]{1,0:T(8,128)(2,1)S(1)} %add_convert_fusion.2), channel_id=1, source_target_pairs={{0,2},{1,3},{2,4},{3,5},{4,6},{5,7},{6,0},{7,1},{8,10},{9,11},{10,... | collective-permute-start | bytes 589832 | tf_op jit(solution)/shard_map/ppermute | solution.py:395
  59.6 7.2 %collective-permute-start.16 = (bf16[32,3072]{1,0:T(8,128)(2,1)S(1)}, bf16[32,3072]{1,0:T(8,128)(2,1)S(1)}, u32[]{:S(2)}, u32[]{:S(2)}) collective-permute-start(bf16[32,3072]{1,0:T(8,128)(2,1)S(1)} %get-tuple-element.62), channel_id=1, source_target_pairs={{0,1},{1,0},{2,3},{3,2},{4,5},{5,4},{6,7},{7,6},{8,9},{9,8},{10,11... | collective-permute-start | bytes 589832 | tf_op jit(solution)/shard_map/ppermute | solution.py:401
  64.1 6.2 %collective-permute-start.15 = (bf16[32,3072]{1,0:T(8,128)(2,1)S(1)}, bf16[32,3072]{1,0:T(8,128)(2,1)S(1)}, u32[]{:S(2)}, u32[]{:S(2)}) collective-permute-start(bf16[32,3072]{1,0:T(8,128)(2,1)S(1)} %add_convert_fusion), channel_id=1, source_target_pairs={{2,0},{3,1},{4,2},{5,3},{6,4},{7,5},{0,6},{1,7},{10,8},{11,9},{12,... | collective-permute-start | bytes 589832 | tf_op jit(solution)/shard_map/ppermute | solution.py:398
  70.9 1.4 %collective-permute-start.17 = (bf16[1,16,3072]{2,1,0:T(8,128)(2,1)S(1)}, bf16[1,16,3072]{2,1,0:T(8,128)(2,1)S(1)}, u32[]{:S(2)}, u32[]{:S(2)}) collective-permute-start(bf16[1,16,3072]{2,1,0:T(8,128)(2,1)S(1)} %get-tuple-element.64), channel_id=1, source_target_pairs={{0,8},{8,0},{1,9},{9,1},{2,10},{10,2},{3,11},{11,3},{4,12},{12,4},... | collective-permute-start | bytes 294920 | tf_op jit(solution)/shard_map/ppermute | solution.py:533

commit v5 on v4

--- a/solution.py
+++ b/solution.py
@@ -11,6 +11,7 @@
 HBM = pl.BlockSpec(memory_space=pltpu.HBM)
 SMEM = pl.BlockSpec(memory_space=pltpu.SMEM)
 MIB = 1 << 20
+LIMITS = (24, 20, 36, 26)
 
 
 def tile_of(size, most):
@@ -37,6 +38,23 @@
         )
         for part in range(parts)
     ]
+
+
+def passengers(later, spans):
+    shapes = [pltpu.VMEM((count, later.shape[1]), later.dtype) for _, _, count in spans]
+    scratch = [pltpu.SemaphoreType.DMA((2,)) for _ in spans]
+    units = later.shape[0] // 2
+
+    def start(core, later_ref, out_refs, sem_refs):
+        copies = []
+        for (whose, first, _), out_ref, sems in zip(spans, out_refs, sem_refs):
+            side = core if whose == 0 else 1 - core
+            copies += row_copies(later_ref, pl.multiple_of(side * units + first, 16), out_ref, sems)
+        for copy in copies:
+            copy.start()
+        return copies
+
+    return shapes, scratch, start
 
 
 def fetch(info, weight, start, count, held, parts=4):
@@ -175,48 +193,61 @@
     tiles(*out_ref.shape, 768, body)
 
 
-def up_other(info, slots, upper, lower):
+def up_other(info, slots, upper, lower, later, spans):
     depth = slots[0].shape[1]
     total = sum(slot.shape[0] for slot in slots)
     width = upper.shape[1] // 2
+    shapes, scratch, start = passengers(later, spans)
 
     def kernel(info_ref, *refs):
-        upper_ref, lower_ref, out_ref, tokens_ref = refs[len(slots) :]
+        upper_ref, lower_ref, later_ref, out_ref, tokens_ref = refs[len(slots) : len(slots) + 5]
+        rest = refs[len(slots) + 5 :]
+        copies = start(info_ref[0], later_ref, rest[: len(spans)], rest[len(spans) :])
         gathered_rows(refs[: len(slots)], tokens_ref)
         product_tiles(tokens_ref, upper_ref, lower_ref, (1 - info_ref[0]) * width, out_ref)
-
-    return pl.pallas_call(
-        kernel,
-        out_shape=(pltpu.VMEM((total, width), BF16), pltpu.VMEM((total, depth), BF16)),
-        in_specs=[SMEM] + [VMEM] * (len(slots) + 2),
-        out_specs=(VMEM, VMEM),
+        for copy in copies:
+            copy.wait()
+
+    out, gathered, *pieces = pl.pallas_call(
+        kernel,
+        out_shape=(pltpu.VMEM((total, width), BF16), pltpu.VMEM((total, depth), BF16), *shapes),
+        in_specs=[SMEM] + [VMEM] * (len(slots) + 2) + [HBM],
+        out_specs=(VMEM,) * (2 + len(spans)),
+        scratch_shapes=scratch,
         cost_estimate=cost(2 * total * depth * width, 2 * depth * width),
-        compiler_params=params(10),
-    )(info, *slots, upper, lower)
-
-
-def up_own(info, tokens, upper, lower):
+        compiler_params=params(LIMITS[0]),
+    )(info, *slots, upper, lower, later)
+    return out, gathered, pieces
+
+
+def up_own(info, tokens, upper, lower, later, spans):
     total, depth = tokens.shape
     width = upper.shape[1] // 2
-
-    def kernel(info_ref, tokens_ref, upper_ref, lower_ref, out_ref):
+    shapes, scratch, start = passengers(later, spans)
+
+    def kernel(info_ref, tokens_ref, upper_ref, lower_ref, later_ref, out_ref, *rest):
+        copies = start(info_ref[0], later_ref, rest[: len(spans)], rest[len(spans) :])
         product_tiles(tokens_ref, upper_ref, lower_ref, info_ref[0] * width, out_ref)
-
-    return pl.pallas_call(
-        kernel,
-        out_shape=pltpu.VMEM((total, width), F32),
-        in_specs=[SMEM] + [VMEM] * 3,
-        out_specs=VMEM,
+        for copy in copies:
+            copy.wait()
+
+    out, *pieces = pl.pallas_call(
+        kernel,
+        out_shape=(pltpu.VMEM((total, width), F32), *shapes),
+        in_specs=[SMEM] + [VMEM] * 3 + [HBM],
+        out_specs=(VMEM,) * (1 + len(spans)),
+        scratch_shapes=scratch,
         cost_estimate=cost(2 * total * depth * width, 2 * depth * width),
-        compiler_params=params(10),
-    )(info, tokens, upper, lower)
+        compiler_params=params(LIMITS[1]),
+    )(info, tokens, upper, lower, later)
+    return out, pieces
 
 
 def gelu(value):
     return 0.5 * value * (1.0 + lax.erf(value * 0.7071067811865476))
 
 
-def conv(info, own, received, up_bias, conv_weight, conv_bias, later, groups, links, rows, grid_y):
+def conv(info, own, received, up_bias, conv_weight, conv_bias, later, spans, groups, links, rows, grid_y):
     width = own[0].shape[1]
     slots = [(group, index) + slot for group, members in enumerate(groups) for index, slot in enumerate(members)]
     blocks = len(slots)
@@ -225,12 +256,14 @@
     lanes = 128
     extent_x = total // grid_y
 
+    shapes, scratch, start_copies = passengers(later, spans)
+
     def kernel(info_ref, *refs):
         own_refs, received_refs = refs[:count], refs[count : 2 * count]
-        up_bias_ref, weight_ref, bias_ref, later_ref, out_ref, later_out, hidden, sems = refs[2 * count :]
-        copies = row_copies(later_ref, pl.multiple_of(info_ref[0] * width, 16), later_out, sems)
-        for copy in copies:
-            copy.start()
+        up_bias_ref, weight_ref, bias_ref, later_ref, out_ref = refs[2 * count : 2 * count + 5]
+        rest = refs[2 * count + 5 :]
+        hidden = rest[len(spans)]
+        copies = start_copies(info_ref[0], later_ref, rest[: len(spans)], rest[len(spans) + 1 :])
         hidden[0:grid_y, :] = jnp.zeros((grid_y, lanes), F32)
         hidden[(extent_x + 1) * grid_y : (extent_x + 2) * grid_y, :] = jnp.zeros((grid_y, lanes), F32)
         at_y = lax.broadcasted_iota(jnp.int32, (grid_y, lanes), 0)
@@ -268,78 +301,82 @@
         for copy in copies:
             copy.wait()
 
-    return pl.pallas_call(
-        kernel,
-        out_shape=(pltpu.VMEM((total, width), BF16), pltpu.VMEM((width, later.shape[1]), BF16)),
+    mixed, *pieces = pl.pallas_call(
+        kernel,
+        out_shape=(pltpu.VMEM((total, width), BF16), *shapes),
         in_specs=[SMEM] + [VMEM] * (2 * count + 3) + [HBM],
-        out_specs=(VMEM, VMEM),
-        scratch_shapes=[pltpu.VMEM(((extent_x + 2) * grid_y, lanes), F32), pltpu.SemaphoreType.DMA((4,))],
+        out_specs=(VMEM,) * (1 + len(spans)),
+        scratch_shapes=[pltpu.VMEM(((extent_x + 2) * grid_y, lanes), F32), *scratch],
         cost_estimate=cost(60 * total * width, 8 * total * width),
-        compiler_params=params(33),
+        compiler_params=params(LIMITS[2]),
     )(info, *own, *received, up_bias, conv_weight, conv_bias, later)
-
-
-def down_own(info, mixed, weight, later):
+    return mixed, pieces
+
+
+def dot_pieces(left_ref, down, piece_refs, across):
+    value, start = None, 0
+    for ref in piece_refs:
+        deep = slice(start, start + ref.shape[0])
+        term = jnp.dot(left_ref[down, deep], ref[:, across], preferred_element_type=F32)
+        value = term if value is None else value + term
+        start = deep.stop
+    return value
+
+
+def down_own(info, mixed, mine, later, spans):
     total, depth = mixed.shape
-    width = weight.shape[1]
-    tile = tile_of(width, 1024)
-    high = tile_of(total, 256)
-
-    def kernel(info_ref, mixed_ref, weight_ref, later_ref, out_ref, later_out, sems):
-        copies = row_copies(later_ref, pl.multiple_of((1 - info_ref[0]) * depth, 16), later_out, sems)
-        for copy in copies:
-            copy.start()
-
-        def body(step, carry):
-            row, col = step // (width // tile), step % (width // tile)
-            down = pl.ds(pl.multiple_of(row * high, high), high)
-            across = pl.ds(pl.multiple_of(col * tile, tile), tile)
-            out_ref[down, across] = jnp.dot(mixed_ref[down, :], weight_ref[:, across], preferred_element_type=F32)
-            return carry
-
-        lax.fori_loop(0, (total // high) * (width // tile), body, 0)
+    width = later.shape[1]
+    shapes, scratch, start = passengers(later, spans)
+
+    def kernel(info_ref, mixed_ref, *refs):
+        later_ref, out_ref = refs[len(mine) : len(mine) + 2]
+        rest = refs[len(mine) + 2 :]
+        copies = start(info_ref[0], later_ref, rest[: len(spans)], rest[len(spans) :])
+
+        def body(down, col, tile):
+            out_ref[down, pl.ds(col, tile)] = dot_pieces(mixed_ref, down, refs[: len(mine)], pl.ds(col, tile))
+
+        tiles(total, width, 1024, body)
         for copy in copies:
             copy.wait()
 
-    return pl.pallas_call(
-        kernel,
-        out_shape=(pltpu.VMEM((total, width), F32), pltpu.VMEM((depth, width), BF16)),
-        in_specs=[SMEM] + [VMEM] * 2 + [HBM],
-        out_specs=(VMEM, VMEM),
-        scratch_shapes=[pltpu.SemaphoreType.DMA((4,))],
+    out, *pieces = pl.pallas_call(
+        kernel,
+        out_shape=(pltpu.VMEM((total, width), F32), *shapes),
+        in_specs=[SMEM] + [VMEM] * (1 + len(mine)) + [HBM],
+        out_specs=(VMEM,) * (1 + len(spans)),
+        scratch_shapes=scratch,
         cost_estimate=cost(2 * total * depth * width, 2 * depth * width),
-        compiler_params=params(26),
-    )(info, mixed, weight, later)
-
-
-def down_other(mixed, weight, partial, first, outs):
+        compiler_params=params(LIMITS[3]),
+    )(info, mixed, *mine, later)
+    return out, pieces
+
+
+def down_other(mixed, theirs, partial, first, outs):
     depth = mixed.shape[1]
-    width = weight.shape[1]
+    width = partial.shape[1]
     total = sum(rows for rows, _ in outs)
     tile = tile_of(width, 1024)
 
-    def kernel(mixed_ref, weight_ref, partial_ref, *out_refs):
+    runs, start = [], 0
+    for index, (rows, _) in enumerate(outs):
+        if not runs or runs[-1][1] + rows > 256:
+            runs.append([start, 0, []])
+        runs[-1][2].append((index, runs[-1][1], rows))
+        runs[-1][1] += rows
+        start += rows
+
+    def kernel(mixed_ref, *refs):
+        partial_ref, out_refs = refs[len(theirs)], refs[len(theirs) + 1 :]
+
         def body(step, carry):
             across = pl.ds(pl.multiple_of(step * tile, tile), tile)
-            start = 0
-            pieces = []
-            for out_ref in out_refs:
-                rows = out_ref.shape[0]
-                pieces.append((out_ref, start, rows))
-                start += rows
-            while pieces:
-                take = 1
-                while take < len(pieces) and sum(rows for _, _, rows in pieces[: take + 1]) <= 256:
-                    take += 1
-                low = pieces[0][1]
-                high = sum(rows for _, _, rows in pieces[:take])
+            for low, high, members in runs:
                 down = slice(first + low, first + low + high)
-                value = partial_ref[down, across] + jnp.dot(
-                    mixed_ref[down, :], weight_ref[:, across], preferred_element_type=F32
-                )
-                for out_ref, at, rows in pieces[:take]:
-                    out_ref[:, across] = value[at - low : at - low + rows].astype(out_ref.dtype)
-                pieces = pieces[take:]
+                value = partial_ref[down, across] + dot_pieces(mixed_ref, down, refs[: len(theirs)], across)
+                for index, at, rows in members:
+                    out_ref = out_refs[index]
+                    out_ref[:, across] = value[at : at + rows].astype(out_ref.dtype)
             return carry
 
         lax.fori_loop(0, width // tile, body, 0)
@@ -347,11 +384,11 @@
     return pl.pallas_call(
         kernel,
         out_shape=tuple(pltpu.VMEM((rows, width), kind) for rows, kind in outs),
-        in_specs=[VMEM] * 3,
+        in_specs=[VMEM] * (2 + len(theirs)),
         out_specs=(VMEM,) * len(outs),
         cost_estimate=cost(2 * total * depth * width, 2 * depth * width),
         compiler_params=params(10),
-    )(mixed, weight, partial)
+    )(mixed, *theirs, partial)
 
 
 def finish(info, totals, bias, cols, grid_half):
@@ -499,12 +536,13 @@
     early, late, groups, upper = gather(links, block, lambda: fetch(info, up_weight, lambda c: 0 * c, part, 0))
 
     early_other, early_own, lower = up_early(info, early, upper, up_weight)
-    own, received = [early_own], [lax.ppermute(early_other, "sp", swap)]
-    if late:
-        late_other, late_tokens = up_other(info, late, upper, lower)
-        received.append(lax.ppermute(late_other, "sp", swap))
-        own.append(up_own(info, late_tokens, upper, lower))
-    mixed, down_mine = conv(
+    third = units_half // 3 // 32 * 32
+    rest = units_half - 2 * third
+    late_other, late_tokens, mine_a = up_other(info, late, upper, lower, down_weight, [(0, 0, third)])
+    late_own, mine_b = up_own(info, late_tokens, upper, lower, down_weight, [(0, third, third)])
+    own = [early_own, late_own]
+    received = [lax.ppermute(early_other, "sp", swap), lax.ppermute(late_other, "sp", swap)]
+    mixed, (mine_c, theirs_a) = conv(
         info,
         own,
         received,
@@ -512,21 +550,25 @@
         conv_weight,
         conv_bias.reshape(1, units),
         down_weight,
+        [(0, 2 * third, rest), (1, 0, third)],
         groups,
         links,
         rows,
         grid_y,
     )
     mixed_received = lax.ppermute(mixed, "sp", swap)
-    product, down_theirs = down_own(info, mixed, down_mine, down_weight)
+    product, theirs_b = down_own(
+        info, mixed, [*mine_a, *mine_b, mine_c], down_weight, [(1, third, units_half - third)]
+    )
+    theirs = [theirs_a, *theirs_b]
 
     early_rows = rows * len(groups[0])
     total = scatter(
         links,
         rows,
         groups,
-        lambda outs: down_other(mixed_received, down_theirs, product, early_rows, outs),
-        lambda outs: down_other(mixed_received, down_theirs, product, 0, outs),
+        lambda outs: down_other(mixed_received, theirs, product, early_rows, outs),
+        lambda outs: down_other(mixed_received, theirs, product, 0, outs),
     )
 
     stay, leave = finish(info, [total], down_bias.reshape(1, width_model), cols, grid_half)

time: 73.1 us -> 71.5 us (0.978)
  waiting for transfers between devices: 26.5 us -> 24.5 us
  starting transfers between devices: 16 us -> 17.8 us
  Pallas kernels: 28.3 us -> 26.7 us
    ppermute x3, waiting for transfers between devices: 12 us -> 8.36 us  [up(): return lax.ppermute(value, 'tp', self.upward)]
    ppermute x3, starting transfers between devices: 2.45 us -> 4.16 us  [up(): return lax.ppermute(value, 'tp', self.upward)]
    pallas_call x3, Pallas kernels: 11 us -> 9.38 us  [the longest x1 3.52 us: down_own(): pl.pallas_call(kernel, out_shape=(pltpu.VMEM((total, width), F32), *shape...]
    ppermute x3, waiting for transfers between devices: 3.64 us -> 5 us  [down(): return lax.ppermute(value, 'tp', self.downward)]
  transfers between devices with their start and end apart: 18 -> 18, of which waited for: 11 -> 10; matrix products, arithmetic and copies ran while one was open for 0% -> 0% of each run, Pallas kernels for 29% -> 29%
where the time goes in v5:
time: 71.5 us; the launch traced here: 71.4 us
  Pallas kernels  26.7 us (37%)
  waiting for transfers between devices  24.5 us (34%)
  starting transfers between devices  17.8 us (25%)
  other arithmetic  1.1 us (2%)
  local copies, waits for them, and re-layouts  0.98 us (1%)
    ppermute x7, waiting for transfers between devices, cross(): return lax.ppermute(value, 'tp', self.pairs)  9.01 us
    ppermute x3, waiting for transfers between devices, up(): return lax.ppermute(value, 'tp', self.upward)  8.36 us
    ppermute x7, starting transfers between devices, cross(): return lax.ppermute(value, 'tp', self.pairs)  8.3 us
    pallas_call x1, Pallas kernels, up_early(): pl.pallas_call(kernel, out_shape=(pltpu.VMEM((total, width), BF16), pltpu...  5.93 us
    ppermute x3, waiting for transfers between devices, down(): return lax.ppermute(value, 'tp', self.downward)  5 us
    pallas_call x1, Pallas kernels, fetch(): pl.pallas_call(kernel, out_shape=pltpu.VMEM((count, weight.shape[1]), wei...  4.34 us
    ppermute x3, starting transfers between devices, up(): return lax.ppermute(value, 'tp', self.upward)  4.16 us
    ppermute x3, starting transfers between devices, down(): return lax.ppermute(value, 'tp', self.downward)  4.12 us
  transfers between devices with their start and end apart: 18, of which 10 were waited for; matrix products, arithmetic and copies ran while one was open for 0% of the time, Pallas kernels for 29%

profile of v5, /device:TPU:0, one launch (start us, length us, event | category | flops | bytes accessed | tf_op | source)
XLA Modules:
  0.0 71.4 jit_solution(16020479977540201284)
XLA Ops:
  2.4 3.0 %collective-permute-start.2 = (bf16[32,3072]{1,0:T(8,128)(2,1)S(1)}, bf16[32,3072]{1,0:T(8,128)(2,1)S(1)}, u32[]{:S(2)}, u32[]{:S(2)}) collective-permute-start(bf16[32,3072]{1,0:T(8,128)(2,1)S(1)} %bitcast.12), channel_id=1, source_target_pairs={{0,2},{1,3},{2,4},{3,5},{4,6},{5,7},{6,0},{7,1},{8,10},{9,11},{10,... | collective-permute-start | bytes 589832 | tf_op jit(solution)/shard_map/ppermute | solution.py:432
  5.4 1.5 %collective-permute-start.1 = (bf16[32,3072]{1,0:T(8,128)(2,1)S(1)}, bf16[32,3072]{1,0:T(8,128)(2,1)S(1)}, u32[]{:S(2)}, u32[]{:S(2)}) collective-permute-start(bf16[32,3072]{1,0:T(8,128)(2,1)S(1)} %bitcast.13), channel_id=1, source_target_pairs={{0,1},{1,0},{2,3},{3,2},{4,5},{5,4},{6,7},{7,6},{8,9},{9,8},{10,11... | collective-permute-start | bytes 589832 | tf_op jit(solution)/shard_map/ppermute | solution.py:438
  6.9 4.3 %shard_map.73.refs_5_.refs_2_.upper_ref = bf16[1536,3072]{1,0:T(8,128)(2,1)S(1)} custom-call(s32[3]{0:T(128)S(1)} %pad_add_fusion.info_ref, bf16[3072,3072]{1,0:T(8,128)(2,1)} %refs_6_.1), custom_call_target="tpu_custom_call" | custom-call | bytes 18874368 | tf_op jit(solution)/shard_map/pallas_call | solution.py:71
  11.3 1.4 %collective-permute-done.2.refs_1_ = bf16[32,3072]{1,0:T(8,128)(2,1)S(1)} collective-permute-done((bf16[32,3072]{1,0:T(8,128)(2,1)S(1)}, bf16[32,3072]{1,0:T(8,128)(2,1)S(1)}, u32[]{:S(2)}, u32[]{:S(2)}) %collective-permute-start.2) | collective-permute-done | bytes 196640 | tf_op jit(solution)/shard_map/ppermute | solution.py:432
  13.7 1.5 %collective-permute-start.4 = (bf16[32,3072]{1,0:T(8,128)(2,1)S(1)}, bf16[32,3072]{1,0:T(8,128)(2,1)S(1)}, u32[]{:S(2)}, u32[]{:S(2)}) collective-permute-start(bf16[32,3072]{1,0:T(8,128)(2,1)S(1)} %collective-permute-done.2.refs_1_), channel_id=1, source_target_pairs={{0,1},{1,0},{2,3},{3,2},{4,5},{5,4},{6,7},{7,6},{8,9},{9,8},{10,11... | collective-permute-start | bytes 589832 | tf_op jit(solution)/shard_map/ppermute | solution.py:438
  15.2 5.9 %collective-permute-done.3.refs_2_ = bf16[32,3072]{1,0:T(8,128)(2,1)S(1)} collective-permute-done((bf16[32,3072]{1,0:T(8,128)(2,1)S(1)}, bf16[32,3072]{1,0:T(8,128)(2,1)S(1)}, u32[]{:S(2)}, u32[]{:S(2)}) %collective-permute-start.3) | collective-permute-done | bytes 196640 | tf_op jit(solution)/shard_map/ppermute | solution.py:432
  21.2 1.1 %collective-permute-start.5 = (bf16[32,3072]{1,0:T(8,128)(2,1)S(1)}, bf16[32,3072]{1,0:T(8,128)(2,1)S(1)}, u32[]{:S(2)}, u32[]{:S(2)}) collective-permute-start(bf16[32,3072]{1,0:T(8,128)(2,1)S(1)} %collective-permute-done.3.refs_2_), channel_id=1, source_target_pairs={{0,1},{1,0},{2,3},{3,2},{4,5},{5,4},{6,7},{7,6},{8,9},{9,8},{10,11... | collective-permute-start | bytes 589832 | tf_op jit(solution)/shard_map/ppermute | solution.py:438
  22.3 5.9 %shard_map.75 = (bf16[160,1536]{1,0:T(8,128)(2,1)S(1)}, f32[160,1536]{1,0:T(8,128)S(1)}, bf16[1536,3072]{1,0:T(8,128)(2,1)S(1)}) custom-call(s32[3]{0:T(128)S(1)} %pad_add_fusion.info_ref, bf16[32,3072]{1,0:T(8,128)(2,1)S(1)} %bitcast.15, bf16[32,3072]{1,0:T(8,128)(2,1)S(1)} %collective-permute-done.2.refs_1_, ...), custom_call_target="tpu_custom_call" | custom-call | flops 3019898880 | bytes 9437184 | tf_op jit(solution)/shard_map/pallas_call | solution.py:148
  28.3 2.3 %collective-permute-done.6.refs_1_ = bf16[64,3072]{1,0:T(8,128)(2,1)S(1)} collective-permute-done((bf16[64,3072]{1,0:T(8,128)(2,1)S(1)}, bf16[64,3072]{1,0:T(8,128)(2,1)S(1)}, u32[]{:S(2)}, u32[]{:S(2)}) %collective-permute-start.6) | collective-permute-done | bytes 393248 | tf_op jit(solution)/shard_map/ppermute | solution.py:435
  30.7 2.4 %shard_map.76 = (bf16[96,1536]{1,0:T(8,128)(2,1)S(1)}, bf16[96,3072]{1,0:T(8,128)(2,1)S(1)}, bf16[512,3072]{1,0:T(8,128)(2,1)S(1)}) custom-call(s32[3]{0:T(128)S(1)} %pad_add_fusion.info_ref, bf16[32,3072]{1,0:T(8,128)(2,1)S(1)} %collective-permute-done.5.refs_0_, bf16[64,3072]{1,0:T(8,128)(2,1)S(1)} %collective-permute-done.6.refs_1_, ...), custom_call_target="tpu_custom_call" | custom-call | flops 905969664 | bytes 9437184 | tf_op jit(solution)/shard_map/pallas_call | solution.py:211
  33.3 2.4 %shard_map.77 = (f32[96,1536]{1,0:T(8,128)S(1)}, bf16[512,3072]{1,0:T(8,128)(2,1)S(1)}) custom-call(s32[3]{0:T(128)S(1)} %pad_add_fusion.info_ref, bf16[96,3072]{1,0:T(8,128)(2,1)S(1)} %get-tuple-element.48.tokens_ref, bf16[1536,3072]{1,0:T(8,128)(2,1)S(1)} %shard_map.73.refs_5_.refs_2_.upper_ref, ...), custom_call_target="tpu_custom_call" | custom-call | flops 905969664 | bytes 9437184 | tf_op jit(solution)/shard_map/pallas_call | solution.py:234
  35.8 3.4 %shard_map.78 = (bf16[256,1536]{1,0:T(8,128)(2,1)S(1)}, bf16[512,3072]{1,0:T(8,128)(2,1)S(1)}, bf16[512,3072]{1,0:T(8,128)(2,1)S(1)}) custom-call(s32[3]{0:T(128)S(1)} %pad_add_fusion.info_ref, f32[160,1536]{1,0:T(8,128)S(1)} %get-tuple-element.45.refs_0_, f32[96,1536]{1,0:T(8,128)S(1)} %get-tuple-element.49.refs_1_, ...), custom_call_target="tpu_custom_call" | custom-call | flops 23592960 | bytes 3145728 | tf_op jit(solution)/shard_map/pallas_call | solution.py:304
  39.7 3.5 %shard_map.79 = (f32[256,3072]{1,0:T(8,128)S(1)}, bf16[1024,3072]{1,0:T(8,128)(2,1)S(1)}) custom-call(s32[3]{0:T(128)S(1)} %pad_add_fusion.info_ref, bf16[256,1536]{1,0:T(8,128)(2,1)S(1)} %get-tuple-element.52.mixed_ref, bf16[512,3072]{1,0:T(8,128)(2,1)S(1)} %get-tuple-element.54.refs_0_, bf16[512,3072]{1,0:T(8,128)(2,1)S(1)} %get-tuple-element.55.refs_1_, ...), custom_call_target="tpu_custom_call" | custom-call | flops 2415919104 | bytes 9437184 | tf_op jit(solution)/shard_map/pallas_call | solution.py:343
  43.2 1.9 %shard_map.80 = (bf16[32,3072]{1,0:T(8,128)(2,1)S(1)}, f32[32,3072]{1,0:T(8,128)S(1)}, bf16[32,3072]{1,0:T(8,128)(2,1)S(1)}) custom-call(bf16[256,1536]{1,0:T(8,128)(2,1)S(1)} %collective-permute-done.9.mixed_ref, bf16[512,3072]{1,0:T(8,128)(2,1)S(1)} %get-tuple-element.53.refs_0_, bf16[1024,3072]{1,0:T(8,128)(2,1)S(1)} %get-tuple-element.57.refs_1_, ...), custom_call_target="tpu_custom_call" | custom-call | flops 905969664 | bytes 9437184 | tf_op jit(solution)/shard_map/pallas_call | solution.py:384
  45.2 1.1 %collective-permute-start.12 = (bf16[32,3072]{1,0:T(8,128)(2,1)S(1)}, bf16[32,3072]{1,0:T(8,128)(2,1)S(1)}, u32[]{:S(2)}, u32[]{:S(2)}) collective-permute-start(bf16[32,3072]{1,0:T(8,128)(2,1)S(1)} %get-tuple-element.66), channel_id=1, source_target_pairs={{0,1},{1,0},{2,3},{3,2},{4,5},{5,4},{6,7},{7,6},{8,9},{9,8},{10,11... | collective-permute-start | bytes 589832 | tf_op jit(solution)/shard_map/ppermute | solution.py:438
  46.3 2.1 %shard_map.81 = (f32[32,3072]{1,0:T(8,128)S(1)}, f32[32,3072]{1,0:T(8,128)S(1)}, f32[32,3072]{1,0:T(8,128)S(1)}, bf16[32,3072]{1,0:T(8,128)(2,1)S(1)}, bf16[32,3072]{1,0:T(8,128)(2,1)S(1)}) custom-call(bf16[256,1536]{1,0:T(8,128)(2,1)S(1)} %collective-permute-done.9.mixed_ref, bf16[512,3072]{1,0:T(8,128)(2,1)S(1)} %get-tuple-element.53.refs_0_, ...), custom_call_target="tpu_custom_call" | custom-call | flops 1509949440 | bytes 9437184 | tf_op jit(solution)/shard_map/pallas_call | solution.py:384
  48.3 1.1 %collective-permute-start.10 = (bf16[32,3072]{1,0:T(8,128)(2,1)S(1)}, bf16[32,3072]{1,0:T(8,128)(2,1)S(1)}, u32[]{:S(2)}, u32[]{:S(2)}) collective-permute-start(bf16[32,3072]{1,0:T(8,128)(2,1)S(1)} %get-tuple-element.63), channel_id=1, source_target_pairs={{0,1},{1,0},{2,3},{3,2},{4,5},{5,4},{6,7},{7,6},{8,9},{9,8},{10,11... | collective-permute-start | bytes 589832 | tf_op jit(solution)/shard_map/ppermute | solution.py:438
  49.4 3.6 %collective-permute-done.12 = bf16[32,3072]{1,0:T(8,128)(2,1)S(1)} collective-permute-done((bf16[32,3072]{1,0:T(8,128)(2,1)S(1)}, bf16[32,3072]{1,0:T(8,128)(2,1)S(1)}, u32[]{:S(2)}, u32[]{:S(2)}) %collective-permute-start.12) | collective-permute-done | bytes 196640 | tf_op jit(solution)/shard_map/ppermute | solution.py:438
  53.1 2.1 %collective-permute-start.13 = (bf16[32,3072]{1,0:T(8,128)(2,1)S(1)}, bf16[32,3072]{1,0:T(8,128)(2,1)S(1)}, u32[]{:S(2)}, u32[]{:S(2)}) collective-permute-start(bf16[32,3072]{1,0:T(8,128)(2,1)S(1)} %add_convert_fusion.1), channel_id=1, source_target_pairs={{2,0},{3,1},{4,2},{5,3},{6,4},{7,5},{0,6},{1,7},{10,8},{11,9},{12,... | collective-permute-start | bytes 589832 | tf_op jit(solution)/shard_map/ppermute | solution.py:435
  57.9 4.8 %collective-permute-done.14 = bf16[32,3072]{1,0:T(8,128)(2,1)S(1)} collective-permute-done((bf16[32,3072]{1,0:T(8,128)(2,1)S(1)}, bf16[32,3072]{1,0:T(8,128)(2,1)S(1)}, u32[]{:S(2)}, u32[]{:S(2)}) %collective-permute-start.14) | collective-permute-done | bytes 196640 | tf_op jit(solution)/shard_map/ppermute | solution.py:438
  62.9 2.0 %collective-permute-start.15 = (bf16[32,3072]{1,0:T(8,128)(2,1)S(1)}, bf16[32,3072]{1,0:T(8,128)(2,1)S(1)}, u32[]{:S(2)}, u32[]{:S(2)}) collective-permute-start(bf16[32,3072]{1,0:T(8,128)(2,1)S(1)} %add_convert_fusion), channel_id=1, source_target_pairs={{2,0},{3,1},{4,2},{5,3},{6,4},{7,5},{0,6},{1,7},{10,8},{11,9},{12,... | collective-permute-start | bytes 589832 | tf_op jit(solution)/shard_map/ppermute | solution.py:435
  64.9 1.1 %collective-permute-done.11 = bf16[32,3072]{1,0:T(8,128)(2,1)S(1)} collective-permute-done((bf16[32,3072]{1,0:T(8,128)(2,1)S(1)}, bf16[32,3072]{1,0:T(8,128)(2,1)S(1)}, u32[]{:S(2)}, u32[]{:S(2)}) %collective-permute-start.11) | collective-permute-done | bytes 196640 | tf_op jit(solution)/shard_map/ppermute | solution.py:432
  65.9 2.7 %collective-permute-done.15 = bf16[32,3072]{1,0:T(8,128)(2,1)S(1)} collective-permute-done((bf16[32,3072]{1,0:T(8,128)(2,1)S(1)}, bf16[32,3072]{1,0:T(8,128)(2,1)S(1)}, u32[]{:S(2)}, u32[]{:S(2)}) %collective-permute-start.15) | collective-permute-done | bytes 196640 | tf_op jit(solution)/shard_map/ppermute | solution.py:435
  69.4 1.3 %collective-permute-done.17 = bf16[1,16,3072]{2,1,0:T(8,128)(2,1)S(1)} collective-permute-done((bf16[1,16,3072]{2,1,0:T(8,128)(2,1)S(1)}, bf16[1,16,3072]{2,1,0:T(8,128)(2,1)S(1)}, u32[]{:S(2)}, u32[]{:S(2)}) %collective-permute-start.17) | collective-permute-done | bytes 98336 | tf_op jit(solution)/shard_map/ppermute | solution.py:575
  (38 shorter events, 8.6 us)
Async XLA Ops:
  1.0 1.5 %collective-permute-start = (bf16[16,3072]{1,0:T(8,128)(2,1)S(1)}, bf16[16,3072]{1,0:T(8,128)(2,1)S(1)}, u32[]{:S(2)}, u32[]{:S(2)}) collective-permute-start(bf16[16,3072]{1,0:T(8,128)(2,1)S(1)} %get-tuple-element.74), channel_id=1, source_target_pairs={{0,8},{8,0},{1,9},{9,1},{2,10},{10,2},{3,11},{11,3},{4,12},{12,4},... | collective-permute-start | bytes 294920 | tf_op jit(solution)/shard_map/ppermute | solution.py:530
  2.4 10.2 %collective-permute-start.2 = (bf16[32,3072]{1,0:T(8,128)(2,1)S(1)}, bf16[32,3072]{1,0:T(8,128)(2,1)S(1)}, u32[]{:S(2)}, u32[]{:S(2)}) collective-permute-start(bf16[32,3072]{1,0:T(8,128)(2,1)S(1)} %bitcast.12), channel_id=1, source_target_pairs={{0,2},{1,3},{2,4},{3,5},{4,6},{5,7},{6,0},{7,1},{8,10},{9,11},{10,... | collective-permute-start | bytes 589832 | tf_op jit(solution)/shard_map/ppermute | solution.py:432
  5.4 7.2 %collective-permute-start.1 = (bf16[32,3072]{1,0:T(8,128)(2,1)S(1)}, bf16[32,3072]{1,0:T(8,128)(2,1)S(1)}, u32[]{:S(2)}, u32[]{:S(2)}) collective-permute-start(bf16[32,3072]{1,0:T(8,128)(2,1)S(1)} %bitcast.13), channel_id=1, source_target_pairs={{0,1},{1,0},{2,3},{3,2},{4,5},{5,4},{6,7},{7,6},{8,9},{9,8},{10,11... | collective-permute-start | bytes 589832 | tf_op jit(solution)/shard_map/ppermute | solution.py:438
  12.7 8.5 %collective-permute-start.3 = (bf16[32,3072]{1,0:T(8,128)(2,1)S(1)}, bf16[32,3072]{1,0:T(8,128)(2,1)S(1)}, u32[]{:S(2)}, u32[]{:S(2)}) collective-permute-start(bf16[32,3072]{1,0:T(8,128)(2,1)S(1)} %collective-permute-done.2.refs_1_), channel_id=1, source_target_pairs={{0,2},{1,3},{2,4},{3,5},{4,6},{5,7},{6,0},{7,1},{8,10},{9,11},{10,... | collective-permute-start | bytes 589832 | tf_op jit(solution)/shard_map/ppermute | solution.py:432
  13.7 8.6 %collective-permute-start.4 = (bf16[32,3072]{1,0:T(8,128)(2,1)S(1)}, bf16[32,3072]{1,0:T(8,128)(2,1)S(1)}, u32[]{:S(2)}, u32[]{:S(2)}) collective-permute-start(bf16[32,3072]{1,0:T(8,128)(2,1)S(1)} %collective-permute-done.2.refs_1_), channel_id=1, source_target_pairs={{0,1},{1,0},{2,3},{3,2},{4,5},{5,4},{6,7},{7,6},{8,9},{9,8},{10,11... | collective-permute-start | bytes 589832 | tf_op jit(solution)/shard_map/ppermute | solution.py:438
  21.2 9.5 %collective-permute-start.6 = (bf16[64,3072]{1,0:T(8,128)(2,1)S(1)}, bf16[64,3072]{1,0:T(8,128)(2,1)S(1)}, u32[]{:S(2)}, u32[]{:S(2)}) collective-permute-start(bf16[64,3072]{1,0:T(8,128)(2,1)S(1)} %shard_map.74), channel_id=1, source_target_pairs={{2,0},{3,1},{4,2},{5,3},{6,4},{7,5},{0,6},{1,7},{10,8},{11,9},{12,... | collective-permute-start | bytes 1179656 | tf_op jit(solution)/shard_map/ppermute | solution.py:435
  21.2 7.2 %collective-permute-start.5 = (bf16[32,3072]{1,0:T(8,128)(2,1)S(1)}, bf16[32,3072]{1,0:T(8,128)(2,1)S(1)}, u32[]{:S(2)}, u32[]{:S(2)}) collective-permute-start(bf16[32,3072]{1,0:T(8,128)(2,1)S(1)} %collective-permute-done.3.refs_2_), channel_id=1, source_target_pairs={{0,1},{1,0},{2,3},{3,2},{4,5},{5,4},{6,7},{7,6},{8,9},{9,8},{10,11... | collective-permute-start | bytes 589832 | tf_op jit(solution)/shard_map/ppermute | solution.py:438
  28.2 7.5 %collective-permute-start.7 = (bf16[160,1536]{1,0:T(8,128)(2,1)S(1)}, bf16[160,1536]{1,0:T(8,128)(2,1)S(1)}, u32[]{:S(2)}, u32[]{:S(2)}) collective-permute-start(bf16[160,1536]{1,0:T(8,128)(2,1)S(1)} %get-tuple-element.50), channel_id=1, source_target_pairs={{0,8},{8,0},{1,9},{9,1},{2,10},{10,2},{3,11},{11,3},{4,12},{12,4},... | collective-permute-start | bytes 1474568 | tf_op jit(solution)/shard_map/ppermute | solution.py:544
  33.1 2.6 %collective-permute-start.8 = (bf16[96,1536]{1,0:T(8,128)(2,1)S(1)}, bf16[96,1536]{1,0:T(8,128)(2,1)S(1)}, u32[]{:S(2)}, u32[]{:S(2)}) collective-permute-start(bf16[96,1536]{1,0:T(8,128)(2,1)S(1)} %get-tuple-element.51), channel_id=1, source_target_pairs={{0,8},{8,0},{1,9},{9,1},{2,10},{10,2},{3,11},{11,3},{4,12},{12,4},... | collective-permute-start | bytes 884744 | tf_op jit(solution)/shard_map/ppermute | solution.py:544
  33.2 2.5 %copy-start = (f32[3,3,3072]{2,1,0:T(4,128)S(1)}, f32[3,3,3072]{2,1,0:T(4,128)}, u32[]{:S(2)}) copy-start(f32[3,3,3072]{2,1,0:T(4,128)} %refs_5_.1) | copy-start | bytes 331780
  33.2 2.5 %copy-start.2 = (f32[3072]{0:T(1024)S(1)}, f32[3072]{0:T(1024)}, u32[]{:S(2)}) copy-start(f32[3072]{0:T(1024)} %param.9) | copy-start | bytes 36868
  33.2 2.5 %copy-start.3 = (f32[3072]{0:T(1024)S(1)}, f32[3072]{0:T(1024)}, u32[]{:S(2)}) copy-start(f32[3072]{0:T(1024)} %param.11) | copy-start | bytes 36868
  39.2 4.1 %collective-permute-start.9 = (bf16[256,1536]{1,0:T(8,128)(2,1)S(1)}, bf16[256,1536]{1,0:T(8,128)(2,1)S(1)}, u32[]{:S(2)}, u32[]{:S(2)}) collective-permute-start(bf16[256,1536]{1,0:T(8,128)(2,1)S(1)} %get-tuple-element.52.mixed_ref), channel_id=1, source_target_pairs={{0,8},{8,0},{1,9},{9,1},{2,10},{10,2},{3,11},{11,3},{4,12},{12,4},... | collective-permute-start | bytes 2359304 | tf_op jit(solution)/shard_map/ppermute | solution.py:559
  45.2 23.5 %copy-start.1 = (f32[6144]{0:T(1024)S(1)}, f32[6144]{0:T(1024)}, u32[]{:S(2)}) copy-start(f32[6144]{0:T(1024)} %param.13) | copy-start | bytes 73732
  45.2 7.8 %collective-permute-start.12 = (bf16[32,3072]{1,0:T(8,128)(2,1)S(1)}, bf16[32,3072]{1,0:T(8,128)(2,1)S(1)}, u32[]{:S(2)}, u32[]{:S(2)}) collective-permute-start(bf16[32,3072]{1,0:T(8,128)(2,1)S(1)} %get-tuple-element.66), channel_id=1, source_target_pairs={{0,1},{1,0},{2,3},{3,2},{4,5},{5,4},{6,7},{7,6},{8,9},{9,8},{10,11... | collective-permute-start | bytes 589832 | tf_op jit(solution)/shard_map/ppermute | solution.py:438
  48.3 8.4 %collective-permute-start.10 = (bf16[32,3072]{1,0:T(8,128)(2,1)S(1)}, bf16[32,3072]{1,0:T(8,128)(2,1)S(1)}, u32[]{:S(2)}, u32[]{:S(2)}) collective-permute-start(bf16[32,3072]{1,0:T(8,128)(2,1)S(1)} %get-tuple-element.63), channel_id=1, source_target_pairs={{0,1},{1,0},{2,3},{3,2},{4,5},{5,4},{6,7},{7,6},{8,9},{9,8},{10,11... | collective-permute-start | bytes 589832 | tf_op jit(solution)/shard_map/ppermute | solution.py:438
  53.1 9.7 %collective-permute-start.13 = (bf16[32,3072]{1,0:T(8,128)(2,1)S(1)}, bf16[32,3072]{1,0:T(8,128)(2,1)S(1)}, u32[]{:S(2)}, u32[]{:S(2)}) collective-permute-start(bf16[32,3072]{1,0:T(8,128)(2,1)S(1)} %add_convert_fusion.1), channel_id=1, source_target_pairs={{2,0},{3,1},{4,2},{5,3},{6,4},{7,5},{0,6},{1,7},{10,8},{11,9},{12,... | collective-permute-start | bytes 589832 | tf_op jit(solution)/shard_map/ppermute | solution.py:435
  55.2 7.6 %collective-permute-start.14 = (bf16[32,3072]{1,0:T(8,128)(2,1)S(1)}, bf16[32,3072]{1,0:T(8,128)(2,1)S(1)}, u32[]{:S(2)}, u32[]{:S(2)}) collective-permute-start(bf16[32,3072]{1,0:T(8,128)(2,1)S(1)} %get-tuple-element.68), channel_id=1, source_target_pairs={{0,1},{1,0},{2,3},{3,2},{4,5},{5,4},{6,7},{7,6},{8,9},{9,8},{10,11... | collective-permute-start | bytes 589832 | tf_op jit(solution)/shard_map/ppermute | solution.py:438
  56.8 9.1 %collective-permute-start.11 = (bf16[32,3072]{1,0:T(8,128)(2,1)S(1)}, bf16[32,3072]{1,0:T(8,128)(2,1)S(1)}, u32[]{:S(2)}, u32[]{:S(2)}) collective-permute-start(bf16[32,3072]{1,0:T(8,128)(2,1)S(1)} %add_convert_fusion.2), channel_id=1, source_target_pairs={{0,2},{1,3},{2,4},{3,5},{4,6},{5,7},{6,0},{7,1},{8,10},{9,11},{10,... | collective-permute-start | bytes 589832 | tf_op jit(solution)/shard_map/ppermute | solution.py:432
  57.0 7.9 %collective-permute-start.16 = (bf16[32,3072]{1,0:T(8,128)(2,1)S(1)}, bf16[32,3072]{1,0:T(8,128)(2,1)S(1)}, u32[]{:S(2)}, u32[]{:S(2)}) collective-permute-start(bf16[32,3072]{1,0:T(8,128)(2,1)S(1)} %get-tuple-element.70), channel_id=1, source_target_pairs={{0,1},{1,0},{2,3},{3,2},{4,5},{5,4},{6,7},{7,6},{8,9},{9,8},{10,11... | collective-permute-start | bytes 589832 | tf_op jit(solution)/shard_map/ppermute | solution.py:438
  62.9 5.7 %collective-permute-start.15 = (bf16[32,3072]{1,0:T(8,128)(2,1)S(1)}, bf16[32,3072]{1,0:T(8,128)(2,1)S(1)}, u32[]{:S(2)}, u32[]{:S(2)}) collective-permute-start(bf16[32,3072]{1,0:T(8,128)(2,1)S(1)} %add_convert_fusion), channel_id=1, source_target_pairs={{2,0},{3,1},{4,2},{5,3},{6,4},{7,5},{0,6},{1,7},{10,8},{11,9},{12,... | collective-permute-start | bytes 589832 | tf_op jit(solution)/shard_map/ppermute | solution.py:435
  69.3 1.4 %collective-permute-start.17 = (bf16[1,16,3072]{2,1,0:T(8,128)(2,1)S(1)}, bf16[1,16,3072]{2,1,0:T(8,128)(2,1)S(1)}, u32[]{:S(2)}, u32[]{:S(2)}) collective-permute-start(bf16[1,16,3072]{2,1,0:T(8,128)(2,1)S(1)} %get-tuple-element.72), channel_id=1, source_target_pairs={{0,8},{8,0},{1,9},{9,1},{2,10},{10,2},{3,11},{11,3},{4,12},{12,4},... | collective-permute-start | bytes 294920 | tf_op jit(solution)/shard_map/ppermute | solution.py:575

commit v6 on v5

--- a/solution.py
+++ b/solution.py
@@ -270,7 +270,8 @@
         first, last = at_y == 0, at_y == grid_y - 1
         base = info_ref[0] * width
         places = [
-            lax.rem(info_ref[1] + (links.ring - j), links.ring) * links.lanes + lax.rem(info_ref[2] + q, links.lanes)
+            links.swapped(lax.rem(info_ref[1] + (links.ring - j), links.ring)) * links.lanes
+            + lax.rem(info_ref[2] + q, links.lanes)
             for _, _, q, j in slots
         ]
 
@@ -424,9 +425,15 @@
         self.lanes = 2 if count % 2 == 0 else 1
         self.ring = count // self.lanes
         self.half = self.ring // 2
-        self.upward = [(t, (t + self.lanes) % count) for t in range(count)]
+        self.upward = []
+        for t in range(count):
+            onward = self.swapped((self.swapped(t // self.lanes) + 1) % self.ring)
+            self.upward.append((t, onward * self.lanes + t % self.lanes))
         self.downward = [(t, s) for s, t in self.upward]
         self.pairs = [(t, t ^ 1) for t in range(count)]
+
+    def swapped(self, place):
+        return place ^ (place >> 1) if self.ring == 4 else place
 
     def up(self, value):
         return lax.ppermute(value, "tp", self.upward)
@@ -522,12 +529,12 @@
     core = lax.axis_index("sp")
     mine = lax.axis_index("tp")
     swap = [(0, 1), (1, 0)]
-    info = jnp.stack([core, mine // links.lanes, mine % links.lanes]).astype(jnp.int32)
+    info = jnp.stack([core, links.swapped(mine // links.lanes), mine % links.lanes]).astype(jnp.int32)
 
     flat = tokens.reshape(cols * grid_half, width_model)
+    whole = lax.ppermute(flat, "sp", swap)
     keep = lax.dynamic_slice_in_dim(flat, core * half, half, axis=1)
-    give = lax.dynamic_slice_in_dim(flat, (1 - core) * half, half, axis=1)
-    take = lax.ppermute(give, "sp", swap)
+    take = lax.dynamic_slice_in_dim(whole, core * half, half, axis=1)
     keep, take = (x.reshape(cols, 1, grid_half, half) for x in (keep, take))
     block = jnp.where(core == 0, jnp.concatenate([keep, take], 1), jnp.concatenate([take, keep], 1))
     block = block.reshape(rows, half)

time: 71.5 us -> 69.5 us (0.972)
  waiting for transfers between devices: 24.5 us -> 15.1 us
  starting transfers between devices: 17.8 us -> 25.4 us
    ppermute x3, waiting for transfers between devices: 8.36 us -> 3.28 us  [up(): return lax.ppermute(value, 'tp', self.upward)]
    ppermute x3, starting transfers between devices: 4.16 us -> 7.81 us  [up(): return lax.ppermute(value, 'tp', self.upward)]
    ppermute x7, waiting for transfers between devices: 9.01 us -> 5.82 us  [cross(): return lax.ppermute(value, 'tp', self.pairs)]
    ppermute x3, starting transfers between devices: 4.12 us -> 6.42 us  [down(): return lax.ppermute(value, 'tp', self.downward)]
    ppermute x7, starting transfers between devices: 8.3 us -> 9.9 us  [cross(): return lax.ppermute(value, 'tp', self.pairs)]
  transfers between devices with their start and end apart: 18 -> 18, of which waited for: 10 -> 11; matrix products, arithmetic and copies ran while one was open for 0% -> 2% of each run, Pallas kernels for 29% -> 30%
where the time goes in v6:
time: 69.5 us; the launch traced here: 69.4 us
  Pallas kernels  26.7 us (38%)
  starting transfers between devices  25.4 us (37%)
  waiting for transfers between devices  15.1 us (22%)
  other arithmetic  1.1 us (2%)
  local copies, waits for them, and re-layouts  0.93 us (1%)
    ppermute x7, starting transfers between devices, cross(): return lax.ppermute(value, 'tp', self.pairs)  9.9 us
    ppermute x3, starting transfers between devices, up(): return lax.ppermute(value, 'tp', self.upward)  7.81 us
    ppermute x3, starting transfers between devices, down(): return lax.ppermute(value, 'tp', self.downward)  6.42 us
    pallas_call x1, Pallas kernels, up_early(): pl.pallas_call(kernel, out_shape=(pltpu.VMEM((total, width), BF16), pltpu...  5.94 us
    ppermute x7, waiting for transfers between devices, cross(): return lax.ppermute(value, 'tp', self.pairs)  5.82 us
    ppermute x3, waiting for transfers between devices, down(): return lax.ppermute(value, 'tp', self.downward)  4.4 us
    pallas_call x1, Pallas kernels, fetch(): pl.pallas_call(kernel, out_shape=pltpu.VMEM((count, weight.shape[1]), wei...  4.34 us
    pallas_call x2, Pallas kernels, down_other(): pl.pallas_call(kernel, out_shape=tuple((pltpu.VMEM((rows, width), kind) f...  3.99 us
  transfers between devices with their start and end apart: 18, of which 11 were waited for; matrix products, arithmetic and copies ran while one was open for 2% of the time, Pallas kernels for 30%

profile of v6, /device:TPU:0, one launch (start us, length us, event | category | flops | bytes accessed | tf_op | source)
XLA Modules:
  0.0 69.4 jit_solution(13059279457813850852)
XLA Ops:
  1.8 3.0 %collective-permute-start.2 = (bf16[32,3072]{1,0:T(8,128)(2,1)S(1)}, bf16[32,3072]{1,0:T(8,128)(2,1)S(1)}, u32[]{:S(2)}, u32[]{:S(2)}) collective-permute-start(bf16[32,3072]{1,0:T(8,128)(2,1)S(1)} %bitcast.12), channel_id=1, source_target_pairs={{0,2},{1,3},{2,6},{3,7},{4,0},{5,1},{6,4},{7,5},{8,10},{9,11},{10,... | collective-permute-start | bytes 589832 | tf_op jit(solution)/shard_map/ppermute | solution.py:439
  4.8 1.5 %collective-permute-start.1 = (bf16[32,3072]{1,0:T(8,128)(2,1)S(1)}, bf16[32,3072]{1,0:T(8,128)(2,1)S(1)}, u32[]{:S(2)}, u32[]{:S(2)}) collective-permute-start(bf16[32,3072]{1,0:T(8,128)(2,1)S(1)} %bitcast.13), channel_id=1, source_target_pairs={{0,1},{1,0},{2,3},{3,2},{4,5},{5,4},{6,7},{7,6},{8,9},{9,8},{10,11... | collective-permute-start | bytes 589832 | tf_op jit(solution)/shard_map/ppermute | solution.py:445
  6.3 4.3 %shard_map.73.refs_5_.refs_2_.upper_ref = bf16[1536,3072]{1,0:T(8,128)(2,1)S(1)} custom-call(s32[3]{0:T(128)S(1)} %pad_add_fusion.info_ref, bf16[3072,3072]{1,0:T(8,128)(2,1)} %refs_6_.1), custom_call_target="tpu_custom_call" | custom-call | bytes 18874368 | tf_op jit(solution)/shard_map/pallas_call | solution.py:71
  11.4 2.6 %collective-permute-start.3 = (bf16[32,3072]{1,0:T(8,128)(2,1)S(1)}, bf16[32,3072]{1,0:T(8,128)(2,1)S(1)}, u32[]{:S(2)}, u32[]{:S(2)}) collective-permute-start(bf16[32,3072]{1,0:T(8,128)(2,1)S(1)} %collective-permute-done.2.refs_1_), channel_id=1, source_target_pairs={{0,2},{1,3},{2,6},{3,7},{4,0},{5,1},{6,4},{7,5},{8,10},{9,11},{10,... | collective-permute-start | bytes 589832 | tf_op jit(solution)/shard_map/ppermute | solution.py:439
  14.0 1.5 %collective-permute-start.4 = (bf16[32,3072]{1,0:T(8,128)(2,1)S(1)}, bf16[32,3072]{1,0:T(8,128)(2,1)S(1)}, u32[]{:S(2)}, u32[]{:S(2)}) collective-permute-start(bf16[32,3072]{1,0:T(8,128)(2,1)S(1)} %collective-permute-done.2.refs_1_), channel_id=1, source_target_pairs={{0,1},{1,0},{2,3},{3,2},{4,5},{5,4},{6,7},{7,6},{8,9},{9,8},{10,11... | collective-permute-start | bytes 589832 | tf_op jit(solution)/shard_map/ppermute | solution.py:445
  15.6 2.7 %collective-permute-done.3.refs_2_ = bf16[32,3072]{1,0:T(8,128)(2,1)S(1)} collective-permute-done((bf16[32,3072]{1,0:T(8,128)(2,1)S(1)}, bf16[32,3072]{1,0:T(8,128)(2,1)S(1)}, u32[]{:S(2)}, u32[]{:S(2)}) %collective-permute-start.3) | collective-permute-done | bytes 196640 | tf_op jit(solution)/shard_map/ppermute | solution.py:439
  18.3 1.2 %collective-permute-start.6 = (bf16[64,3072]{1,0:T(8,128)(2,1)S(1)}, bf16[64,3072]{1,0:T(8,128)(2,1)S(1)}, u32[]{:S(2)}, u32[]{:S(2)}) collective-permute-start(bf16[64,3072]{1,0:T(8,128)(2,1)S(1)} %shard_map.74), channel_id=1, source_target_pairs={{2,0},{3,1},{6,2},{7,3},{0,4},{1,5},{4,6},{5,7},{10,8},{11,9},{14,... | collective-permute-start | bytes 1179656 | tf_op jit(solution)/shard_map/ppermute | solution.py:442
  19.6 1.5 %collective-permute-start.5 = (bf16[32,3072]{1,0:T(8,128)(2,1)S(1)}, bf16[32,3072]{1,0:T(8,128)(2,1)S(1)}, u32[]{:S(2)}, u32[]{:S(2)}) collective-permute-start(bf16[32,3072]{1,0:T(8,128)(2,1)S(1)} %collective-permute-done.3.refs_2_), channel_id=1, source_target_pairs={{0,1},{1,0},{2,3},{3,2},{4,5},{5,4},{6,7},{7,6},{8,9},{9,8},{10,11... | collective-permute-start | bytes 589832 | tf_op jit(solution)/shard_map/ppermute | solution.py:445
  21.1 5.9 %shard_map.75 = (bf16[160,1536]{1,0:T(8,128)(2,1)S(1)}, f32[160,1536]{1,0:T(8,128)S(1)}, bf16[1536,3072]{1,0:T(8,128)(2,1)S(1)}) custom-call(s32[3]{0:T(128)S(1)} %pad_add_fusion.info_ref, bf16[32,3072]{1,0:T(8,128)(2,1)S(1)} %bitcast.15, bf16[32,3072]{1,0:T(8,128)(2,1)S(1)} %collective-permute-done.2.refs_1_, ...), custom_call_target="tpu_custom_call" | custom-call | flops 3019898880 | bytes 9437184 | tf_op jit(solution)/shard_map/pallas_call | solution.py:148
  27.6 2.4 %shard_map.76 = (bf16[96,1536]{1,0:T(8,128)(2,1)S(1)}, bf16[96,3072]{1,0:T(8,128)(2,1)S(1)}, bf16[512,3072]{1,0:T(8,128)(2,1)S(1)}) custom-call(s32[3]{0:T(128)S(1)} %pad_add_fusion.info_ref, bf16[32,3072]{1,0:T(8,128)(2,1)S(1)} %collective-permute-done.5.refs_0_, bf16[64,3072]{1,0:T(8,128)(2,1)S(1)} %collective-permute-done.6.refs_1_, ...), custom_call_target="tpu_custom_call" | custom-call | flops 905969664 | bytes 9437184 | tf_op jit(solution)/shard_map/pallas_call | solution.py:211
  30.1 2.4 %shard_map.77 = (f32[96,1536]{1,0:T(8,128)S(1)}, bf16[512,3072]{1,0:T(8,128)(2,1)S(1)}) custom-call(s32[3]{0:T(128)S(1)} %pad_add_fusion.info_ref, bf16[96,3072]{1,0:T(8,128)(2,1)S(1)} %get-tuple-element.48.tokens_ref, bf16[1536,3072]{1,0:T(8,128)(2,1)S(1)} %shard_map.73.refs_5_.refs_2_.upper_ref, ...), custom_call_target="tpu_custom_call" | custom-call | flops 905969664 | bytes 9437184 | tf_op jit(solution)/shard_map/pallas_call | solution.py:234
  32.6 3.4 %shard_map.78 = (bf16[256,1536]{1,0:T(8,128)(2,1)S(1)}, bf16[512,3072]{1,0:T(8,128)(2,1)S(1)}, bf16[512,3072]{1,0:T(8,128)(2,1)S(1)}) custom-call(s32[3]{0:T(128)S(1)} %pad_add_fusion.info_ref, f32[160,1536]{1,0:T(8,128)S(1)} %get-tuple-element.45.refs_0_, f32[96,1536]{1,0:T(8,128)S(1)} %get-tuple-element.49.refs_1_, ...), custom_call_target="tpu_custom_call" | custom-call | flops 23592960 | bytes 3145728 | tf_op jit(solution)/shard_map/pallas_call | solution.py:305
  36.6 3.5 %shard_map.79 = (f32[256,3072]{1,0:T(8,128)S(1)}, bf16[1024,3072]{1,0:T(8,128)(2,1)S(1)}) custom-call(s32[3]{0:T(128)S(1)} %pad_add_fusion.info_ref, bf16[256,1536]{1,0:T(8,128)(2,1)S(1)} %get-tuple-element.52.mixed_ref, bf16[512,3072]{1,0:T(8,128)(2,1)S(1)} %get-tuple-element.54.refs_0_, bf16[512,3072]{1,0:T(8,128)(2,1)S(1)} %get-tuple-element.55.refs_1_, ...), custom_call_target="tpu_custom_call" | custom-call | flops 2415919104 | bytes 9437184 | tf_op jit(solution)/shard_map/pallas_call | solution.py:344
  40.1 1.9 %shard_map.80 = (bf16[32,3072]{1,0:T(8,128)(2,1)S(1)}, f32[32,3072]{1,0:T(8,128)S(1)}, bf16[32,3072]{1,0:T(8,128)(2,1)S(1)}) custom-call(bf16[256,1536]{1,0:T(8,128)(2,1)S(1)} %collective-permute-done.9.mixed_ref, bf16[512,3072]{1,0:T(8,128)(2,1)S(1)} %get-tuple-element.53.refs_0_, bf16[1024,3072]{1,0:T(8,128)(2,1)S(1)} %get-tuple-element.57.refs_1_, ...), custom_call_target="tpu_custom_call" | custom-call | flops 905969664 | bytes 9437184 | tf_op jit(solution)/shard_map/pallas_call | solution.py:385
  43.3 2.1 %shard_map.81 = (f32[32,3072]{1,0:T(8,128)S(1)}, f32[32,3072]{1,0:T(8,128)S(1)}, f32[32,3072]{1,0:T(8,128)S(1)}, bf16[32,3072]{1,0:T(8,128)(2,1)S(1)}, bf16[32,3072]{1,0:T(8,128)(2,1)S(1)}) custom-call(bf16[256,1536]{1,0:T(8,128)(2,1)S(1)} %collective-permute-done.9.mixed_ref, bf16[512,3072]{1,0:T(8,128)(2,1)S(1)} %get-tuple-element.53.refs_0_, ...), custom_call_target="tpu_custom_call" | custom-call | flops 1509949440 | bytes 9437184 | tf_op jit(solution)/shard_map/pallas_call | solution.py:385
  46.3 3.6 %collective-permute-done.12 = bf16[32,3072]{1,0:T(8,128)(2,1)S(1)} collective-permute-done((bf16[32,3072]{1,0:T(8,128)(2,1)S(1)}, bf16[32,3072]{1,0:T(8,128)(2,1)S(1)}, u32[]{:S(2)}, u32[]{:S(2)}) %collective-permute-start.12) | collective-permute-done | bytes 196640 | tf_op jit(solution)/shard_map/ppermute | solution.py:445
  50.0 2.6 %collective-permute-start.13 = (bf16[32,3072]{1,0:T(8,128)(2,1)S(1)}, bf16[32,3072]{1,0:T(8,128)(2,1)S(1)}, u32[]{:S(2)}, u32[]{:S(2)}) collective-permute-start(bf16[32,3072]{1,0:T(8,128)(2,1)S(1)} %add_convert_fusion.1), channel_id=1, source_target_pairs={{2,0},{3,1},{6,2},{7,3},{0,4},{1,5},{4,6},{5,7},{10,8},{11,9},{14,... | collective-permute-start | bytes 589832 | tf_op jit(solution)/shard_map/ppermute | solution.py:442
  52.6 1.5 %collective-permute-start.14 = (bf16[32,3072]{1,0:T(8,128)(2,1)S(1)}, bf16[32,3072]{1,0:T(8,128)(2,1)S(1)}, u32[]{:S(2)}, u32[]{:S(2)}) collective-permute-start(bf16[32,3072]{1,0:T(8,128)(2,1)S(1)} %get-tuple-element.68), channel_id=1, source_target_pairs={{0,1},{1,0},{2,3},{3,2},{4,5},{5,4},{6,7},{7,6},{8,9},{9,8},{10,11... | collective-permute-start | bytes 589832 | tf_op jit(solution)/shard_map/ppermute | solution.py:445
  54.2 2.2 %collective-permute-start.11 = (bf16[32,3072]{1,0:T(8,128)(2,1)S(1)}, bf16[32,3072]{1,0:T(8,128)(2,1)S(1)}, u32[]{:S(2)}, u32[]{:S(2)}) collective-permute-start(bf16[32,3072]{1,0:T(8,128)(2,1)S(1)} %add_convert_fusion.2), channel_id=1, source_target_pairs={{0,2},{1,3},{2,6},{3,7},{4,0},{5,1},{6,4},{7,5},{8,10},{9,11},{10,... | collective-permute-start | bytes 589832 | tf_op jit(solution)/shard_map/ppermute | solution.py:439
  56.4 1.6 %collective-permute-start.16 = (bf16[32,3072]{1,0:T(8,128)(2,1)S(1)}, bf16[32,3072]{1,0:T(8,128)(2,1)S(1)}, u32[]{:S(2)}, u32[]{:S(2)}) collective-permute-start(bf16[32,3072]{1,0:T(8,128)(2,1)S(1)} %get-tuple-element.70), channel_id=1, source_target_pairs={{0,1},{1,0},{2,3},{3,2},{4,5},{5,4},{6,7},{7,6},{8,9},{9,8},{10,11... | collective-permute-start | bytes 589832 | tf_op jit(solution)/shard_map/ppermute | solution.py:445
  58.0 1.2 %collective-permute-done.14 = bf16[32,3072]{1,0:T(8,128)(2,1)S(1)} collective-permute-done((bf16[32,3072]{1,0:T(8,128)(2,1)S(1)}, bf16[32,3072]{1,0:T(8,128)(2,1)S(1)}, u32[]{:S(2)}, u32[]{:S(2)}) %collective-permute-start.14) | collective-permute-done | bytes 196640 | tf_op jit(solution)/shard_map/ppermute | solution.py:445
  59.3 2.6 %collective-permute-start.15 = (bf16[32,3072]{1,0:T(8,128)(2,1)S(1)}, bf16[32,3072]{1,0:T(8,128)(2,1)S(1)}, u32[]{:S(2)}, u32[]{:S(2)}) collective-permute-start(bf16[32,3072]{1,0:T(8,128)(2,1)S(1)} %add_convert_fusion), channel_id=1, source_target_pairs={{2,0},{3,1},{6,2},{7,3},{0,4},{1,5},{4,6},{5,7},{10,8},{11,9},{14,... | collective-permute-start | bytes 589832 | tf_op jit(solution)/shard_map/ppermute | solution.py:442
  62.6 3.9 %collective-permute-done.15 = bf16[32,3072]{1,0:T(8,128)(2,1)S(1)} collective-permute-done((bf16[32,3072]{1,0:T(8,128)(2,1)S(1)}, bf16[32,3072]{1,0:T(8,128)(2,1)S(1)}, u32[]{:S(2)}, u32[]{:S(2)}) %collective-permute-start.15) | collective-permute-done | bytes 196640 | tf_op jit(solution)/shard_map/ppermute | solution.py:442
  67.4 1.3 %collective-permute-done.17 = bf16[1,16,3072]{2,1,0:T(8,128)(2,1)S(1)} collective-permute-done((bf16[1,16,3072]{2,1,0:T(8,128)(2,1)S(1)}, bf16[1,16,3072]{2,1,0:T(8,128)(2,1)S(1)}, u32[]{:S(2)}, u32[]{:S(2)}) %collective-permute-start.17) | collective-permute-done | bytes 98336 | tf_op jit(solution)/shard_map/ppermute | solution.py:582
  (39 shorter events, 8.3 us)
Async XLA Ops:
  0.0 1.7 %collective-permute-start = (bf16[16,6144]{1,0:T(8,128)(2,1)}, bf16[16,6144]{1,0:T(8,128)(2,1)S(1)}, u32[]{:S(2)}, u32[]{:S(2)}) collective-permute-start(bf16[16,6144]{1,0:T(8,128)(2,1)} %bitcast.19), channel_id=1, source_target_pairs={{0,8},{8,0},{1,9},{9,1},{2,10},{10,2},{3,11},{11,3},{4,12},{12,4},... | collective-permute-start | bytes 589832 | tf_op jit(solution)/shard_map/ppermute | solution.py:535
  1.8 9.2 %collective-permute-start.2 = (bf16[32,3072]{1,0:T(8,128)(2,1)S(1)}, bf16[32,3072]{1,0:T(8,128)(2,1)S(1)}, u32[]{:S(2)}, u32[]{:S(2)}) collective-permute-start(bf16[32,3072]{1,0:T(8,128)(2,1)S(1)} %bitcast.12), channel_id=1, source_target_pairs={{0,2},{1,3},{2,6},{3,7},{4,0},{5,1},{6,4},{7,5},{8,10},{9,11},{10,... | collective-permute-start | bytes 589832 | tf_op jit(solution)/shard_map/ppermute | solution.py:439
  4.8 6.7 %collective-permute-start.1 = (bf16[32,3072]{1,0:T(8,128)(2,1)S(1)}, bf16[32,3072]{1,0:T(8,128)(2,1)S(1)}, u32[]{:S(2)}, u32[]{:S(2)}) collective-permute-start(bf16[32,3072]{1,0:T(8,128)(2,1)S(1)} %bitcast.13), channel_id=1, source_target_pairs={{0,1},{1,0},{2,3},{3,2},{4,5},{5,4},{6,7},{7,6},{8,9},{9,8},{10,11... | collective-permute-start | bytes 589832 | tf_op jit(solution)/shard_map/ppermute | solution.py:445
  11.4 6.9 %collective-permute-start.3 = (bf16[32,3072]{1,0:T(8,128)(2,1)S(1)}, bf16[32,3072]{1,0:T(8,128)(2,1)S(1)}, u32[]{:S(2)}, u32[]{:S(2)}) collective-permute-start(bf16[32,3072]{1,0:T(8,128)(2,1)S(1)} %collective-permute-done.2.refs_1_), channel_id=1, source_target_pairs={{0,2},{1,3},{2,6},{3,7},{4,0},{5,1},{6,4},{7,5},{8,10},{9,11},{10,... | collective-permute-start | bytes 589832 | tf_op jit(solution)/shard_map/ppermute | solution.py:439
  14.0 7.1 %collective-permute-start.4 = (bf16[32,3072]{1,0:T(8,128)(2,1)S(1)}, bf16[32,3072]{1,0:T(8,128)(2,1)S(1)}, u32[]{:S(2)}, u32[]{:S(2)}) collective-permute-start(bf16[32,3072]{1,0:T(8,128)(2,1)S(1)} %collective-permute-done.2.refs_1_), channel_id=1, source_target_pairs={{0,1},{1,0},{2,3},{3,2},{4,5},{5,4},{6,7},{7,6},{8,9},{9,8},{10,11... | collective-permute-start | bytes 589832 | tf_op jit(solution)/shard_map/ppermute | solution.py:445
  18.3 9.3 %collective-permute-start.6 = (bf16[64,3072]{1,0:T(8,128)(2,1)S(1)}, bf16[64,3072]{1,0:T(8,128)(2,1)S(1)}, u32[]{:S(2)}, u32[]{:S(2)}) collective-permute-start(bf16[64,3072]{1,0:T(8,128)(2,1)S(1)} %shard_map.74), channel_id=1, source_target_pairs={{2,0},{3,1},{6,2},{7,3},{0,4},{1,5},{4,6},{5,7},{10,8},{11,9},{14,... | collective-permute-start | bytes 1179656 | tf_op jit(solution)/shard_map/ppermute | solution.py:442
  19.6 7.6 %collective-permute-start.5 = (bf16[32,3072]{1,0:T(8,128)(2,1)S(1)}, bf16[32,3072]{1,0:T(8,128)(2,1)S(1)}, u32[]{:S(2)}, u32[]{:S(2)}) collective-permute-start(bf16[32,3072]{1,0:T(8,128)(2,1)S(1)} %collective-permute-done.3.refs_2_), channel_id=1, source_target_pairs={{0,1},{1,0},{2,3},{3,2},{4,5},{5,4},{6,7},{7,6},{8,9},{9,8},{10,11... | collective-permute-start | bytes 589832 | tf_op jit(solution)/shard_map/ppermute | solution.py:445
  27.0 5.6 %collective-permute-start.7 = (bf16[160,1536]{1,0:T(8,128)(2,1)S(1)}, bf16[160,1536]{1,0:T(8,128)(2,1)S(1)}, u32[]{:S(2)}, u32[]{:S(2)}) collective-permute-start(bf16[160,1536]{1,0:T(8,128)(2,1)S(1)} %get-tuple-element.50), channel_id=1, source_target_pairs={{0,8},{8,0},{1,9},{9,1},{2,10},{10,2},{3,11},{11,3},{4,12},{12,4},... | collective-permute-start | bytes 1474568 | tf_op jit(solution)/shard_map/ppermute | solution.py:551
  30.0 2.6 %collective-permute-start.8 = (bf16[96,1536]{1,0:T(8,128)(2,1)S(1)}, bf16[96,1536]{1,0:T(8,128)(2,1)S(1)}, u32[]{:S(2)}, u32[]{:S(2)}) collective-permute-start(bf16[96,1536]{1,0:T(8,128)(2,1)S(1)} %get-tuple-element.51), channel_id=1, source_target_pairs={{0,8},{8,0},{1,9},{9,1},{2,10},{10,2},{3,11},{11,3},{4,12},{12,4},... | collective-permute-start | bytes 884744 | tf_op jit(solution)/shard_map/ppermute | solution.py:551
  30.1 2.5 %copy-start = (f32[3,3,3072]{2,1,0:T(4,128)S(1)}, f32[3,3,3072]{2,1,0:T(4,128)}, u32[]{:S(2)}) copy-start(f32[3,3,3072]{2,1,0:T(4,128)} %refs_5_.1) | copy-start | bytes 331780
  30.1 2.5 %copy-start.2 = (f32[3072]{0:T(1024)S(1)}, f32[3072]{0:T(1024)}, u32[]{:S(2)}) copy-start(f32[3072]{0:T(1024)} %param.9) | copy-start | bytes 36868
  30.1 2.5 %copy-start.3 = (f32[3072]{0:T(1024)S(1)}, f32[3072]{0:T(1024)}, u32[]{:S(2)}) copy-start(f32[3072]{0:T(1024)} %param.11) | copy-start | bytes 36868
  36.1 4.1 %collective-permute-start.9 = (bf16[256,1536]{1,0:T(8,128)(2,1)S(1)}, bf16[256,1536]{1,0:T(8,128)(2,1)S(1)}, u32[]{:S(2)}, u32[]{:S(2)}) collective-permute-start(bf16[256,1536]{1,0:T(8,128)(2,1)S(1)} %get-tuple-element.52.mixed_ref), channel_id=1, source_target_pairs={{0,8},{8,0},{1,9},{9,1},{2,10},{10,2},{3,11},{11,3},{4,12},{12,4},... | collective-permute-start | bytes 2359304 | tf_op jit(solution)/shard_map/ppermute | solution.py:566
  42.1 24.6 %copy-start.1 = (f32[6144]{0:T(1024)S(1)}, f32[6144]{0:T(1024)}, u32[]{:S(2)}) copy-start(f32[6144]{0:T(1024)} %param.13) | copy-start | bytes 73732
  42.1 7.8 %collective-permute-start.12 = (bf16[32,3072]{1,0:T(8,128)(2,1)S(1)}, bf16[32,3072]{1,0:T(8,128)(2,1)S(1)}, u32[]{:S(2)}, u32[]{:S(2)}) collective-permute-start(bf16[32,3072]{1,0:T(8,128)(2,1)S(1)} %get-tuple-element.66), channel_id=1, source_target_pairs={{0,1},{1,0},{2,3},{3,2},{4,5},{5,4},{6,7},{7,6},{8,9},{9,8},{10,11... | collective-permute-start | bytes 589832 | tf_op jit(solution)/shard_map/ppermute | solution.py:445
  45.3 8.8 %collective-permute-start.10 = (bf16[32,3072]{1,0:T(8,128)(2,1)S(1)}, bf16[32,3072]{1,0:T(8,128)(2,1)S(1)}, u32[]{:S(2)}, u32[]{:S(2)}) collective-permute-start(bf16[32,3072]{1,0:T(8,128)(2,1)S(1)} %get-tuple-element.63), channel_id=1, source_target_pairs={{0,1},{1,0},{2,3},{3,2},{4,5},{5,4},{6,7},{7,6},{8,9},{9,8},{10,11... | collective-permute-start | bytes 589832 | tf_op jit(solution)/shard_map/ppermute | solution.py:445
  50.0 9.3 %collective-permute-start.13 = (bf16[32,3072]{1,0:T(8,128)(2,1)S(1)}, bf16[32,3072]{1,0:T(8,128)(2,1)S(1)}, u32[]{:S(2)}, u32[]{:S(2)}) collective-permute-start(bf16[32,3072]{1,0:T(8,128)(2,1)S(1)} %add_convert_fusion.1), channel_id=1, source_target_pairs={{2,0},{3,1},{6,2},{7,3},{0,4},{1,5},{4,6},{5,7},{10,8},{11,9},{14,... | collective-permute-start | bytes 589832 | tf_op jit(solution)/shard_map/ppermute | solution.py:442
  52.6 6.7 %collective-permute-start.14 = (bf16[32,3072]{1,0:T(8,128)(2,1)S(1)}, bf16[32,3072]{1,0:T(8,128)(2,1)S(1)}, u32[]{:S(2)}, u32[]{:S(2)}) collective-permute-start(bf16[32,3072]{1,0:T(8,128)(2,1)S(1)} %get-tuple-element.68), channel_id=1, source_target_pairs={{0,1},{1,0},{2,3},{3,2},{4,5},{5,4},{6,7},{7,6},{8,9},{9,8},{10,11... | collective-permute-start | bytes 589832 | tf_op jit(solution)/shard_map/ppermute | solution.py:445
  54.2 8.5 %collective-permute-start.11 = (bf16[32,3072]{1,0:T(8,128)(2,1)S(1)}, bf16[32,3072]{1,0:T(8,128)(2,1)S(1)}, u32[]{:S(2)}, u32[]{:S(2)}) collective-permute-start(bf16[32,3072]{1,0:T(8,128)(2,1)S(1)} %add_convert_fusion.2), channel_id=1, source_target_pairs={{0,2},{1,3},{2,6},{3,7},{4,0},{5,1},{6,4},{7,5},{8,10},{9,11},{10,... | collective-permute-start | bytes 589832 | tf_op jit(solution)/shard_map/ppermute | solution.py:439
  56.4 6.1 %collective-permute-start.16 = (bf16[32,3072]{1,0:T(8,128)(2,1)S(1)}, bf16[32,3072]{1,0:T(8,128)(2,1)S(1)}, u32[]{:S(2)}, u32[]{:S(2)}) collective-permute-start(bf16[32,3072]{1,0:T(8,128)(2,1)S(1)} %get-tuple-element.70), channel_id=1, source_target_pairs={{0,1},{1,0},{2,3},{3,2},{4,5},{5,4},{6,7},{7,6},{8,9},{9,8},{10,11... | collective-permute-start | bytes 589832 | tf_op jit(solution)/shard_map/ppermute | solution.py:445
  59.3 7.3 %collective-permute-start.15 = (bf16[32,3072]{1,0:T(8,128)(2,1)S(1)}, bf16[32,3072]{1,0:T(8,128)(2,1)S(1)}, u32[]{:S(2)}, u32[]{:S(2)}) collective-permute-start(bf16[32,3072]{1,0:T(8,128)(2,1)S(1)} %add_convert_fusion), channel_id=1, source_target_pairs={{2,0},{3,1},{6,2},{7,3},{0,4},{1,5},{4,6},{5,7},{10,8},{11,9},{14,... | collective-permute-start | bytes 589832 | tf_op jit(solution)/shard_map/ppermute | solution.py:442
  67.3 1.4 %collective-permute-start.17 = (bf16[1,16,3072]{2,1,0:T(8,128)(2,1)S(1)}, bf16[1,16,3072]{2,1,0:T(8,128)(2,1)S(1)}, u32[]{:S(2)}, u32[]{:S(2)}) collective-permute-start(bf16[1,16,3072]{2,1,0:T(8,128)(2,1)S(1)} %get-tuple-element.72), channel_id=1, source_target_pairs={{0,8},{8,0},{1,9},{9,1},{2,10},{10,2},{3,11},{11,3},{4,12},{12,4},... | collective-permute-start | bytes 294920 | tf_op jit(solution)/shard_map/ppermute | solution.py:582

commit v7 on v6

--- a/solution.py
+++ b/solution.py
@@ -315,13 +315,8 @@
 
 
 def dot_pieces(left_ref, down, piece_refs, across):
-    value, start = None, 0
-    for ref in piece_refs:
-        deep = slice(start, start + ref.shape[0])
-        term = jnp.dot(left_ref[down, deep], ref[:, across], preferred_element_type=F32)
-        value = term if value is None else value + term
-        start = deep.stop
-    return value
+    right = jnp.concatenate([ref[:, across] for ref in piece_refs], axis=0)
+    return jnp.dot(left_ref[down, :], right, preferred_element_type=F32)
 
 
 def down_own(info, mixed, mine, later, spans):
@@ -357,7 +352,7 @@
     depth = mixed.shape[1]
     width = partial.shape[1]
     total = sum(rows for rows, _ in outs)
-    tile = tile_of(width, 1024)
+    tile = tile_of(width, 3072)
 
     runs, start = [], 0
     for index, (rows, _) in enumerate(outs):

time: 69.5 us -> 69.3 us (level)
  Pallas kernels: 26.7 us -> 26 us
where the time goes in v7:
time: 69.3 us; the launch traced here: 69.1 us
  Pallas kernels  26 us (38%)
  starting transfers between devices  25.3 us (37%)
  waiting for transfers between devices  15.5 us (22%)
  other arithmetic  1.1 us (2%)
  local copies, waits for them, and re-layouts  0.93 us (1%)
    ppermute x7, starting transfers between devices, cross(): return lax.ppermute(value, 'tp', self.pairs)  9.77 us
    ppermute x3, starting transfers between devices, up(): return lax.ppermute(value, 'tp', self.upward)  7.93 us
    ppermute x3, starting transfers between devices, down(): return lax.ppermute(value, 'tp', self.downward)  6.4 us
    ppermute x7, waiting for transfers between devices, cross(): return lax.ppermute(value, 'tp', self.pairs)  6.21 us
    pallas_call x1, Pallas kernels, up_early(): pl.pallas_call(kernel, out_shape=(pltpu.VMEM((total, width), BF16), pltpu...  5.94 us
    pallas_call x1, Pallas kernels, fetch(): pl.pallas_call(kernel, out_shape=pltpu.VMEM((count, weight.shape[1]), wei...  4.34 us
    ppermute x3, waiting for transfers between devices, down(): return lax.ppermute(value, 'tp', self.downward)  4.21 us
    pallas_call x1, Pallas kernels, down_own(): pl.pallas_call(kernel, out_shape=(pltpu.VMEM((total, width), F32), *shape...  3.52 us
  transfers between devices with their start and end apart: 18, of which 11 were waited for; matrix products, arithmetic and copies ran while one was open for 2% of the time, Pallas kernels for 30%

profile of v7, /device:TPU:0, one launch (start us, length us, event | category | flops | bytes accessed | tf_op | source)
XLA Modules:
  0.0 69.1 jit_solution(11472844358496306241)
XLA Ops:
  1.8 3.0 %collective-permute-start.2 = (bf16[32,3072]{1,0:T(8,128)(2,1)S(1)}, bf16[32,3072]{1,0:T(8,128)(2,1)S(1)}, u32[]{:S(2)}, u32[]{:S(2)}) collective-permute-start(bf16[32,3072]{1,0:T(8,128)(2,1)S(1)} %bitcast.12), channel_id=1, source_target_pairs={{0,2},{1,3},{2,6},{3,7},{4,0},{5,1},{6,4},{7,5},{8,10},{9,11},{10,... | collective-permute-start | bytes 589832 | tf_op jit(solution)/shard_map/ppermute | solution.py:434
  4.8 1.5 %collective-permute-start.1 = (bf16[32,3072]{1,0:T(8,128)(2,1)S(1)}, bf16[32,3072]{1,0:T(8,128)(2,1)S(1)}, u32[]{:S(2)}, u32[]{:S(2)}) collective-permute-start(bf16[32,3072]{1,0:T(8,128)(2,1)S(1)} %bitcast.13), channel_id=1, source_target_pairs={{0,1},{1,0},{2,3},{3,2},{4,5},{5,4},{6,7},{7,6},{8,9},{9,8},{10,11... | collective-permute-start | bytes 589832 | tf_op jit(solution)/shard_map/ppermute | solution.py:440
  6.3 4.3 %shard_map.73.refs_5_.refs_2_.upper_ref = bf16[1536,3072]{1,0:T(8,128)(2,1)S(1)} custom-call(s32[3]{0:T(128)S(1)} %pad_add_fusion.info_ref, bf16[3072,3072]{1,0:T(8,128)(2,1)} %refs_6_.1), custom_call_target="tpu_custom_call" | custom-call | bytes 18874368 | tf_op jit(solution)/shard_map/pallas_call | solution.py:71
  11.4 2.6 %collective-permute-start.3 = (bf16[32,3072]{1,0:T(8,128)(2,1)S(1)}, bf16[32,3072]{1,0:T(8,128)(2,1)S(1)}, u32[]{:S(2)}, u32[]{:S(2)}) collective-permute-start(bf16[32,3072]{1,0:T(8,128)(2,1)S(1)} %collective-permute-done.2.refs_1_), channel_id=1, source_target_pairs={{0,2},{1,3},{2,6},{3,7},{4,0},{5,1},{6,4},{7,5},{8,10},{9,11},{10,... | collective-permute-start | bytes 589832 | tf_op jit(solution)/shard_map/ppermute | solution.py:434
  14.0 1.5 %collective-permute-start.4 = (bf16[32,3072]{1,0:T(8,128)(2,1)S(1)}, bf16[32,3072]{1,0:T(8,128)(2,1)S(1)}, u32[]{:S(2)}, u32[]{:S(2)}) collective-permute-start(bf16[32,3072]{1,0:T(8,128)(2,1)S(1)} %collective-permute-done.2.refs_1_), channel_id=1, source_target_pairs={{0,1},{1,0},{2,3},{3,2},{4,5},{5,4},{6,7},{7,6},{8,9},{9,8},{10,11... | collective-permute-start | bytes 589832 | tf_op jit(solution)/shard_map/ppermute | solution.py:440
  15.6 2.7 %collective-permute-done.3.refs_2_ = bf16[32,3072]{1,0:T(8,128)(2,1)S(1)} collective-permute-done((bf16[32,3072]{1,0:T(8,128)(2,1)S(1)}, bf16[32,3072]{1,0:T(8,128)(2,1)S(1)}, u32[]{:S(2)}, u32[]{:S(2)}) %collective-permute-start.3) | collective-permute-done | bytes 196640 | tf_op jit(solution)/shard_map/ppermute | solution.py:434
  18.3 1.2 %collective-permute-start.6 = (bf16[64,3072]{1,0:T(8,128)(2,1)S(1)}, bf16[64,3072]{1,0:T(8,128)(2,1)S(1)}, u32[]{:S(2)}, u32[]{:S(2)}) collective-permute-start(bf16[64,3072]{1,0:T(8,128)(2,1)S(1)} %shard_map.74), channel_id=1, source_target_pairs={{2,0},{3,1},{6,2},{7,3},{0,4},{1,5},{4,6},{5,7},{10,8},{11,9},{14,... | collective-permute-start | bytes 1179656 | tf_op jit(solution)/shard_map/ppermute | solution.py:437
  19.6 1.5 %collective-permute-start.5 = (bf16[32,3072]{1,0:T(8,128)(2,1)S(1)}, bf16[32,3072]{1,0:T(8,128)(2,1)S(1)}, u32[]{:S(2)}, u32[]{:S(2)}) collective-permute-start(bf16[32,3072]{1,0:T(8,128)(2,1)S(1)} %collective-permute-done.3.refs_2_), channel_id=1, source_target_pairs={{0,1},{1,0},{2,3},{3,2},{4,5},{5,4},{6,7},{7,6},{8,9},{9,8},{10,11... | collective-permute-start | bytes 589832 | tf_op jit(solution)/shard_map/ppermute | solution.py:440
  21.1 5.9 %shard_map.75 = (bf16[160,1536]{1,0:T(8,128)(2,1)S(1)}, f32[160,1536]{1,0:T(8,128)S(1)}, bf16[1536,3072]{1,0:T(8,128)(2,1)S(1)}) custom-call(s32[3]{0:T(128)S(1)} %pad_add_fusion.info_ref, bf16[32,3072]{1,0:T(8,128)(2,1)S(1)} %bitcast.15, bf16[32,3072]{1,0:T(8,128)(2,1)S(1)} %collective-permute-done.2.refs_1_, ...), custom_call_target="tpu_custom_call" | custom-call | flops 3019898880 | bytes 9437184 | tf_op jit(solution)/shard_map/pallas_call | solution.py:148
  27.6 2.4 %shard_map.76 = (bf16[96,1536]{1,0:T(8,128)(2,1)S(1)}, bf16[96,3072]{1,0:T(8,128)(2,1)S(1)}, bf16[512,3072]{1,0:T(8,128)(2,1)S(1)}) custom-call(s32[3]{0:T(128)S(1)} %pad_add_fusion.info_ref, bf16[32,3072]{1,0:T(8,128)(2,1)S(1)} %collective-permute-done.5.refs_0_, bf16[64,3072]{1,0:T(8,128)(2,1)S(1)} %collective-permute-done.6.refs_1_, ...), custom_call_target="tpu_custom_call" | custom-call | flops 905969664 | bytes 9437184 | tf_op jit(solution)/shard_map/pallas_call | solution.py:211
  30.1 2.4 %shard_map.77 = (f32[96,1536]{1,0:T(8,128)S(1)}, bf16[512,3072]{1,0:T(8,128)(2,1)S(1)}) custom-call(s32[3]{0:T(128)S(1)} %pad_add_fusion.info_ref, bf16[96,3072]{1,0:T(8,128)(2,1)S(1)} %get-tuple-element.48.tokens_ref, bf16[1536,3072]{1,0:T(8,128)(2,1)S(1)} %shard_map.73.refs_5_.refs_2_.upper_ref, ...), custom_call_target="tpu_custom_call" | custom-call | flops 905969664 | bytes 9437184 | tf_op jit(solution)/shard_map/pallas_call | solution.py:234
  32.6 3.4 %shard_map.78 = (bf16[256,1536]{1,0:T(8,128)(2,1)S(1)}, bf16[512,3072]{1,0:T(8,128)(2,1)S(1)}, bf16[512,3072]{1,0:T(8,128)(2,1)S(1)}) custom-call(s32[3]{0:T(128)S(1)} %pad_add_fusion.info_ref, f32[160,1536]{1,0:T(8,128)S(1)} %get-tuple-element.45.refs_0_, f32[96,1536]{1,0:T(8,128)S(1)} %get-tuple-element.49.refs_1_, ...), custom_call_target="tpu_custom_call" | custom-call | flops 23592960 | bytes 3145728 | tf_op jit(solution)/shard_map/pallas_call | solution.py:305
  36.6 3.5 %shard_map.79 = (f32[256,3072]{1,0:T(8,128)S(1)}, bf16[1024,3072]{1,0:T(8,128)(2,1)S(1)}) custom-call(s32[3]{0:T(128)S(1)} %pad_add_fusion.info_ref, bf16[256,1536]{1,0:T(8,128)(2,1)S(1)} %get-tuple-element.52.mixed_ref, bf16[512,3072]{1,0:T(8,128)(2,1)S(1)} %get-tuple-element.54.refs_0_, bf16[512,3072]{1,0:T(8,128)(2,1)S(1)} %get-tuple-element.55.refs_1_, ...), custom_call_target="tpu_custom_call" | custom-call | flops 2415919104 | bytes 9437184 | tf_op jit(solution)/shard_map/pallas_call | solution.py:339
  40.1 1.6 %shard_map.80 = (bf16[32,3072]{1,0:T(8,128)(2,1)S(1)}, f32[32,3072]{1,0:T(8,128)S(1)}, bf16[32,3072]{1,0:T(8,128)(2,1)S(1)}) custom-call(bf16[256,1536]{1,0:T(8,128)(2,1)S(1)} %collective-permute-done.9.mixed_ref, bf16[512,3072]{1,0:T(8,128)(2,1)S(1)} %get-tuple-element.53.refs_0_, bf16[1024,3072]{1,0:T(8,128)(2,1)S(1)} %get-tuple-element.57.refs_1_, ...), custom_call_target="tpu_custom_call" | custom-call | flops 905969664 | bytes 9437184 | tf_op jit(solution)/shard_map/pallas_call | solution.py:380
  43.0 1.7 %shard_map.81 = (f32[32,3072]{1,0:T(8,128)S(1)}, f32[32,3072]{1,0:T(8,128)S(1)}, f32[32,3072]{1,0:T(8,128)S(1)}, bf16[32,3072]{1,0:T(8,128)(2,1)S(1)}, bf16[32,3072]{1,0:T(8,128)(2,1)S(1)}) custom-call(bf16[256,1536]{1,0:T(8,128)(2,1)S(1)} %collective-permute-done.9.mixed_ref, bf16[512,3072]{1,0:T(8,128)(2,1)S(1)} %get-tuple-element.53.refs_0_, ...), custom_call_target="tpu_custom_call" | custom-call | flops 1509949440 | bytes 9437184 | tf_op jit(solution)/shard_map/pallas_call | solution.py:380
  45.7 4.0 %collective-permute-done.12 = bf16[32,3072]{1,0:T(8,128)(2,1)S(1)} collective-permute-done((bf16[32,3072]{1,0:T(8,128)(2,1)S(1)}, bf16[32,3072]{1,0:T(8,128)(2,1)S(1)}, u32[]{:S(2)}, u32[]{:S(2)}) %collective-permute-start.12) | collective-permute-done | bytes 196640 | tf_op jit(solution)/shard_map/ppermute | solution.py:440
  49.7 2.6 %collective-permute-start.13 = (bf16[32,3072]{1,0:T(8,128)(2,1)S(1)}, bf16[32,3072]{1,0:T(8,128)(2,1)S(1)}, u32[]{:S(2)}, u32[]{:S(2)}) collective-permute-start(bf16[32,3072]{1,0:T(8,128)(2,1)S(1)} %add_convert_fusion.1), channel_id=1, source_target_pairs={{2,0},{3,1},{6,2},{7,3},{0,4},{1,5},{4,6},{5,7},{10,8},{11,9},{14,... | collective-permute-start | bytes 589832 | tf_op jit(solution)/shard_map/ppermute | solution.py:437
  52.3 1.5 %collective-permute-start.14 = (bf16[32,3072]{1,0:T(8,128)(2,1)S(1)}, bf16[32,3072]{1,0:T(8,128)(2,1)S(1)}, u32[]{:S(2)}, u32[]{:S(2)}) collective-permute-start(bf16[32,3072]{1,0:T(8,128)(2,1)S(1)} %get-tuple-element.68), channel_id=1, source_target_pairs={{0,1},{1,0},{2,3},{3,2},{4,5},{5,4},{6,7},{7,6},{8,9},{9,8},{10,11... | collective-permute-start | bytes 589832 | tf_op jit(solution)/shard_map/ppermute | solution.py:440
  53.9 2.3 %collective-permute-start.11 = (bf16[32,3072]{1,0:T(8,128)(2,1)S(1)}, bf16[32,3072]{1,0:T(8,128)(2,1)S(1)}, u32[]{:S(2)}, u32[]{:S(2)}) collective-permute-start(bf16[32,3072]{1,0:T(8,128)(2,1)S(1)} %add_convert_fusion.2), channel_id=1, source_target_pairs={{0,2},{1,3},{2,6},{3,7},{4,0},{5,1},{6,4},{7,5},{8,10},{9,11},{10,... | collective-permute-start | bytes 589832 | tf_op jit(solution)/shard_map/ppermute | solution.py:434
  56.2 1.5 %collective-permute-start.16 = (bf16[32,3072]{1,0:T(8,128)(2,1)S(1)}, bf16[32,3072]{1,0:T(8,128)(2,1)S(1)}, u32[]{:S(2)}, u32[]{:S(2)}) collective-permute-start(bf16[32,3072]{1,0:T(8,128)(2,1)S(1)} %get-tuple-element.70), channel_id=1, source_target_pairs={{0,1},{1,0},{2,3},{3,2},{4,5},{5,4},{6,7},{7,6},{8,9},{9,8},{10,11... | collective-permute-start | bytes 589832 | tf_op jit(solution)/shard_map/ppermute | solution.py:440
  57.7 1.4 %collective-permute-done.14 = bf16[32,3072]{1,0:T(8,128)(2,1)S(1)} collective-permute-done((bf16[32,3072]{1,0:T(8,128)(2,1)S(1)}, bf16[32,3072]{1,0:T(8,128)(2,1)S(1)}, u32[]{:S(2)}, u32[]{:S(2)}) %collective-permute-start.14) | collective-permute-done | bytes 196640 | tf_op jit(solution)/shard_map/ppermute | solution.py:440
  59.2 2.5 %collective-permute-start.15 = (bf16[32,3072]{1,0:T(8,128)(2,1)S(1)}, bf16[32,3072]{1,0:T(8,128)(2,1)S(1)}, u32[]{:S(2)}, u32[]{:S(2)}) collective-permute-start(bf16[32,3072]{1,0:T(8,128)(2,1)S(1)} %add_convert_fusion), channel_id=1, source_target_pairs={{2,0},{3,1},{6,2},{7,3},{0,4},{1,5},{4,6},{5,7},{10,8},{11,9},{14,... | collective-permute-start | bytes 589832 | tf_op jit(solution)/shard_map/ppermute | solution.py:437
  62.6 3.7 %collective-permute-done.15 = bf16[32,3072]{1,0:T(8,128)(2,1)S(1)} collective-permute-done((bf16[32,3072]{1,0:T(8,128)(2,1)S(1)}, bf16[32,3072]{1,0:T(8,128)(2,1)S(1)}, u32[]{:S(2)}, u32[]{:S(2)}) %collective-permute-start.15) | collective-permute-done | bytes 196640 | tf_op jit(solution)/shard_map/ppermute | solution.py:437
  67.1 1.3 %collective-permute-done.17 = bf16[1,16,3072]{2,1,0:T(8,128)(2,1)S(1)} collective-permute-done((bf16[1,16,3072]{2,1,0:T(8,128)(2,1)S(1)}, bf16[1,16,3072]{2,1,0:T(8,128)(2,1)S(1)}, u32[]{:S(2)}, u32[]{:S(2)}) %collective-permute-start.17) | collective-permute-done | bytes 98336 | tf_op jit(solution)/shard_map/ppermute | solution.py:577
  (39 shorter events, 8.4 us)
Async XLA Ops:
  0.0 1.7 %collective-permute-start = (bf16[16,6144]{1,0:T(8,128)(2,1)}, bf16[16,6144]{1,0:T(8,128)(2,1)S(1)}, u32[]{:S(2)}, u32[]{:S(2)}) collective-permute-start(bf16[16,6144]{1,0:T(8,128)(2,1)} %bitcast.19), channel_id=1, source_target_pairs={{0,8},{8,0},{1,9},{9,1},{2,10},{10,2},{3,11},{11,3},{4,12},{12,4},... | collective-permute-start | bytes 589832 | tf_op jit(solution)/shard_map/ppermute | solution.py:530
  1.8 9.2 %collective-permute-start.2 = (bf16[32,3072]{1,0:T(8,128)(2,1)S(1)}, bf16[32,3072]{1,0:T(8,128)(2,1)S(1)}, u32[]{:S(2)}, u32[]{:S(2)}) collective-permute-start(bf16[32,3072]{1,0:T(8,128)(2,1)S(1)} %bitcast.12), channel_id=1, source_target_pairs={{0,2},{1,3},{2,6},{3,7},{4,0},{5,1},{6,4},{7,5},{8,10},{9,11},{10,... | collective-permute-start | bytes 589832 | tf_op jit(solution)/shard_map/ppermute | solution.py:434
  4.8 6.7 %collective-permute-start.1 = (bf16[32,3072]{1,0:T(8,128)(2,1)S(1)}, bf16[32,3072]{1,0:T(8,128)(2,1)S(1)}, u32[]{:S(2)}, u32[]{:S(2)}) collective-permute-start(bf16[32,3072]{1,0:T(8,128)(2,1)S(1)} %bitcast.13), channel_id=1, source_target_pairs={{0,1},{1,0},{2,3},{3,2},{4,5},{5,4},{6,7},{7,6},{8,9},{9,8},{10,11... | collective-permute-start | bytes 589832 | tf_op jit(solution)/shard_map/ppermute | solution.py:440
  11.4 6.9 %collective-permute-start.3 = (bf16[32,3072]{1,0:T(8,128)(2,1)S(1)}, bf16[32,3072]{1,0:T(8,128)(2,1)S(1)}, u32[]{:S(2)}, u32[]{:S(2)}) collective-permute-start(bf16[32,3072]{1,0:T(8,128)(2,1)S(1)} %collective-permute-done.2.refs_1_), channel_id=1, source_target_pairs={{0,2},{1,3},{2,6},{3,7},{4,0},{5,1},{6,4},{7,5},{8,10},{9,11},{10,... | collective-permute-start | bytes 589832 | tf_op jit(solution)/shard_map/ppermute | solution.py:434
  14.0 7.1 %collective-permute-start.4 = (bf16[32,3072]{1,0:T(8,128)(2,1)S(1)}, bf16[32,3072]{1,0:T(8,128)(2,1)S(1)}, u32[]{:S(2)}, u32[]{:S(2)}) collective-permute-start(bf16[32,3072]{1,0:T(8,128)(2,1)S(1)} %collective-permute-done.2.refs_1_), channel_id=1, source_target_pairs={{0,1},{1,0},{2,3},{3,2},{4,5},{5,4},{6,7},{7,6},{8,9},{9,8},{10,11... | collective-permute-start | bytes 589832 | tf_op jit(solution)/shard_map/ppermute | solution.py:440
  18.3 9.3 %collective-permute-start.6 = (bf16[64,3072]{1,0:T(8,128)(2,1)S(1)}, bf16[64,3072]{1,0:T(8,128)(2,1)S(1)}, u32[]{:S(2)}, u32[]{:S(2)}) collective-permute-start(bf16[64,3072]{1,0:T(8,128)(2,1)S(1)} %shard_map.74), channel_id=1, source_target_pairs={{2,0},{3,1},{6,2},{7,3},{0,4},{1,5},{4,6},{5,7},{10,8},{11,9},{14,... | collective-permute-start | bytes 1179656 | tf_op jit(solution)/shard_map/ppermute | solution.py:437
  19.6 7.6 %collective-permute-start.5 = (bf16[32,3072]{1,0:T(8,128)(2,1)S(1)}, bf16[32,3072]{1,0:T(8,128)(2,1)S(1)}, u32[]{:S(2)}, u32[]{:S(2)}) collective-permute-start(bf16[32,3072]{1,0:T(8,128)(2,1)S(1)} %collective-permute-done.3.refs_2_), channel_id=1, source_target_pairs={{0,1},{1,0},{2,3},{3,2},{4,5},{5,4},{6,7},{7,6},{8,9},{9,8},{10,11... | collective-permute-start | bytes 589832 | tf_op jit(solution)/shard_map/ppermute | solution.py:440
  27.0 5.6 %collective-permute-start.7 = (bf16[160,1536]{1,0:T(8,128)(2,1)S(1)}, bf16[160,1536]{1,0:T(8,128)(2,1)S(1)}, u32[]{:S(2)}, u32[]{:S(2)}) collective-permute-start(bf16[160,1536]{1,0:T(8,128)(2,1)S(1)} %get-tuple-element.50), channel_id=1, source_target_pairs={{0,8},{8,0},{1,9},{9,1},{2,10},{10,2},{3,11},{11,3},{4,12},{12,4},... | collective-permute-start | bytes 1474568 | tf_op jit(solution)/shard_map/ppermute | solution.py:546
  30.0 2.6 %collective-permute-start.8 = (bf16[96,1536]{1,0:T(8,128)(2,1)S(1)}, bf16[96,1536]{1,0:T(8,128)(2,1)S(1)}, u32[]{:S(2)}, u32[]{:S(2)}) collective-permute-start(bf16[96,1536]{1,0:T(8,128)(2,1)S(1)} %get-tuple-element.51), channel_id=1, source_target_pairs={{0,8},{8,0},{1,9},{9,1},{2,10},{10,2},{3,11},{11,3},{4,12},{12,4},... | collective-permute-start | bytes 884744 | tf_op jit(solution)/shard_map/ppermute | solution.py:546
  30.1 2.5 %copy-start = (f32[3,3,3072]{2,1,0:T(4,128)S(1)}, f32[3,3,3072]{2,1,0:T(4,128)}, u32[]{:S(2)}) copy-start(f32[3,3,3072]{2,1,0:T(4,128)} %refs_5_.1) | copy-start | bytes 331780
  30.1 2.5 %copy-start.2 = (f32[3072]{0:T(1024)S(1)}, f32[3072]{0:T(1024)}, u32[]{:S(2)}) copy-start(f32[3072]{0:T(1024)} %param.9) | copy-start | bytes 36868
  30.1 2.5 %copy-start.3 = (f32[3072]{0:T(1024)S(1)}, f32[3072]{0:T(1024)}, u32[]{:S(2)}) copy-start(f32[3072]{0:T(1024)} %param.11) | copy-start | bytes 36868
  36.1 4.1 %collective-permute-start.9 = (bf16[256,1536]{1,0:T(8,128)(2,1)S(1)}, bf16[256,1536]{1,0:T(8,128)(2,1)S(1)}, u32[]{:S(2)}, u32[]{:S(2)}) collective-permute-start(bf16[256,1536]{1,0:T(8,128)(2,1)S(1)} %get-tuple-element.52.mixed_ref), channel_id=1, source_target_pairs={{0,8},{8,0},{1,9},{9,1},{2,10},{10,2},{3,11},{11,3},{4,12},{12,4},... | collective-permute-start | bytes 2359304 | tf_op jit(solution)/shard_map/ppermute | solution.py:561
  41.8 24.7 %copy-start.1 = (f32[6144]{0:T(1024)S(1)}, f32[6144]{0:T(1024)}, u32[]{:S(2)}) copy-start(f32[6144]{0:T(1024)} %param.13) | copy-start | bytes 73732
  41.8 7.8 %collective-permute-start.12 = (bf16[32,3072]{1,0:T(8,128)(2,1)S(1)}, bf16[32,3072]{1,0:T(8,128)(2,1)S(1)}, u32[]{:S(2)}, u32[]{:S(2)}) collective-permute-start(bf16[32,3072]{1,0:T(8,128)(2,1)S(1)} %get-tuple-element.66), channel_id=1, source_target_pairs={{0,1},{1,0},{2,3},{3,2},{4,5},{5,4},{6,7},{7,6},{8,9},{9,8},{10,11... | collective-permute-start | bytes 589832 | tf_op jit(solution)/shard_map/ppermute | solution.py:440
  44.7 9.1 %collective-permute-start.10 = (bf16[32,3072]{1,0:T(8,128)(2,1)S(1)}, bf16[32,3072]{1,0:T(8,128)(2,1)S(1)}, u32[]{:S(2)}, u32[]{:S(2)}) collective-permute-start(bf16[32,3072]{1,0:T(8,128)(2,1)S(1)} %get-tuple-element.63), channel_id=1, source_target_pairs={{0,1},{1,0},{2,3},{3,2},{4,5},{5,4},{6,7},{7,6},{8,9},{9,8},{10,11... | collective-permute-start | bytes 589832 | tf_op jit(solution)/shard_map/ppermute | solution.py:440
  49.7 9.4 %collective-permute-start.13 = (bf16[32,3072]{1,0:T(8,128)(2,1)S(1)}, bf16[32,3072]{1,0:T(8,128)(2,1)S(1)}, u32[]{:S(2)}, u32[]{:S(2)}) collective-permute-start(bf16[32,3072]{1,0:T(8,128)(2,1)S(1)} %add_convert_fusion.1), channel_id=1, source_target_pairs={{2,0},{3,1},{6,2},{7,3},{0,4},{1,5},{4,6},{5,7},{10,8},{11,9},{14,... | collective-permute-start | bytes 589832 | tf_op jit(solution)/shard_map/ppermute | solution.py:437
  52.3 6.8 %collective-permute-start.14 = (bf16[32,3072]{1,0:T(8,128)(2,1)S(1)}, bf16[32,3072]{1,0:T(8,128)(2,1)S(1)}, u32[]{:S(2)}, u32[]{:S(2)}) collective-permute-start(bf16[32,3072]{1,0:T(8,128)(2,1)S(1)} %get-tuple-element.68), channel_id=1, source_target_pairs={{0,1},{1,0},{2,3},{3,2},{4,5},{5,4},{6,7},{7,6},{8,9},{9,8},{10,11... | collective-permute-start | bytes 589832 | tf_op jit(solution)/shard_map/ppermute | solution.py:440
  53.9 8.7 %collective-permute-start.11 = (bf16[32,3072]{1,0:T(8,128)(2,1)S(1)}, bf16[32,3072]{1,0:T(8,128)(2,1)S(1)}, u32[]{:S(2)}, u32[]{:S(2)}) collective-permute-start(bf16[32,3072]{1,0:T(8,128)(2,1)S(1)} %add_convert_fusion.2), channel_id=1, source_target_pairs={{0,2},{1,3},{2,6},{3,7},{4,0},{5,1},{6,4},{7,5},{8,10},{9,11},{10,... | collective-permute-start | bytes 589832 | tf_op jit(solution)/shard_map/ppermute | solution.py:434
  56.2 6.0 %collective-permute-start.16 = (bf16[32,3072]{1,0:T(8,128)(2,1)S(1)}, bf16[32,3072]{1,0:T(8,128)(2,1)S(1)}, u32[]{:S(2)}, u32[]{:S(2)}) collective-permute-start(bf16[32,3072]{1,0:T(8,128)(2,1)S(1)} %get-tuple-element.70), channel_id=1, source_target_pairs={{0,1},{1,0},{2,3},{3,2},{4,5},{5,4},{6,7},{7,6},{8,9},{9,8},{10,11... | collective-permute-start | bytes 589832 | tf_op jit(solution)/shard_map/ppermute | solution.py:440
  59.2 7.2 %collective-permute-start.15 = (bf16[32,3072]{1,0:T(8,128)(2,1)S(1)}, bf16[32,3072]{1,0:T(8,128)(2,1)S(1)}, u32[]{:S(2)}, u32[]{:S(2)}) collective-permute-start(bf16[32,3072]{1,0:T(8,128)(2,1)S(1)} %add_convert_fusion), channel_id=1, source_target_pairs={{2,0},{3,1},{6,2},{7,3},{0,4},{1,5},{4,6},{5,7},{10,8},{11,9},{14,... | collective-permute-start | bytes 589832 | tf_op jit(solution)/shard_map/ppermute | solution.py:437
  67.0 1.4 %collective-permute-start.17 = (bf16[1,16,3072]{2,1,0:T(8,128)(2,1)S(1)}, bf16[1,16,3072]{2,1,0:T(8,128)(2,1)S(1)}, u32[]{:S(2)}, u32[]{:S(2)}) collective-permute-start(bf16[1,16,3072]{2,1,0:T(8,128)(2,1)S(1)} %get-tuple-element.72), channel_id=1, source_target_pairs={{0,8},{8,0},{1,9},{9,1},{2,10},{10,2},{3,11},{11,3},{4,12},{12,4},... | collective-permute-start | bytes 294920 | tf_op jit(solution)/shard_map/ppermute | solution.py:577

commit v8 on v7

--- a/solution.py
+++ b/solution.py
@@ -540,6 +540,7 @@
     early_other, early_own, lower = up_early(info, early, upper, up_weight)
     third = units_half // 3 // 32 * 32
     rest = units_half - 2 * third
+    less = third * 3 // 4 // 32 * 32
     late_other, late_tokens, mine_a = up_other(info, late, upper, lower, down_weight, [(0, 0, third)])
     late_own, mine_b = up_own(info, late_tokens, upper, lower, down_weight, [(0, third, third)])
     own = [early_own, late_own]
@@ -552,7 +553,7 @@
         conv_weight,
         conv_bias.reshape(1, units),
         down_weight,
-        [(0, 2 * third, rest), (1, 0, third)],
+        [(0, 2 * third, rest), (1, 0, less)],
         groups,
         links,
         rows,
@@ -560,7 +561,7 @@
     )
     mixed_received = lax.ppermute(mixed, "sp", swap)
     product, theirs_b = down_own(
-        info, mixed, [*mine_a, *mine_b, mine_c], down_weight, [(1, third, units_half - third)]
+        info, mixed, [*mine_a, *mine_b, mine_c], down_weight, [(1, less, units_half - less)]
     )
     theirs = [theirs_a, *theirs_b]
 

time: 69.3 us -> 69.1 us (level)
  no operation moved by 1% of the time
where the time goes in v8:
time: 69.1 us; the launch traced here: 69 us
  Pallas kernels  25.9 us (37%)
  starting transfers between devices  25.3 us (37%)
  waiting for transfers between devices  15.5 us (22%)
  other arithmetic  1.1 us (2%)
  local copies, waits for them, and re-layouts  0.93 us (1%)
    ppermute x7, starting transfers between devices, cross(): return lax.ppermute(value, 'tp', self.pairs)  9.77 us
    ppermute x3, starting transfers between devices, up(): return lax.ppermute(value, 'tp', self.upward)  7.94 us
    ppermute x3, starting transfers between devices, down(): return lax.ppermute(value, 'tp', self.downward)  6.4 us
    ppermute x7, waiting for transfers between devices, cross(): return lax.ppermute(value, 'tp', self.pairs)  6.21 us
    pallas_call x1, Pallas kernels, up_early(): pl.pallas_call(kernel, out_shape=(pltpu.VMEM((total, width), BF16), pltpu...  5.94 us
    pallas_call x1, Pallas kernels, fetch(): pl.pallas_call(kernel, out_shape=pltpu.VMEM((count, weight.shape[1]), wei...  4.34 us
    ppermute x3, waiting for transfers between devices, down(): return lax.ppermute(value, 'tp', self.downward)  4.21 us
    pallas_call x1, Pallas kernels, down_own(): pl.pallas_call(kernel, out_shape=(pltpu.VMEM((total, width), F32), *shape...  3.64 us
  transfers between devices with their start and end apart: 18, of which 11 were waited for; matrix products, arithmetic and copies ran while one was open for 2% of the time, Pallas kernels for 30%

profile of v8, /device:TPU:0, one launch (start us, length us, event | category | flops | bytes accessed | tf_op | source)
XLA Modules:
  0.0 69.0 jit_solution(8924887195118923027)
XLA Ops:
  1.8 3.0 %collective-permute-start.2 = (bf16[32,3072]{1,0:T(8,128)(2,1)S(1)}, bf16[32,3072]{1,0:T(8,128)(2,1)S(1)}, u32[]{:S(2)}, u32[]{:S(2)}) collective-permute-start(bf16[32,3072]{1,0:T(8,128)(2,1)S(1)} %bitcast.12), channel_id=1, source_target_pairs={{0,2},{1,3},{2,6},{3,7},{4,0},{5,1},{6,4},{7,5},{8,10},{9,11},{10,... | collective-permute-start | bytes 589832 | tf_op jit(solution)/shard_map/ppermute | solution.py:434
  4.8 1.5 %collective-permute-start.1 = (bf16[32,3072]{1,0:T(8,128)(2,1)S(1)}, bf16[32,3072]{1,0:T(8,128)(2,1)S(1)}, u32[]{:S(2)}, u32[]{:S(2)}) collective-permute-start(bf16[32,3072]{1,0:T(8,128)(2,1)S(1)} %bitcast.13), channel_id=1, source_target_pairs={{0,1},{1,0},{2,3},{3,2},{4,5},{5,4},{6,7},{7,6},{8,9},{9,8},{10,11... | collective-permute-start | bytes 589832 | tf_op jit(solution)/shard_map/ppermute | solution.py:440
  6.3 4.3 %shard_map.73.refs_5_.refs_2_.upper_ref = bf16[1536,3072]{1,0:T(8,128)(2,1)S(1)} custom-call(s32[3]{0:T(128)S(1)} %pad_add_fusion.info_ref, bf16[3072,3072]{1,0:T(8,128)(2,1)} %refs_6_.1), custom_call_target="tpu_custom_call" | custom-call | bytes 18874368 | tf_op jit(solution)/shard_map/pallas_call | solution.py:71
  11.4 2.6 %collective-permute-start.3 = (bf16[32,3072]{1,0:T(8,128)(2,1)S(1)}, bf16[32,3072]{1,0:T(8,128)(2,1)S(1)}, u32[]{:S(2)}, u32[]{:S(2)}) collective-permute-start(bf16[32,3072]{1,0:T(8,128)(2,1)S(1)} %collective-permute-done.2.refs_1_), channel_id=1, source_target_pairs={{0,2},{1,3},{2,6},{3,7},{4,0},{5,1},{6,4},{7,5},{8,10},{9,11},{10,... | collective-permute-start | bytes 589832 | tf_op jit(solution)/shard_map/ppermute | solution.py:434
  14.0 1.5 %collective-permute-start.4 = (bf16[32,3072]{1,0:T(8,128)(2,1)S(1)}, bf16[32,3072]{1,0:T(8,128)(2,1)S(1)}, u32[]{:S(2)}, u32[]{:S(2)}) collective-permute-start(bf16[32,3072]{1,0:T(8,128)(2,1)S(1)} %collective-permute-done.2.refs_1_), channel_id=1, source_target_pairs={{0,1},{1,0},{2,3},{3,2},{4,5},{5,4},{6,7},{7,6},{8,9},{9,8},{10,11... | collective-permute-start | bytes 589832 | tf_op jit(solution)/shard_map/ppermute | solution.py:440
  15.6 2.7 %collective-permute-done.3.refs_2_ = bf16[32,3072]{1,0:T(8,128)(2,1)S(1)} collective-permute-done((bf16[32,3072]{1,0:T(8,128)(2,1)S(1)}, bf16[32,3072]{1,0:T(8,128)(2,1)S(1)}, u32[]{:S(2)}, u32[]{:S(2)}) %collective-permute-start.3) | collective-permute-done | bytes 196640 | tf_op jit(solution)/shard_map/ppermute | solution.py:434
  18.3 1.2 %collective-permute-start.6 = (bf16[64,3072]{1,0:T(8,128)(2,1)S(1)}, bf16[64,3072]{1,0:T(8,128)(2,1)S(1)}, u32[]{:S(2)}, u32[]{:S(2)}) collective-permute-start(bf16[64,3072]{1,0:T(8,128)(2,1)S(1)} %shard_map.74), channel_id=1, source_target_pairs={{2,0},{3,1},{6,2},{7,3},{0,4},{1,5},{4,6},{5,7},{10,8},{11,9},{14,... | collective-permute-start | bytes 1179656 | tf_op jit(solution)/shard_map/ppermute | solution.py:437
  19.6 1.5 %collective-permute-start.5 = (bf16[32,3072]{1,0:T(8,128)(2,1)S(1)}, bf16[32,3072]{1,0:T(8,128)(2,1)S(1)}, u32[]{:S(2)}, u32[]{:S(2)}) collective-permute-start(bf16[32,3072]{1,0:T(8,128)(2,1)S(1)} %collective-permute-done.3.refs_2_), channel_id=1, source_target_pairs={{0,1},{1,0},{2,3},{3,2},{4,5},{5,4},{6,7},{7,6},{8,9},{9,8},{10,11... | collective-permute-start | bytes 589832 | tf_op jit(solution)/shard_map/ppermute | solution.py:440
  21.1 5.9 %shard_map.75 = (bf16[160,1536]{1,0:T(8,128)(2,1)S(1)}, f32[160,1536]{1,0:T(8,128)S(1)}, bf16[1536,3072]{1,0:T(8,128)(2,1)S(1)}) custom-call(s32[3]{0:T(128)S(1)} %pad_add_fusion.info_ref, bf16[32,3072]{1,0:T(8,128)(2,1)S(1)} %bitcast.15, bf16[32,3072]{1,0:T(8,128)(2,1)S(1)} %collective-permute-done.2.refs_1_, ...), custom_call_target="tpu_custom_call" | custom-call | flops 3019898880 | bytes 9437184 | tf_op jit(solution)/shard_map/pallas_call | solution.py:148
  27.6 2.4 %shard_map.76 = (bf16[96,1536]{1,0:T(8,128)(2,1)S(1)}, bf16[96,3072]{1,0:T(8,128)(2,1)S(1)}, bf16[512,3072]{1,0:T(8,128)(2,1)S(1)}) custom-call(s32[3]{0:T(128)S(1)} %pad_add_fusion.info_ref, bf16[32,3072]{1,0:T(8,128)(2,1)S(1)} %collective-permute-done.5.refs_0_, bf16[64,3072]{1,0:T(8,128)(2,1)S(1)} %collective-permute-done.6.refs_1_, ...), custom_call_target="tpu_custom_call" | custom-call | flops 905969664 | bytes 9437184 | tf_op jit(solution)/shard_map/pallas_call | solution.py:211
  30.1 2.4 %shard_map.77 = (f32[96,1536]{1,0:T(8,128)S(1)}, bf16[512,3072]{1,0:T(8,128)(2,1)S(1)}) custom-call(s32[3]{0:T(128)S(1)} %pad_add_fusion.info_ref, bf16[96,3072]{1,0:T(8,128)(2,1)S(1)} %get-tuple-element.48.tokens_ref, bf16[1536,3072]{1,0:T(8,128)(2,1)S(1)} %shard_map.73.refs_5_.refs_2_.upper_ref, ...), custom_call_target="tpu_custom_call" | custom-call | flops 905969664 | bytes 9437184 | tf_op jit(solution)/shard_map/pallas_call | solution.py:234
  32.6 3.2 %shard_map.78 = (bf16[256,1536]{1,0:T(8,128)(2,1)S(1)}, bf16[512,3072]{1,0:T(8,128)(2,1)S(1)}, bf16[384,3072]{1,0:T(8,128)(2,1)S(1)}) custom-call(s32[3]{0:T(128)S(1)} %pad_add_fusion.info_ref, f32[160,1536]{1,0:T(8,128)S(1)} %get-tuple-element.45.refs_0_, f32[96,1536]{1,0:T(8,128)S(1)} %get-tuple-element.49.refs_1_, ...), custom_call_target="tpu_custom_call" | custom-call | flops 23592960 | bytes 3145728 | tf_op jit(solution)/shard_map/pallas_call | solution.py:305
  36.3 3.6 %shard_map.79 = (f32[256,3072]{1,0:T(8,128)S(1)}, bf16[1152,3072]{1,0:T(8,128)(2,1)S(1)}) custom-call(s32[3]{0:T(128)S(1)} %pad_add_fusion.info_ref, bf16[256,1536]{1,0:T(8,128)(2,1)S(1)} %get-tuple-element.52.mixed_ref, bf16[512,3072]{1,0:T(8,128)(2,1)S(1)} %get-tuple-element.54.refs_0_, bf16[512,3072]{1,0:T(8,128)(2,1)S(1)} %get-tuple-element.55.refs_1_, ...), custom_call_target="tpu_custom_call" | custom-call | flops 2415919104 | bytes 9437184 | tf_op jit(solution)/shard_map/pallas_call | solution.py:339
  40.0 1.6 %shard_map.80 = (bf16[32,3072]{1,0:T(8,128)(2,1)S(1)}, f32[32,3072]{1,0:T(8,128)S(1)}, bf16[32,3072]{1,0:T(8,128)(2,1)S(1)}) custom-call(bf16[256,1536]{1,0:T(8,128)(2,1)S(1)} %collective-permute-done.9.mixed_ref, bf16[384,3072]{1,0:T(8,128)(2,1)S(1)} %get-tuple-element.53.refs_0_, bf16[1152,3072]{1,0:T(8,128)(2,1)S(1)} %get-tuple-element.57.refs_1_, ...), custom_call_target="tpu_custom_call" | custom-call | flops 905969664 | bytes 9437184 | tf_op jit(solution)/shard_map/pallas_call | solution.py:380
  42.8 1.7 %shard_map.81 = (f32[32,3072]{1,0:T(8,128)S(1)}, f32[32,3072]{1,0:T(8,128)S(1)}, f32[32,3072]{1,0:T(8,128)S(1)}, bf16[32,3072]{1,0:T(8,128)(2,1)S(1)}, bf16[32,3072]{1,0:T(8,128)(2,1)S(1)}) custom-call(bf16[256,1536]{1,0:T(8,128)(2,1)S(1)} %collective-permute-done.9.mixed_ref, bf16[384,3072]{1,0:T(8,128)(2,1)S(1)} %get-tuple-element.53.refs_0_, ...), custom_call_target="tpu_custom_call" | custom-call | flops 1509949440 | bytes 9437184 | tf_op jit(solution)/shard_map/pallas_call | solution.py:380
  45.5 4.0 %collective-permute-done.12 = bf16[32,3072]{1,0:T(8,128)(2,1)S(1)} collective-permute-done((bf16[32,3072]{1,0:T(8,128)(2,1)S(1)}, bf16[32,3072]{1,0:T(8,128)(2,1)S(1)}, u32[]{:S(2)}, u32[]{:S(2)}) %collective-permute-start.12) | collective-permute-done | bytes 196640 | tf_op jit(solution)/shard_map/ppermute | solution.py:440
  49.5 2.6 %collective-permute-start.13 = (bf16[32,3072]{1,0:T(8,128)(2,1)S(1)}, bf16[32,3072]{1,0:T(8,128)(2,1)S(1)}, u32[]{:S(2)}, u32[]{:S(2)}) collective-permute-start(bf16[32,3072]{1,0:T(8,128)(2,1)S(1)} %add_convert_fusion.1), channel_id=1, source_target_pairs={{2,0},{3,1},{6,2},{7,3},{0,4},{1,5},{4,6},{5,7},{10,8},{11,9},{14,... | collective-permute-start | bytes 589832 | tf_op jit(solution)/shard_map/ppermute | solution.py:437
  52.1 1.5 %collective-permute-start.14 = (bf16[32,3072]{1,0:T(8,128)(2,1)S(1)}, bf16[32,3072]{1,0:T(8,128)(2,1)S(1)}, u32[]{:S(2)}, u32[]{:S(2)}) collective-permute-start(bf16[32,3072]{1,0:T(8,128)(2,1)S(1)} %get-tuple-element.68), channel_id=1, source_target_pairs={{0,1},{1,0},{2,3},{3,2},{4,5},{5,4},{6,7},{7,6},{8,9},{9,8},{10,11... | collective-permute-start | bytes 589832 | tf_op jit(solution)/shard_map/ppermute | solution.py:440
  53.7 2.3 %collective-permute-start.11 = (bf16[32,3072]{1,0:T(8,128)(2,1)S(1)}, bf16[32,3072]{1,0:T(8,128)(2,1)S(1)}, u32[]{:S(2)}, u32[]{:S(2)}) collective-permute-start(bf16[32,3072]{1,0:T(8,128)(2,1)S(1)} %add_convert_fusion.2), channel_id=1, source_target_pairs={{0,2},{1,3},{2,6},{3,7},{4,0},{5,1},{6,4},{7,5},{8,10},{9,11},{10,... | collective-permute-start | bytes 589832 | tf_op jit(solution)/shard_map/ppermute | solution.py:434
  56.1 1.5 %collective-permute-start.16 = (bf16[32,3072]{1,0:T(8,128)(2,1)S(1)}, bf16[32,3072]{1,0:T(8,128)(2,1)S(1)}, u32[]{:S(2)}, u32[]{:S(2)}) collective-permute-start(bf16[32,3072]{1,0:T(8,128)(2,1)S(1)} %get-tuple-element.70), channel_id=1, source_target_pairs={{0,1},{1,0},{2,3},{3,2},{4,5},{5,4},{6,7},{7,6},{8,9},{9,8},{10,11... | collective-permute-start | bytes 589832 | tf_op jit(solution)/shard_map/ppermute | solution.py:440
  57.6 1.3 %collective-permute-done.14 = bf16[32,3072]{1,0:T(8,128)(2,1)S(1)} collective-permute-done((bf16[32,3072]{1,0:T(8,128)(2,1)S(1)}, bf16[32,3072]{1,0:T(8,128)(2,1)S(1)}, u32[]{:S(2)}, u32[]{:S(2)}) %collective-permute-start.14) | collective-permute-done | bytes 196640 | tf_op jit(solution)/shard_map/ppermute | solution.py:440
  59.0 2.6 %collective-permute-start.15 = (bf16[32,3072]{1,0:T(8,128)(2,1)S(1)}, bf16[32,3072]{1,0:T(8,128)(2,1)S(1)}, u32[]{:S(2)}, u32[]{:S(2)}) collective-permute-start(bf16[32,3072]{1,0:T(8,128)(2,1)S(1)} %add_convert_fusion), channel_id=1, source_target_pairs={{2,0},{3,1},{6,2},{7,3},{0,4},{1,5},{4,6},{5,7},{10,8},{11,9},{14,... | collective-permute-start | bytes 589832 | tf_op jit(solution)/shard_map/ppermute | solution.py:437
  62.4 3.8 %collective-permute-done.15 = bf16[32,3072]{1,0:T(8,128)(2,1)S(1)} collective-permute-done((bf16[32,3072]{1,0:T(8,128)(2,1)S(1)}, bf16[32,3072]{1,0:T(8,128)(2,1)S(1)}, u32[]{:S(2)}, u32[]{:S(2)}) %collective-permute-start.15) | collective-permute-done | bytes 196640 | tf_op jit(solution)/shard_map/ppermute | solution.py:437
  67.0 1.3 %collective-permute-done.17 = bf16[1,16,3072]{2,1,0:T(8,128)(2,1)S(1)} collective-permute-done((bf16[1,16,3072]{2,1,0:T(8,128)(2,1)S(1)}, bf16[1,16,3072]{2,1,0:T(8,128)(2,1)S(1)}, u32[]{:S(2)}, u32[]{:S(2)}) %collective-permute-start.17) | collective-permute-done | bytes 98336 | tf_op jit(solution)/shard_map/ppermute | solution.py:578
  (39 shorter events, 8.4 us)
Async XLA Ops:
  0.0 1.7 %collective-permute-start = (bf16[16,6144]{1,0:T(8,128)(2,1)}, bf16[16,6144]{1,0:T(8,128)(2,1)S(1)}, u32[]{:S(2)}, u32[]{:S(2)}) collective-permute-start(bf16[16,6144]{1,0:T(8,128)(2,1)} %bitcast.19), channel_id=1, source_target_pairs={{0,8},{8,0},{1,9},{9,1},{2,10},{10,2},{3,11},{11,3},{4,12},{12,4},... | collective-permute-start | bytes 589832 | tf_op jit(solution)/shard_map/ppermute | solution.py:530
  1.8 9.2 %collective-permute-start.2 = (bf16[32,3072]{1,0:T(8,128)(2,1)S(1)}, bf16[32,3072]{1,0:T(8,128)(2,1)S(1)}, u32[]{:S(2)}, u32[]{:S(2)}) collective-permute-start(bf16[32,3072]{1,0:T(8,128)(2,1)S(1)} %bitcast.12), channel_id=1, source_target_pairs={{0,2},{1,3},{2,6},{3,7},{4,0},{5,1},{6,4},{7,5},{8,10},{9,11},{10,... | collective-permute-start | bytes 589832 | tf_op jit(solution)/shard_map/ppermute | solution.py:434
  4.8 6.7 %collective-permute-start.1 = (bf16[32,3072]{1,0:T(8,128)(2,1)S(1)}, bf16[32,3072]{1,0:T(8,128)(2,1)S(1)}, u32[]{:S(2)}, u32[]{:S(2)}) collective-permute-start(bf16[32,3072]{1,0:T(8,128)(2,1)S(1)} %bitcast.13), channel_id=1, source_target_pairs={{0,1},{1,0},{2,3},{3,2},{4,5},{5,4},{6,7},{7,6},{8,9},{9,8},{10,11... | collective-permute-start | bytes 589832 | tf_op jit(solution)/shard_map/ppermute | solution.py:440
  11.4 6.9 %collective-permute-start.3 = (bf16[32,3072]{1,0:T(8,128)(2,1)S(1)}, bf16[32,3072]{1,0:T(8,128)(2,1)S(1)}, u32[]{:S(2)}, u32[]{:S(2)}) collective-permute-start(bf16[32,3072]{1,0:T(8,128)(2,1)S(1)} %collective-permute-done.2.refs_1_), channel_id=1, source_target_pairs={{0,2},{1,3},{2,6},{3,7},{4,0},{5,1},{6,4},{7,5},{8,10},{9,11},{10,... | collective-permute-start | bytes 589832 | tf_op jit(solution)/shard_map/ppermute | solution.py:434
  14.0 7.1 %collective-permute-start.4 = (bf16[32,3072]{1,0:T(8,128)(2,1)S(1)}, bf16[32,3072]{1,0:T(8,128)(2,1)S(1)}, u32[]{:S(2)}, u32[]{:S(2)}) collective-permute-start(bf16[32,3072]{1,0:T(8,128)(2,1)S(1)} %collective-permute-done.2.refs_1_), channel_id=1, source_target_pairs={{0,1},{1,0},{2,3},{3,2},{4,5},{5,4},{6,7},{7,6},{8,9},{9,8},{10,11... | collective-permute-start | bytes 589832 | tf_op jit(solution)/shard_map/ppermute | solution.py:440
  18.3 9.3 %collective-permute-start.6 = (bf16[64,3072]{1,0:T(8,128)(2,1)S(1)}, bf16[64,3072]{1,0:T(8,128)(2,1)S(1)}, u32[]{:S(2)}, u32[]{:S(2)}) collective-permute-start(bf16[64,3072]{1,0:T(8,128)(2,1)S(1)} %shard_map.74), channel_id=1, source_target_pairs={{2,0},{3,1},{6,2},{7,3},{0,4},{1,5},{4,6},{5,7},{10,8},{11,9},{14,... | collective-permute-start | bytes 1179656 | tf_op jit(solution)/shard_map/ppermute | solution.py:437
  19.6 7.6 %collective-permute-start.5 = (bf16[32,3072]{1,0:T(8,128)(2,1)S(1)}, bf16[32,3072]{1,0:T(8,128)(2,1)S(1)}, u32[]{:S(2)}, u32[]{:S(2)}) collective-permute-start(bf16[32,3072]{1,0:T(8,128)(2,1)S(1)} %collective-permute-done.3.refs_2_), channel_id=1, source_target_pairs={{0,1},{1,0},{2,3},{3,2},{4,5},{5,4},{6,7},{7,6},{8,9},{9,8},{10,11... | collective-permute-start | bytes 589832 | tf_op jit(solution)/shard_map/ppermute | solution.py:440
  27.0 5.6 %collective-permute-start.7 = (bf16[160,1536]{1,0:T(8,128)(2,1)S(1)}, bf16[160,1536]{1,0:T(8,128)(2,1)S(1)}, u32[]{:S(2)}, u32[]{:S(2)}) collective-permute-start(bf16[160,1536]{1,0:T(8,128)(2,1)S(1)} %get-tuple-element.50), channel_id=1, source_target_pairs={{0,8},{8,0},{1,9},{9,1},{2,10},{10,2},{3,11},{11,3},{4,12},{12,4},... | collective-permute-start | bytes 1474568 | tf_op jit(solution)/shard_map/ppermute | solution.py:547
  30.0 2.6 %collective-permute-start.8 = (bf16[96,1536]{1,0:T(8,128)(2,1)S(1)}, bf16[96,1536]{1,0:T(8,128)(2,1)S(1)}, u32[]{:S(2)}, u32[]{:S(2)}) collective-permute-start(bf16[96,1536]{1,0:T(8,128)(2,1)S(1)} %get-tuple-element.51), channel_id=1, source_target_pairs={{0,8},{8,0},{1,9},{9,1},{2,10},{10,2},{3,11},{11,3},{4,12},{12,4},... | collective-permute-start | bytes 884744 | tf_op jit(solution)/shard_map/ppermute | solution.py:547
  30.1 2.5 %copy-start = (f32[3,3,3072]{2,1,0:T(4,128)S(1)}, f32[3,3,3072]{2,1,0:T(4,128)}, u32[]{:S(2)}) copy-start(f32[3,3,3072]{2,1,0:T(4,128)} %refs_5_.1) | copy-start | bytes 331780
  30.1 2.5 %copy-start.2 = (f32[3072]{0:T(1024)S(1)}, f32[3072]{0:T(1024)}, u32[]{:S(2)}) copy-start(f32[3072]{0:T(1024)} %param.9) | copy-start | bytes 36868
  30.1 2.5 %copy-start.3 = (f32[3072]{0:T(1024)S(1)}, f32[3072]{0:T(1024)}, u32[]{:S(2)}) copy-start(f32[3072]{0:T(1024)} %param.11) | copy-start | bytes 36868
  35.8 4.2 %collective-permute-start.9 = (bf16[256,1536]{1,0:T(8,128)(2,1)S(1)}, bf16[256,1536]{1,0:T(8,128)(2,1)S(1)}, u32[]{:S(2)}, u32[]{:S(2)}) collective-permute-start(bf16[256,1536]{1,0:T(8,128)(2,1)S(1)} %get-tuple-element.52.mixed_ref), channel_id=1, source_target_pairs={{0,8},{8,0},{1,9},{9,1},{2,10},{10,2},{3,11},{11,3},{4,12},{12,4},... | collective-permute-start | bytes 2359304 | tf_op jit(solution)/shard_map/ppermute | solution.py:562
  41.6 24.7 %copy-start.1 = (f32[6144]{0:T(1024)S(1)}, f32[6144]{0:T(1024)}, u32[]{:S(2)}) copy-start(f32[6144]{0:T(1024)} %param.13) | copy-start | bytes 73732
  41.6 7.8 %collective-permute-start.12 = (bf16[32,3072]{1,0:T(8,128)(2,1)S(1)}, bf16[32,3072]{1,0:T(8,128)(2,1)S(1)}, u32[]{:S(2)}, u32[]{:S(2)}) collective-permute-start(bf16[32,3072]{1,0:T(8,128)(2,1)S(1)} %get-tuple-element.66), channel_id=1, source_target_pairs={{0,1},{1,0},{2,3},{3,2},{4,5},{5,4},{6,7},{7,6},{8,9},{9,8},{10,11... | collective-permute-start | bytes 589832 | tf_op jit(solution)/shard_map/ppermute | solution.py:440
  44.5 9.1 %collective-permute-start.10 = (bf16[32,3072]{1,0:T(8,128)(2,1)S(1)}, bf16[32,3072]{1,0:T(8,128)(2,1)S(1)}, u32[]{:S(2)}, u32[]{:S(2)}) collective-permute-start(bf16[32,3072]{1,0:T(8,128)(2,1)S(1)} %get-tuple-element.63), channel_id=1, source_target_pairs={{0,1},{1,0},{2,3},{3,2},{4,5},{5,4},{6,7},{7,6},{8,9},{9,8},{10,11... | collective-permute-start | bytes 589832 | tf_op jit(solution)/shard_map/ppermute | solution.py:440
  49.5 9.4 %collective-permute-start.13 = (bf16[32,3072]{1,0:T(8,128)(2,1)S(1)}, bf16[32,3072]{1,0:T(8,128)(2,1)S(1)}, u32[]{:S(2)}, u32[]{:S(2)}) collective-permute-start(bf16[32,3072]{1,0:T(8,128)(2,1)S(1)} %add_convert_fusion.1), channel_id=1, source_target_pairs={{2,0},{3,1},{6,2},{7,3},{0,4},{1,5},{4,6},{5,7},{10,8},{11,9},{14,... | collective-permute-start | bytes 589832 | tf_op jit(solution)/shard_map/ppermute | solution.py:437
  52.1 6.8 %collective-permute-start.14 = (bf16[32,3072]{1,0:T(8,128)(2,1)S(1)}, bf16[32,3072]{1,0:T(8,128)(2,1)S(1)}, u32[]{:S(2)}, u32[]{:S(2)}) collective-permute-start(bf16[32,3072]{1,0:T(8,128)(2,1)S(1)} %get-tuple-element.68), channel_id=1, source_target_pairs={{0,1},{1,0},{2,3},{3,2},{4,5},{5,4},{6,7},{7,6},{8,9},{9,8},{10,11... | collective-permute-start | bytes 589832 | tf_op jit(solution)/shard_map/ppermute | solution.py:440
  53.7 8.7 %collective-permute-start.11 = (bf16[32,3072]{1,0:T(8,128)(2,1)S(1)}, bf16[32,3072]{1,0:T(8,128)(2,1)S(1)}, u32[]{:S(2)}, u32[]{:S(2)}) collective-permute-start(bf16[32,3072]{1,0:T(8,128)(2,1)S(1)} %add_convert_fusion.2), channel_id=1, source_target_pairs={{0,2},{1,3},{2,6},{3,7},{4,0},{5,1},{6,4},{7,5},{8,10},{9,11},{10,... | collective-permute-start | bytes 589832 | tf_op jit(solution)/shard_map/ppermute | solution.py:434
  56.1 5.9 %collective-permute-start.16 = (bf16[32,3072]{1,0:T(8,128)(2,1)S(1)}, bf16[32,3072]{1,0:T(8,128)(2,1)S(1)}, u32[]{:S(2)}, u32[]{:S(2)}) collective-permute-start(bf16[32,3072]{1,0:T(8,128)(2,1)S(1)} %get-tuple-element.70), channel_id=1, source_target_pairs={{0,1},{1,0},{2,3},{3,2},{4,5},{5,4},{6,7},{7,6},{8,9},{9,8},{10,11... | collective-permute-start | bytes 589832 | tf_op jit(solution)/shard_map/ppermute | solution.py:440
  59.0 7.2 %collective-permute-start.15 = (bf16[32,3072]{1,0:T(8,128)(2,1)S(1)}, bf16[32,3072]{1,0:T(8,128)(2,1)S(1)}, u32[]{:S(2)}, u32[]{:S(2)}) collective-permute-start(bf16[32,3072]{1,0:T(8,128)(2,1)S(1)} %add_convert_fusion), channel_id=1, source_target_pairs={{2,0},{3,1},{6,2},{7,3},{0,4},{1,5},{4,6},{5,7},{10,8},{11,9},{14,... | collective-permute-start | bytes 589832 | tf_op jit(solution)/shard_map/ppermute | solution.py:437
  66.9 1.4 %collective-permute-start.17 = (bf16[1,16,3072]{2,1,0:T(8,128)(2,1)S(1)}, bf16[1,16,3072]{2,1,0:T(8,128)(2,1)S(1)}, u32[]{:S(2)}, u32[]{:S(2)}) collective-permute-start(bf16[1,16,3072]{2,1,0:T(8,128)(2,1)S(1)} %get-tuple-element.72), channel_id=1, source_target_pairs={{0,8},{8,0},{1,9},{9,1},{2,10},{10,2},{3,11},{11,3},{4,12},{12,4},... | collective-permute-start | bytes 294920 | tf_op jit(solution)/shard_map/ppermute | solution.py:578
